TPU v7x, 32 devices: a whole 2x2x4 slice. The times are simulated.
32 devices in a mesh: group: 2 (over y), gx: 4 (over z), gy: 2 (over x), ta: 2 (over core).
Axes of the slice: x: 2, y: 2, z: 4, core: 2. Of those that a mesh axis runs over, the one named last changes fastest.
Arguments:
- t_initial: float32 [8, 2048, 512], P('ta', ('group', 'gx'), 'gy'), parts along dimension 1, may hold values from -4 to 4
- power_mantissa: bfloat16 [8, 3072, 768], P('ta', ('group', 'gx'), 'gy'), parts along dimension 1, may hold values from -6 to 6
- tile_exponent: int32 [8, 48, 12], P('ta', ('group', 'gx'), 'gy'), parts along dimension 1, may hold values from -2 to 2
- channel_mask: int32 [8, 512], replicated, may hold values 0 or 1
- material: int32 [8], replicated, may hold values from 0 to 3
- conductivity: float32 [4], replicated, may hold values from 0.3 to 3
Outputs:
- temperature: float32 [8, 2048, 512], P('ta', ('group', 'gx'), 'gy'), parts along dimension 1
- heat_source: float32 [8, 2048, 512], P('ta', ('group', 'gx'), 'gy'), parts along dimension 1
There are 2 independent parts, one for each index of `group`. A program takes and returns all parts, laid end to end along the dimension named above; an argument that names none is the same for every part. Nothing has to cross between parts.
All inputs are finite; a program needn't handle non-finite values.
Results may differ from a plain program's by a relative error of at most 0.0003.
Values sent between devices are 32-bit elements; how exact they have to be, the bound alone decides.
No kernel may reach another device: no remote copies, remote signals or barrier semaphores. Data moves between devices by JAX's collectives and lax.ppermute only.
A program may use at most 192 MiB of HBM per device.

v0:
```python
import jax
import jax.numpy as jnp
from jax import lax
from jax.sharding import PartitionSpec as P

RIM = 64
TILE = 64
MATS = 4
STEPS = 2
SWEEPS = 3


CAPACITY = 1.0
COOLANT = 2.0
VERTICAL = 2.0


def from_behind(value, axis, steps):
    count = lax.axis_size(axis)
    first, last = (max(0, -steps), min(count, count - steps))
    return lax.ppermute(value, axis, [(source, source + steps) for source in range(first, last)])


def padded_2(cells, sides, width):
    for axis, dim in sides:
        count = lax.axis_size(axis)
        ends = count - 1
        head = lax.slice_in_dim(cells, 0, width, axis=dim)
        tail = lax.slice_in_dim(cells, cells.shape[dim] - width, cells.shape[dim], axis=dim)
        cells = jnp.concatenate(
            [
                lax.ppermute(tail, axis, [(i, (i + 1) % count) for i in range(ends)]),
                cells,
                lax.ppermute(head, axis, [((i + 1) % count, i) for i in range(ends)]),
            ],
            axis=dim,
        )
    return cells


def decode(mantissa, exponent):
    scales = jnp.exp2(exponent.astype(jnp.float32))
    depth, rows, cols = scales.shape
    scales = jnp.broadcast_to(scales[:, :, None, :, None], (depth, rows, TILE, cols, TILE))
    return mantissa.astype(jnp.float32) * scales.reshape(depth, rows * TILE, cols * TILE)


def add_edges(inner, from_prev, from_next, axis):
    length = inner.shape[axis]
    widths_head = [(0, 0)] * inner.ndim
    widths_head[axis] = (0, length - RIM)
    widths_tail = [(0, 0)] * inner.ndim
    widths_tail[axis] = (length - RIM, 0)
    inner = inner + jnp.pad(from_prev, widths_head)
    return inner + jnp.pad(from_next, widths_tail)


def send_rows(values, offset):
    return from_behind(values, "gx", offset)


def send_cols(values, offset):
    return from_behind(values, "gy", offset)


def fold_rim(power, axis, sender):
    length = power.shape[axis]
    inner = lax.slice_in_dim(power, RIM, length - RIM, axis=axis)
    upper = lax.slice_in_dim(power, 0, RIM, axis=axis)
    lower = lax.slice_in_dim(power, length - RIM, length, axis=axis)
    from_prev = sender(lower, 1)
    from_next = sender(upper, -1)
    return add_edges(inner, from_prev, from_next, axis)


def neighbours(padded):
    return [
        padded[:-2, 1:-1, 1:-1],
        padded[2:, 1:-1, 1:-1],
        padded[1:-1, :-2, 1:-1],
        padded[1:-1, 2:, 1:-1],
        padded[1:-1, 1:-1, :-2],
        padded[1:-1, 1:-1, 2:],
    ]


def face_coeffs(cond_padded):
    centre = cond_padded[1:-1, 1:-1, 1:-1]
    weights = (VERTICAL, VERTICAL, 1.0, 1.0, 1.0, 1.0)
    return [
        weight * 0.5 * (centre + other) for weight, other in zip(weights, neighbours(cond_padded))
    ]


def denominator(coeffs, flow):
    total = CAPACITY + flow
    for coeff in coeffs:
        total = total + coeff
    return total


def sweep(padded, coeffs, base, denom, flow):
    others = neighbours(padded)
    total = base
    for coeff, other in zip(coeffs, others):
        total = total + coeff * other
    total = total + flow * others[2]
    return total / denom


def whole_tables(material, channel_mask, conductivity, cols):
    col_start = lax.axis_index("gy") * cols
    onehot = (material[:, None] == jnp.arange(MATS, dtype=jnp.int32)[None, :]).astype(jnp.float32)
    layer_cond = jnp.sum(onehot * conductivity[None, :], axis=1)
    mask_local = lax.dynamic_slice_in_dim(channel_mask, col_start, cols, 1)
    flow = COOLANT * mask_local.astype(jnp.float32)[:, None, :]
    return (layer_cond, flow)


def pad_layers(values, layer_dim):
    widths = [(0, 0)] * values.ndim
    widths[layer_dim] = (1, 1)
    return jnp.pad(values, widths)


def on_device(t_initial, power_mantissa, tile_exponent, channel_mask, material, conductivity):
    depth, rows, cols = t_initial.shape
    power = decode(power_mantissa, tile_exponent)
    power = fold_rim(power, 1, send_rows)
    power = fold_rim(power, 2, send_cols)
    older = t_initial
    layer_cond, flow = whole_tables(material, channel_mask, conductivity, cols)
    older_rows, heat_rows = (
        lax.all_to_all(older, "ta", split_axis=1, concat_axis=0, tiled=True),
        lax.all_to_all(power, "ta", split_axis=1, concat_axis=0, tiled=True),
    )
    for step_index in range(STEPS):
        cond = layer_cond[:, None, None] * (1.0 + 0.5 * jnp.tanh(older_rows))
        padded = padded_2(jnp.stack([older_rows, cond]), ((("gx", "ta"), 2), ("gy", 3)), 1)
        padded = pad_layers(padded, 1)
        coeffs = face_coeffs(padded[1])
        denom = denominator(coeffs, flow)
        base = CAPACITY * older_rows + heat_rows
        field = sweep(padded[0], coeffs, base, denom, flow)
        for sweep_index in range(SWEEPS - 1):
            field_padded = padded_2(field, ((("gx", "ta"), 1), ("gy", 2)), 1)
            field = sweep(pad_layers(field_padded, 0), coeffs, base, denom, flow)
        older_rows = field
    older = lax.all_to_all(older_rows, "ta", split_axis=0, concat_axis=1, tiled=True)
    return (older, power)


def solution(mesh):
    placed = (
        P("ta", ("group", "gx"), "gy"),
        P("ta", ("group", "gx"), "gy"),
        P("ta", ("group", "gx"), "gy"),
        P(),
        P(),
        P(),
    )
    return jax.shard_map(
        on_device,
        mesh=mesh,
        in_specs=placed,
        out_specs=(P("ta", ("group", "gx"), "gy"), P("ta", ("group", "gx"), "gy")),
        check_vma=False,
    )
```

profile of v0, /device:TPU:21, one launch (start us, length us, event | category | flops | bytes accessed | tf_op | source)
XLA Modules:
  0.0 216.8 jit_solution(6103337994758293012)
XLA Ops:
  0.6 1.9 copy.96
  2.5 4.9 %all_to_all.54 = f32[4,256,256]{2,0,1:T(4,128)S(1)} all-to-all(f32[4,256,256]{2,0,1:T(4,128)S(1)} %copy.96), channel_id=1, replica_groups=mesh['group'=2,'gx'=4,'gy'=2,'ta'=2] {'ta'}, dimensions={1} | all-to-all | bytes 2097152 | tf_op jit(solution)/shard_map/all_to_all | solution.py:134
  8.4 3.5 %collective-permute-start.4 = (f32[2,8,1,256]{3,2,1,0:T(1,128)S(1)}, f32[2,8,1,256]{3,2,1,0:T(1,128)S(1)}, u32[]{:S(2)}, u32[]{:S(2)}) collective-permute-start(f32[2,8,1,256]{3,2,1,0:T(1,128)S(1)} %get-tuple-element.18), channel_id=1, source_target_pairs={{0,1},{1,4},{4,5},{5,8},{8,9},{9,12},{12,13},{2,3},{3,6},{6,7},{7,... | collective-permute-start | bytes 49160 | tf_op jit(solution)/shard_map/ppermute | solution.py:32
  11.9 1.9 collective-permute-start.5
  13.8 3.1 %broadcast_in_dim.2 = f32[4,6,64,6,64]{4,3,2,1,0:T(8,128)} broadcast(f32[4,6,6]{2,1,0:T(8,128)S(1)} %copy.99), dimensions={0,1,3} | broadcast | bytes 2359872 | tf_op jit(solution)/shard_map/broadcast_in_dim | solution.py:44
  16.9 5.8 %reshape.35 = f32[4,384,384]{2,1,0:T(8,128)} reshape(f32[4,6,64,6,64]{4,3,2,1,0:T(8,128)} %broadcast_in_dim.2) | data formatting | bytes 4718592 | tf_op jit(solution)/shard_map/reshape | solution.py:45
  26.9 2.1 collective-permute-start
  29.1 3.1 %collective-permute-start.1 = (f32[4,64,384]{2,1,0:T(8,128)}, f32[4,64,384]{2,1,0:T(8,128)}, u32[]{:S(2)}, u32[]{:S(2)}) collective-permute-start(f32[4,64,384]{2,1,0:T(8,128)} %get-tuple-element.11), channel_id=1, source_target_pairs={{4,0},{8,4},{12,8},{5,1},{9,5},{13,9},{6,2},{10,6},{14,10},{7,3},{... | collective-permute-start | bytes 1179656 | tf_op jit(solution)/shard_map/ppermute | solution.py:21
  33.8 1.9 copy.104
  35.7 3.1 %collective-permute-start.6 = (f32[2,8,130,1]{2,1,3,0:T(8,128)S(1)}, f32[2,8,130,1]{2,1,3,0:T(8,128)S(1)}, u32[]{:S(2)}, u32[]{:S(2)}) collective-permute-start(f32[2,8,130,1]{2,1,3,0:T(8,128)S(1)} %copy.104), channel_id=1, source_target_pairs={{0,2},{1,3},{4,6},{5,7},{8,10},{9,11},{12,14},{13,15},{16,18},{17,... | collective-permute-start | bytes 24968 | tf_op jit(solution)/shard_map/ppermute | solution.py:32
  41.2 2.7 %collective-permute-done.7 = f32[2,8,130,1]{2,1,3,0:T(8,128)S(1)} collective-permute-done((f32[2,8,130,1]{2,1,3,0:T(8,128)S(1)}, f32[2,8,130,1]{2,1,3,0:T(8,128)S(1)}, u32[]{:S(2)}, u32[]{:S(2)}) %collective-permute-start.7) | collective-permute-done | bytes 8352 | tf_op jit(solution)/shard_map/ppermute | solution.py:34
  45.3 4.6 %select_maximum_fusion.5 = f32[2,10,130,258]{3,2,1,0:T(8,128)S(1)} fusion(f32[2,8,130,1]{3,2,1,0:T(8,128)} %copy.107, f32[2,8,130,1]{3,2,1,0:T(8,128)S(1)} %copy.106, f32[2,8,1,256]{3,2,1,0:T(1,128)S(1)} %collective-permute-done.5, f32[2,8,1,256]{3,2,1,0:T(1,128)S(1)} %collective-permute-done.4, f32[1,8,128,256]{3,2,1,0:T(8,128)S(1)} %add_multiply_fusion, ...), kind=kLoop, calls=%fused_computation.7 | loop fusion | flops 9391200 | bytes 4829760 | tf_op jit(solution)/shard_map/concatenate | solution.py:30
  54.7 7.3 %collective-permute-done.2 = f32[4,256,64]{2,1,0:T(8,128)S(1)} collective-permute-done((f32[4,256,64]{2,1,0:T(8,128)S(1)}, f32[4,256,64]{2,1,0:T(8,128)S(1)}, u32[]{:S(2)}, u32[]{:S(2)}) %collective-permute-start.2) | collective-permute-done | bytes 262176 | tf_op jit(solution)/shard_map/ppermute | solution.py:21
  62.1 3.9 %collective-permute-done.3 = f32[4,256,64]{2,1,0:T(8,128)S(1)} collective-permute-done((f32[4,256,64]{2,1,0:T(8,128)S(1)}, f32[4,256,64]{2,1,0:T(8,128)S(1)}, u32[]{:S(2)}, u32[]{:S(2)}) %collective-permute-start.3) | collective-permute-done | bytes 262176 | tf_op jit(solution)/shard_map/ppermute | solution.py:21
  67.1 7.7 %all_to_all.55 = f32[4,256,256]{2,0,1:T(4,128)S(1)} all-to-all(f32[4,256,256]{2,0,1:T(4,128)S(1)} %copy.100), channel_id=1, replica_groups=mesh['group'=2,'gx'=4,'gy'=2,'ta'=2] {'ta'}, dimensions={1} | all-to-all | bytes 2097152 | tf_op jit(solution)/shard_map/all_to_all | solution.py:135
  75.1 3.6 %fusion.61 = f32[8,128,256]{2,1,0:T(8,128)S(1)} fusion(f32[10,130,258]{2,1,0:T(8,128)S(1)} %get-tuple-element.9, f32[8,256]{1,0:T(8,128)S(1)} %get-tuple-element.4, f32[8,256]{1,0:T(8,128)S(1)} %get-tuple-element.5, f32[2,4,128,256]{3,2,1,0:T(8,128)S(1)} %copy.102, f32[2,4,128,256]{3,2,1,0:T(8,128)S(1)} %copy.98, f32[10,130,258]{2,1,0:T(8,128)S(1)} %get-tuple-element.8), kind=kLoop, calls=%fused_computation.155 | loop fusion | flops 8388608 | bytes 16793600 | tf_op jit(solution)/shard_map/div | solution.py:108
  78.7 3.1 %collective-permute-start.8 = (f32[8,1,256]{2,1,0:T(1,128)S(1)}, f32[8,1,256]{2,1,0:T(1,128)S(1)}, u32[]{:S(2)}, u32[]{:S(2)}) collective-permute-start(f32[8,1,256]{2,1,0:T(1,128)S(1)} %get-tuple-element.36), channel_id=1, source_target_pairs={{0,1},{1,4},{4,5},{5,8},{8,9},{9,12},{12,13},{2,3},{3,6},{6,7},{7,... | collective-permute-start | bytes 24584 | tf_op jit(solution)/shard_map/ppermute | solution.py:32
  81.9 1.9 collective-permute-start.9
  83.8 3.0 %collective-permute-done.9 = f32[8,1,256]{2,1,0:T(1,128)S(1)} collective-permute-done((f32[8,1,256]{2,1,0:T(1,128)S(1)}, f32[8,1,256]{2,1,0:T(1,128)S(1)}, u32[]{:S(2)}, u32[]{:S(2)}) %collective-permute-start.9) | collective-permute-done | bytes 8224 | tf_op jit(solution)/shard_map/ppermute | solution.py:34
  94.8 1.9 collective-permute-done.11
  97.8 2.4 %select_maximum_fusion.22 = f32[10,130,258]{2,1,0:T(8,128)S(1)} fusion(f32[8,130,1]{2,1,0:T(8,128)} %copy.111, f32[8,130,1]{2,1,0:T(8,128)} %copy.110, f32[8,1,256]{2,1,0:T(1,128)S(1)} %collective-permute-done.9, f32[8,128,256]{2,1,0:T(8,128)} %copy-done.13, f32[8,1,256]{2,1,0:T(1,128)S(1)} %collective-permute-done.8), kind=kLoop, calls=%fused_computation.32 | loop fusion | flops 4024800 | bytes 2414880 | tf_op jit(solution)/shard_map/concatenate | solution.py:30
  100.3 3.9 %fusion.51 = f32[8,128,256]{2,1,0:T(8,128)S(1)} fusion(f32[8,130,1]{2,1,0:T(8,128)S(1)} %copy-done.27, f32[8,1,256]{2,1,0:T(1,128)S(1)} %collective-permute-done.9, f32[8,128,256]{2,1,0:T(8,128)S(1)} %copy-done.14, f32[8,1,256]{2,1,0:T(1,128)S(1)} %collective-permute-done.8, f32[8,130,1]{2,1,0:T(8,128)S(1)} %copy-done.23, ...), kind=kLoop, calls=%fused_computation.135 | loop fusion | flops 10485760 | bytes 13672576 | tf_op jit(solution)/shard_map/div | solution.py:108
  104.3 3.2 %collective-permute-start.12 = (f32[8,1,256]{2,1,0:T(1,128)S(1)}, f32[8,1,256]{2,1,0:T(1,128)S(1)}, u32[]{:S(2)}, u32[]{:S(2)}) collective-permute-start(f32[8,1,256]{2,1,0:T(1,128)S(1)} %get-tuple-element.34), channel_id=1, source_target_pairs={{0,1},{1,4},{4,5},{5,8},{8,9},{9,12},{12,13},{2,3},{3,6},{6,7},{7,... | collective-permute-start | bytes 24584 | tf_op jit(solution)/shard_map/ppermute | solution.py:32
  107.5 1.9 collective-permute-start.13
  109.4 3.0 %collective-permute-done.13 = f32[8,1,256]{2,1,0:T(1,128)S(1)} collective-permute-done((f32[8,1,256]{2,1,0:T(1,128)S(1)}, f32[8,1,256]{2,1,0:T(1,128)S(1)}, u32[]{:S(2)}, u32[]{:S(2)}) %collective-permute-start.13) | collective-permute-done | bytes 8224 | tf_op jit(solution)/shard_map/ppermute | solution.py:34
  120.3 2.2 %collective-permute-done.15 = f32[8,130,1]{1,0,2:T(8,128)S(1)} collective-permute-done((f32[8,130,1]{1,0,2:T(8,128)S(1)}, f32[8,130,1]{1,0,2:T(8,128)S(1)}, u32[]{:S(2)}, u32[]{:S(2)}) %collective-permute-start.15) | collective-permute-done | bytes 4192 | tf_op jit(solution)/shard_map/ppermute | solution.py:34
  123.6 2.4 %select_maximum_fusion.18 = f32[10,130,258]{2,1,0:T(8,128)S(1)} fusion(f32[8,130,1]{2,1,0:T(8,128)} %copy.117, f32[8,130,1]{2,1,0:T(8,128)} %copy.116, f32[8,1,256]{2,1,0:T(1,128)S(1)} %collective-permute-done.13, f32[8,128,256]{2,1,0:T(8,128)} %copy-done.11, f32[8,1,256]{2,1,0:T(1,128)S(1)} %collective-permute-done.12), kind=kLoop, calls=%fused_computation.28 | loop fusion | flops 4024800 | bytes 2414880 | tf_op jit(solution)/shard_map/concatenate | solution.py:30
  126.1 4.1 %multiply_bitcast_fusion = (f32[1,8,128,256]{3,2,1,0:T(8,128)S(1)}, f32[8,128,256]{2,1,0:T(8,128)S(1)}) fusion(f32[8]{0:T(128)S(1)} %select_reduce_fusion, f32[8,256]{1,0:T(8,128)S(1)} %get-tuple-element.4, f32[8,256]{1,0:T(8,128)S(1)} %get-tuple-element.5, f32[8,130,1]{2,1,0:T(8,128)S(1)} %copy-done.24, f32[8,1,256]{2,1,0:T(1,128)S(1)} %collective-permute-done.13, ...), kind=kLoop, calls=%fused_computation.181 | loop fusion | flops 11272192 | bytes 14721184 | tf_op jit(solution)/shard_map/stack | solution.py:139
  130.2 3.1 %collective-permute-start.16 = (f32[2,8,1,256]{3,2,1,0:T(1,128)S(1)}, f32[2,8,1,256]{3,2,1,0:T(1,128)S(1)}, u32[]{:S(2)}, u32[]{:S(2)}) collective-permute-start(f32[2,8,1,256]{3,2,1,0:T(1,128)S(1)} %get-tuple-element.16), channel_id=1, source_target_pairs={{0,1},{1,4},{4,5},{5,8},{8,9},{9,12},{12,13},{2,3},{3,6},{6,7},{7,... | collective-permute-start | bytes 49160 | tf_op jit(solution)/shard_map/ppermute | solution.py:32
  133.4 1.9 collective-permute-start.17
  135.3 3.1 %collective-permute-done.17 = f32[2,8,1,256]{3,2,1,0:T(1,128)S(1)} collective-permute-done((f32[2,8,1,256]{3,2,1,0:T(1,128)S(1)}, f32[2,8,1,256]{3,2,1,0:T(1,128)S(1)}, u32[]{:S(2)}, u32[]{:S(2)}) %collective-permute-start.17) | collective-permute-done | bytes 16416 | tf_op jit(solution)/shard_map/ppermute | solution.py:34
  140.1 2.0 copy.120
  146.0 2.8 %collective-permute-done.19 = f32[2,8,130,1]{2,1,3,0:T(8,128)S(1)} collective-permute-done((f32[2,8,130,1]{2,1,3,0:T(8,128)S(1)}, f32[2,8,130,1]{2,1,3,0:T(8,128)S(1)}, u32[]{:S(2)}, u32[]{:S(2)}) %collective-permute-start.19) | collective-permute-done | bytes 8352 | tf_op jit(solution)/shard_map/ppermute | solution.py:34
  150.3 4.4 %select_maximum_fusion = f32[2,10,130,258]{3,2,1,0:T(8,128)S(1)} fusion(f32[2,8,130,1]{3,2,1,0:T(8,128)} %copy.123, f32[2,8,130,1]{3,2,1,0:T(8,128)S(1)} %copy.122, f32[2,8,1,256]{3,2,1,0:T(1,128)S(1)} %collective-permute-done.17, f32[2,8,1,256]{3,2,1,0:T(1,128)S(1)} %collective-permute-done.16, f32[1,8,128,256]{3,2,1,0:T(8,128)S(1)} %copy-done.18, ...), kind=kLoop, calls=%fused_computation.2 | loop fusion | flops 9391200 | bytes 4829760 | tf_op jit(solution)/shard_map/concatenate | solution.py:30
  156.3 3.5 %fusion.27 = f32[8,128,256]{2,1,0:T(8,128)S(1)} fusion(f32[10,130,258]{2,1,0:T(8,128)S(1)} %get-tuple-element.7, f32[8,256]{1,0:T(8,128)S(1)} %get-tuple-element.4, f32[8,256]{1,0:T(8,128)S(1)} %get-tuple-element.5, f32[8,128,256]{2,1,0:T(8,128)S(1)} %copy-done.6, f32[2,4,128,256]{3,2,1,0:T(8,128)S(1)} %copy-done.3, f32[10,130,258]{2,1,0:T(8,128)S(1)} %get-tuple-element.6), kind=kLoop, calls=%fused_computation.90 | loop fusion | flops 8388608 | bytes 16793600 | tf_op jit(solution)/shard_map/div | solution.py:108
  159.8 3.1 %collective-permute-start.20 = (f32[8,1,256]{2,1,0:T(1,128)S(1)}, f32[8,1,256]{2,1,0:T(1,128)S(1)}, u32[]{:S(2)}, u32[]{:S(2)}) collective-permute-start(f32[8,1,256]{2,1,0:T(1,128)S(1)} %get-tuple-element.32), channel_id=1, source_target_pairs={{0,1},{1,4},{4,5},{5,8},{8,9},{9,12},{12,13},{2,3},{3,6},{6,7},{7,... | collective-permute-start | bytes 24584 | tf_op jit(solution)/shard_map/ppermute | solution.py:32
  162.9 1.9 collective-permute-start.21
  164.9 3.0 %collective-permute-done.21 = f32[8,1,256]{2,1,0:T(1,128)S(1)} collective-permute-done((f32[8,1,256]{2,1,0:T(1,128)S(1)}, f32[8,1,256]{2,1,0:T(1,128)S(1)}, u32[]{:S(2)}, u32[]{:S(2)}) %collective-permute-start.21) | collective-permute-done | bytes 8224 | tf_op jit(solution)/shard_map/ppermute | solution.py:34
  175.7 2.2 %collective-permute-done.23 = f32[8,130,1]{1,0,2:T(8,128)S(1)} collective-permute-done((f32[8,130,1]{1,0,2:T(8,128)S(1)}, f32[8,130,1]{1,0,2:T(8,128)S(1)}, u32[]{:S(2)}, u32[]{:S(2)}) %collective-permute-start.23) | collective-permute-done | bytes 4192 | tf_op jit(solution)/shard_map/ppermute | solution.py:34
  179.1 2.4 %select_maximum_fusion.14 = f32[10,130,258]{2,1,0:T(8,128)S(1)} fusion(f32[8,130,1]{2,1,0:T(8,128)} %copy.127, f32[8,130,1]{2,1,0:T(8,128)} %copy.126, f32[8,1,256]{2,1,0:T(1,128)S(1)} %collective-permute-done.21, f32[8,128,256]{2,1,0:T(8,128)} %copy-done.15, f32[8,1,256]{2,1,0:T(1,128)S(1)} %collective-permute-done.20), kind=kLoop, calls=%fused_computation.22 | loop fusion | flops 4024800 | bytes 2414880 | tf_op jit(solution)/shard_map/concatenate | solution.py:30
  181.6 3.9 %fusion.17 = f32[8,128,256]{2,1,0:T(8,128)S(1)} fusion(f32[8,130,1]{2,1,0:T(8,128)S(1)} %copy-done.28, f32[8,1,256]{2,1,0:T(1,128)S(1)} %collective-permute-done.21, f32[8,128,256]{2,1,0:T(8,128)S(1)} %copy-done.16, f32[8,1,256]{2,1,0:T(1,128)S(1)} %collective-permute-done.20, f32[8,130,1]{2,1,0:T(8,128)S(1)} %copy-done.25, ...), kind=kLoop, calls=%fused_computation.70 | loop fusion | flops 10485760 | bytes 13672576 | tf_op jit(solution)/shard_map/div | solution.py:108
  185.5 3.1 %collective-permute-start.24 = (f32[8,1,256]{2,1,0:T(1,128)S(1)}, f32[8,1,256]{2,1,0:T(1,128)S(1)}, u32[]{:S(2)}, u32[]{:S(2)}) collective-permute-start(f32[8,1,256]{2,1,0:T(1,128)S(1)} %get-tuple-element.30), channel_id=1, source_target_pairs={{0,1},{1,4},{4,5},{5,8},{8,9},{9,12},{12,13},{2,3},{3,6},{6,7},{7,... | collective-permute-start | bytes 24584 | tf_op jit(solution)/shard_map/ppermute | solution.py:32
  188.6 1.9 collective-permute-start.25
  190.6 3.0 %collective-permute-done.25 = f32[8,1,256]{2,1,0:T(1,128)S(1)} collective-permute-done((f32[8,1,256]{2,1,0:T(1,128)S(1)}, f32[8,1,256]{2,1,0:T(1,128)S(1)}, u32[]{:S(2)}, u32[]{:S(2)}) %collective-permute-start.25) | collective-permute-done | bytes 8224 | tf_op jit(solution)/shard_map/ppermute | solution.py:34
  201.5 2.2 %collective-permute-done.27 = f32[8,130,1]{1,0,2:T(8,128)S(1)} collective-permute-done((f32[8,130,1]{1,0,2:T(8,128)S(1)}, f32[8,130,1]{1,0,2:T(8,128)S(1)}, u32[]{:S(2)}, u32[]{:S(2)}) %collective-permute-start.27) | collective-permute-done | bytes 4192 | tf_op jit(solution)/shard_map/ppermute | solution.py:34
  204.8 2.4 %select_maximum_fusion.10 = f32[10,130,258]{2,1,0:T(8,128)S(1)} fusion(f32[8,130,1]{2,1,0:T(8,128)} %copy.133, f32[8,130,1]{2,1,0:T(8,128)} %copy.132, f32[8,1,256]{2,1,0:T(1,128)S(1)} %collective-permute-done.25, f32[8,128,256]{2,1,0:T(8,128)} %copy-done.9, f32[8,1,256]{2,1,0:T(1,128)S(1)} %collective-permute-done.24), kind=kLoop, calls=%fused_computation.18 | loop fusion | flops 4024800 | bytes 2414880 | tf_op jit(solution)/shard_map/concatenate | solution.py:30
  207.3 3.9 %fusion.6 = f32[8,128,256]{2,1,0:T(8,128)S(1)} fusion(f32[8,130,1]{2,1,0:T(8,128)S(1)} %copy-done.26, f32[8,1,256]{2,1,0:T(1,128)S(1)} %collective-permute-done.25, f32[8,128,256]{2,1,0:T(8,128)S(1)} %copy-done.10, f32[8,1,256]{2,1,0:T(1,128)S(1)} %collective-permute-done.24, f32[8,130,1]{2,1,0:T(8,128)S(1)} %copy-done.22, ...), kind=kLoop, calls=%fused_computation.49 | loop fusion | flops 10485760 | bytes 13672576 | tf_op jit(solution)/shard_map/div | solution.py:108
  211.2 4.6 %all_to_all.56 = f32[8,128,256]{2,1,0:T(8,128)S(1)} all-to-all(f32[8,128,256]{2,1,0:T(8,128)S(1)} %fusion.6), channel_id=1, replica_groups=mesh['group'=2,'gx'=4,'gy'=2,'ta'=2] {'ta'}, dimensions={0} | all-to-all | bytes 2097152 | tf_op jit(solution)/shard_map/all_to_all | solution.py:149
  (156 shorter events, 62.1 us)
Async XLA Ops:
  8.2 5.6 %copy-start.31 = (s32[4,6,6]{2,0,1:T(4,128)S(1)}, s32[4,6,6]{2,0,1:T(4,128)}, u32[]{:S(2)}) copy-start(s32[4,6,6]{2,0,1:T(4,128)} %param.8) | copy-start | bytes 1732
  8.4 23.9 %collective-permute-start.4 = (f32[2,8,1,256]{3,2,1,0:T(1,128)S(1)}, f32[2,8,1,256]{3,2,1,0:T(1,128)S(1)}, u32[]{:S(2)}, u32[]{:S(2)}) collective-permute-start(f32[2,8,1,256]{3,2,1,0:T(1,128)S(1)} %get-tuple-element.18), channel_id=1, source_target_pairs={{0,1},{1,4},{4,5},{5,8},{8,9},{9,12},{12,13},{2,3},{3,6},{6,7},{7,... | collective-permute-start | bytes 49160 | tf_op jit(solution)/shard_map/ppermute | solution.py:32
  11.9 20.4 %collective-permute-start.5 = (f32[2,8,1,256]{3,2,1,0:T(1,128)S(1)}, f32[2,8,1,256]{3,2,1,0:T(1,128)S(1)}, u32[]{:S(2)}, u32[]{:S(2)}) collective-permute-start(f32[2,8,1,256]{3,2,1,0:T(1,128)S(1)} %get-tuple-element.19), channel_id=1, source_target_pairs={{1,0},{4,1},{5,4},{8,5},{9,8},{12,9},{13,12},{3,2},{6,3},{7,6},{10... | collective-permute-start | bytes 49160 | tf_op jit(solution)/shard_map/ppermute | solution.py:34
  16.9 5.8 %copy-start.30 = (bf16[4,384,384]{2,1,0:T(8,128)(2,1)S(1)}, bf16[4,384,384]{2,1,0:T(8,128)(2,1)}, u32[]{:S(2)}) copy-start(bf16[4,384,384]{2,1,0:T(8,128)(2,1)} %param.7) | copy-start | bytes 3538948
  26.9 23.0 %collective-permute-start = (f32[4,64,384]{2,1,0:T(8,128)}, f32[4,64,384]{2,1,0:T(8,128)}, u32[]{:S(2)}, u32[]{:S(2)}) collective-permute-start(f32[4,64,384]{2,1,0:T(8,128)} %get-tuple-element.10), channel_id=1, source_target_pairs={{0,4},{4,8},{8,12},{1,5},{5,9},{9,13},{2,6},{6,10},{10,14},{3,7},{... | collective-permute-start | bytes 1179656 | tf_op jit(solution)/shard_map/ppermute | solution.py:21
  29.1 20.9 %collective-permute-start.1 = (f32[4,64,384]{2,1,0:T(8,128)}, f32[4,64,384]{2,1,0:T(8,128)}, u32[]{:S(2)}, u32[]{:S(2)}) collective-permute-start(f32[4,64,384]{2,1,0:T(8,128)} %get-tuple-element.11), channel_id=1, source_target_pairs={{4,0},{8,4},{12,8},{5,1},{9,5},{13,9},{6,2},{10,6},{14,10},{7,3},{... | collective-permute-start | bytes 1179656 | tf_op jit(solution)/shard_map/ppermute | solution.py:21
  33.8 6.9 %copy-start.32 = (s32[8,512]{1,0:T(8,128)S(1)}, s32[8,512]{1,0:T(8,128)}, u32[]{:S(2)}) copy-start(s32[8,512]{1,0:T(8,128)} %param.9) | copy-start | bytes 49156
  35.7 5.1 %collective-permute-start.6 = (f32[2,8,130,1]{2,1,3,0:T(8,128)S(1)}, f32[2,8,130,1]{2,1,3,0:T(8,128)S(1)}, u32[]{:S(2)}, u32[]{:S(2)}) collective-permute-start(f32[2,8,130,1]{2,1,3,0:T(8,128)S(1)} %copy.104), channel_id=1, source_target_pairs={{0,2},{1,3},{4,6},{5,7},{8,10},{9,11},{12,14},{13,15},{16,18},{17,... | collective-permute-start | bytes 24968 | tf_op jit(solution)/shard_map/ppermute | solution.py:32
  39.4 4.5 %collective-permute-start.7 = (f32[2,8,130,1]{2,1,3,0:T(8,128)S(1)}, f32[2,8,130,1]{2,1,3,0:T(8,128)S(1)}, u32[]{:S(2)}, u32[]{:S(2)}) collective-permute-start(f32[2,8,130,1]{2,1,3,0:T(8,128)S(1)} %copy.105), channel_id=1, source_target_pairs={{2,0},{3,1},{6,4},{7,5},{10,8},{11,9},{14,12},{15,13},{18,16},{19,... | collective-permute-start | bytes 24968 | tf_op jit(solution)/shard_map/ppermute | solution.py:34
  45.3 4.6 %copy-start.20 = (f32[4,384,384]{2,1,0:T(8,128)S(1)}, f32[4,384,384]{2,1,0:T(8,128)}, u32[]{:S(2)}) copy-start(f32[4,384,384]{2,1,0:T(8,128)} %copy-done.19) | copy-start | bytes 7077892
  51.5 10.6 %collective-permute-start.2 = (f32[4,256,64]{2,1,0:T(8,128)S(1)}, f32[4,256,64]{2,1,0:T(8,128)S(1)}, u32[]{:S(2)}, u32[]{:S(2)}) collective-permute-start(f32[4,256,64]{2,1,0:T(8,128)S(1)} %get-tuple-element.20), channel_id=1, source_target_pairs={{0,2},{1,3},{4,6},{5,7},{8,10},{9,11},{12,14},{13,15},{16,18},{17,... | collective-permute-start | bytes 786440 | tf_op jit(solution)/shard_map/ppermute | solution.py:21
  53.1 12.8 %collective-permute-start.3 = (f32[4,256,64]{2,1,0:T(8,128)S(1)}, f32[4,256,64]{2,1,0:T(8,128)S(1)}, u32[]{:S(2)}, u32[]{:S(2)}) collective-permute-start(f32[4,256,64]{2,1,0:T(8,128)S(1)} %get-tuple-element.21), channel_id=1, source_target_pairs={{2,0},{3,1},{6,4},{7,5},{10,8},{11,9},{14,12},{15,13},{18,16},{19,... | collective-permute-start | bytes 786440 | tf_op jit(solution)/shard_map/ppermute | solution.py:21
  66.4 8.4 %copy-start.29 = (f32[4,256,256]{2,1,0:T(8,128)}, f32[4,256,256]{2,1,0:T(8,128)S(1)}, u32[]{:S(2)}) copy-start(f32[4,256,256]{2,1,0:T(8,128)S(1)} %fusion.71) | copy-start | bytes 3145732
  75.0 3.6 %copy-start = (f32[2,4,128,256]{3,2,1,0:T(8,128)}, f32[2,4,128,256]{3,2,1,0:T(8,128)S(1)}, u32[]{:S(2)}) copy-start(f32[2,4,128,256]{3,2,1,0:T(8,128)S(1)} %copy.102) | copy-start | bytes 3145732
  78.7 9.5 %copy-start.13 = (f32[8,128,256]{2,1,0:T(8,128)}, f32[8,128,256]{2,1,0:T(8,128)S(1)}, u32[]{:S(2)}) copy-start(f32[8,128,256]{2,1,0:T(8,128)S(1)} %fusion.61) | copy-start | bytes 3145732
  78.7 5.1 %collective-permute-start.8 = (f32[8,1,256]{2,1,0:T(1,128)S(1)}, f32[8,1,256]{2,1,0:T(1,128)S(1)}, u32[]{:S(2)}, u32[]{:S(2)}) collective-permute-start(f32[8,1,256]{2,1,0:T(1,128)S(1)} %get-tuple-element.36), channel_id=1, source_target_pairs={{0,1},{1,4},{4,5},{5,8},{8,9},{9,12},{12,13},{2,3},{3,6},{6,7},{7,... | collective-permute-start | bytes 24584 | tf_op jit(solution)/shard_map/ppermute | solution.py:32
  81.9 5.0 %collective-permute-start.9 = (f32[8,1,256]{2,1,0:T(1,128)S(1)}, f32[8,1,256]{2,1,0:T(1,128)S(1)}, u32[]{:S(2)}, u32[]{:S(2)}) collective-permute-start(f32[8,1,256]{2,1,0:T(1,128)S(1)} %get-tuple-element.37), channel_id=1, source_target_pairs={{1,0},{4,1},{5,4},{8,5},{9,8},{12,9},{13,12},{3,2},{6,3},{7,6},{10... | collective-permute-start | bytes 24584 | tf_op jit(solution)/shard_map/ppermute | solution.py:34
  89.5 4.2 %collective-permute-start.10 = (f32[8,130,1]{1,0,2:T(8,128)S(1)}, f32[8,130,1]{1,0,2:T(8,128)S(1)}, u32[]{:S(2)}, u32[]{:S(2)}) collective-permute-start(f32[8,130,1]{1,0,2:T(8,128)S(1)} %copy.108), channel_id=1, source_target_pairs={{0,2},{1,3},{4,6},{5,7},{8,10},{9,11},{12,14},{13,15},{16,18},{17,... | collective-permute-start | bytes 12488 | tf_op jit(solution)/shard_map/ppermute | solution.py:32
  92.2 4.5 %collective-permute-start.11 = (f32[8,130,1]{1,0,2:T(8,128)S(1)}, f32[8,130,1]{1,0,2:T(8,128)S(1)}, u32[]{:S(2)}, u32[]{:S(2)}) collective-permute-start(f32[8,130,1]{1,0,2:T(8,128)S(1)} %copy.109), channel_id=1, source_target_pairs={{2,0},{3,1},{6,4},{7,5},{10,8},{11,9},{14,12},{15,13},{18,16},{19,... | collective-permute-start | bytes 12488 | tf_op jit(solution)/shard_map/ppermute | solution.py:34
  97.8 2.5 %copy-start.23 = (f32[8,130,1]{2,1,0:T(8,128)S(1)}, f32[8,130,1]{2,1,0:T(8,128)}, u32[]{:S(2)}) copy-start(f32[8,130,1]{2,1,0:T(8,128)} %copy.110) | copy-start | bytes 12484
  97.8 2.5 %copy-start.27 = (f32[8,130,1]{2,1,0:T(8,128)S(1)}, f32[8,130,1]{2,1,0:T(8,128)}, u32[]{:S(2)}) copy-start(f32[8,130,1]{2,1,0:T(8,128)} %copy.111) | copy-start | bytes 12484
  104.3 9.5 %copy-start.11 = (f32[8,128,256]{2,1,0:T(8,128)}, f32[8,128,256]{2,1,0:T(8,128)S(1)}, u32[]{:S(2)}) copy-start(f32[8,128,256]{2,1,0:T(8,128)S(1)} %fusion.51) | copy-start | bytes 3145732
  104.3 5.1 %collective-permute-start.12 = (f32[8,1,256]{2,1,0:T(1,128)S(1)}, f32[8,1,256]{2,1,0:T(1,128)S(1)}, u32[]{:S(2)}, u32[]{:S(2)}) collective-permute-start(f32[8,1,256]{2,1,0:T(1,128)S(1)} %get-tuple-element.34), channel_id=1, source_target_pairs={{0,1},{1,4},{4,5},{5,8},{8,9},{9,12},{12,13},{2,3},{3,6},{6,7},{7,... | collective-permute-start | bytes 24584 | tf_op jit(solution)/shard_map/ppermute | solution.py:32
  107.5 5.0 %collective-permute-start.13 = (f32[8,1,256]{2,1,0:T(1,128)S(1)}, f32[8,1,256]{2,1,0:T(1,128)S(1)}, u32[]{:S(2)}, u32[]{:S(2)}) collective-permute-start(f32[8,1,256]{2,1,0:T(1,128)S(1)} %get-tuple-element.35), channel_id=1, source_target_pairs={{1,0},{4,1},{5,4},{8,5},{9,8},{12,9},{13,12},{3,2},{6,3},{7,6},{10... | collective-permute-start | bytes 24584 | tf_op jit(solution)/shard_map/ppermute | solution.py:34
  115.1 4.1 %collective-permute-start.14 = (f32[8,130,1]{1,0,2:T(8,128)S(1)}, f32[8,130,1]{1,0,2:T(8,128)S(1)}, u32[]{:S(2)}, u32[]{:S(2)}) collective-permute-start(f32[8,130,1]{1,0,2:T(8,128)S(1)} %copy.114), channel_id=1, source_target_pairs={{0,2},{1,3},{4,6},{5,7},{8,10},{9,11},{12,14},{13,15},{16,18},{17,... | collective-permute-start | bytes 12488 | tf_op jit(solution)/shard_map/ppermute | solution.py:32
  117.9 4.6 %collective-permute-start.15 = (f32[8,130,1]{1,0,2:T(8,128)S(1)}, f32[8,130,1]{1,0,2:T(8,128)S(1)}, u32[]{:S(2)}, u32[]{:S(2)}) collective-permute-start(f32[8,130,1]{1,0,2:T(8,128)S(1)} %copy.115), channel_id=1, source_target_pairs={{2,0},{3,1},{6,4},{7,5},{10,8},{11,9},{14,12},{15,13},{18,16},{19,... | collective-permute-start | bytes 12488 | tf_op jit(solution)/shard_map/ppermute | solution.py:34
  123.6 2.5 %copy-start.21 = (f32[8,130,1]{2,1,0:T(8,128)S(1)}, f32[8,130,1]{2,1,0:T(8,128)}, u32[]{:S(2)}) copy-start(f32[8,130,1]{2,1,0:T(8,128)} %copy.116) | copy-start | bytes 12484
  123.6 2.5 %copy-start.24 = (f32[8,130,1]{2,1,0:T(8,128)S(1)}, f32[8,130,1]{2,1,0:T(8,128)}, u32[]{:S(2)}) copy-start(f32[8,130,1]{2,1,0:T(8,128)} %copy.117) | copy-start | bytes 12484
  130.2 8.5 %copy-start.4 = (f32[8,128,256]{2,1,0:T(8,128)}, f32[8,128,256]{2,1,0:T(8,128)S(1)}, u32[]{:S(2)}) copy-start(f32[8,128,256]{2,1,0:T(8,128)S(1)} %get-tuple-element.3) | copy-start | bytes 3145732
  130.2 8.5 %copy-start.17 = (f32[1,8,128,256]{3,2,1,0:T(8,128)}, f32[1,8,128,256]{3,2,1,0:T(8,128)S(1)}, u32[]{:S(2)}) copy-start(f32[1,8,128,256]{3,2,1,0:T(8,128)S(1)} %get-tuple-element.2) | copy-start | bytes 3145732
  130.2 5.1 %collective-permute-start.16 = (f32[2,8,1,256]{3,2,1,0:T(1,128)S(1)}, f32[2,8,1,256]{3,2,1,0:T(1,128)S(1)}, u32[]{:S(2)}, u32[]{:S(2)}) collective-permute-start(f32[2,8,1,256]{3,2,1,0:T(1,128)S(1)} %get-tuple-element.16), channel_id=1, source_target_pairs={{0,1},{1,4},{4,5},{5,8},{8,9},{9,12},{12,13},{2,3},{3,6},{6,7},{7,... | collective-permute-start | bytes 49160 | tf_op jit(solution)/shard_map/ppermute | solution.py:32
  133.4 5.1 %collective-permute-start.17 = (f32[2,8,1,256]{3,2,1,0:T(1,128)S(1)}, f32[2,8,1,256]{3,2,1,0:T(1,128)S(1)}, u32[]{:S(2)}, u32[]{:S(2)}) collective-permute-start(f32[2,8,1,256]{3,2,1,0:T(1,128)S(1)} %get-tuple-element.17), channel_id=1, source_target_pairs={{1,0},{4,1},{5,4},{8,5},{9,8},{12,9},{13,12},{3,2},{6,3},{7,6},{10... | collective-permute-start | bytes 49160 | tf_op jit(solution)/shard_map/ppermute | solution.py:34
  140.1 10.2 %copy-start.5 = (f32[8,128,256]{2,1,0:T(8,128)S(1)}, f32[8,128,256]{2,1,0:T(8,128)}, u32[]{:S(2)}) copy-start(f32[8,128,256]{2,1,0:T(8,128)} %copy-done.4) | copy-start | bytes 3145732
  140.1 10.2 %copy-start.18 = (f32[1,8,128,256]{3,2,1,0:T(8,128)S(1)}, f32[1,8,128,256]{3,2,1,0:T(8,128)}, u32[]{:S(2)}) copy-start(f32[1,8,128,256]{3,2,1,0:T(8,128)} %copy-done.17) | copy-start | bytes 3145732
  142.1 3.5 %collective-permute-start.18 = (f32[2,8,130,1]{2,1,3,0:T(8,128)S(1)}, f32[2,8,130,1]{2,1,3,0:T(8,128)S(1)}, u32[]{:S(2)}, u32[]{:S(2)}) collective-permute-start(f32[2,8,130,1]{2,1,3,0:T(8,128)S(1)} %copy.120), channel_id=1, source_target_pairs={{0,2},{1,3},{4,6},{5,7},{8,10},{9,11},{12,14},{13,15},{16,18},{17,... | collective-permute-start | bytes 24968 | tf_op jit(solution)/shard_map/ppermute | solution.py:32
  144.0 4.8 %collective-permute-start.19 = (f32[2,8,130,1]{2,1,3,0:T(8,128)S(1)}, f32[2,8,130,1]{2,1,3,0:T(8,128)S(1)}, u32[]{:S(2)}, u32[]{:S(2)}) collective-permute-start(f32[2,8,130,1]{2,1,3,0:T(8,128)S(1)} %copy.121), channel_id=1, source_target_pairs={{2,0},{3,1},{6,4},{7,5},{10,8},{11,9},{14,12},{15,13},{18,16},{19,... | collective-permute-start | bytes 24968 | tf_op jit(solution)/shard_map/ppermute | solution.py:34
  159.8 9.4 %copy-start.15 = (f32[8,128,256]{2,1,0:T(8,128)}, f32[8,128,256]{2,1,0:T(8,128)S(1)}, u32[]{:S(2)}) copy-start(f32[8,128,256]{2,1,0:T(8,128)S(1)} %fusion.27) | copy-start | bytes 3145732
  159.8 5.0 %collective-permute-start.20 = (f32[8,1,256]{2,1,0:T(1,128)S(1)}, f32[8,1,256]{2,1,0:T(1,128)S(1)}, u32[]{:S(2)}, u32[]{:S(2)}) collective-permute-start(f32[8,1,256]{2,1,0:T(1,128)S(1)} %get-tuple-element.32), channel_id=1, source_target_pairs={{0,1},{1,4},{4,5},{5,8},{8,9},{9,12},{12,13},{2,3},{3,6},{6,7},{7,... | collective-permute-start | bytes 24584 | tf_op jit(solution)/shard_map/ppermute | solution.py:32
  162.9 5.0 %collective-permute-start.21 = (f32[8,1,256]{2,1,0:T(1,128)S(1)}, f32[8,1,256]{2,1,0:T(1,128)S(1)}, u32[]{:S(2)}, u32[]{:S(2)}) collective-permute-start(f32[8,1,256]{2,1,0:T(1,128)S(1)} %get-tuple-element.33), channel_id=1, source_target_pairs={{1,0},{4,1},{5,4},{8,5},{9,8},{12,9},{13,12},{3,2},{6,3},{7,6},{10... | collective-permute-start | bytes 24584 | tf_op jit(solution)/shard_map/ppermute | solution.py:34
  170.6 4.0 %collective-permute-start.22 = (f32[8,130,1]{1,0,2:T(8,128)S(1)}, f32[8,130,1]{1,0,2:T(8,128)S(1)}, u32[]{:S(2)}, u32[]{:S(2)}) collective-permute-start(f32[8,130,1]{1,0,2:T(8,128)S(1)} %copy.124), channel_id=1, source_target_pairs={{0,2},{1,3},{4,6},{5,7},{8,10},{9,11},{12,14},{13,15},{16,18},{17,... | collective-permute-start | bytes 12488 | tf_op jit(solution)/shard_map/ppermute | solution.py:32
  173.3 4.6 %collective-permute-start.23 = (f32[8,130,1]{1,0,2:T(8,128)S(1)}, f32[8,130,1]{1,0,2:T(8,128)S(1)}, u32[]{:S(2)}, u32[]{:S(2)}) collective-permute-start(f32[8,130,1]{1,0,2:T(8,128)S(1)} %copy.125), channel_id=1, source_target_pairs={{2,0},{3,1},{6,4},{7,5},{10,8},{11,9},{14,12},{15,13},{18,16},{19,... | collective-permute-start | bytes 12488 | tf_op jit(solution)/shard_map/ppermute | solution.py:34
  179.1 2.5 %copy-start.28 = (f32[8,130,1]{2,1,0:T(8,128)S(1)}, f32[8,130,1]{2,1,0:T(8,128)}, u32[]{:S(2)}) copy-start(f32[8,130,1]{2,1,0:T(8,128)} %copy.127) | copy-start | bytes 12484
  185.5 9.5 %copy-start.9 = (f32[8,128,256]{2,1,0:T(8,128)}, f32[8,128,256]{2,1,0:T(8,128)S(1)}, u32[]{:S(2)}) copy-start(f32[8,128,256]{2,1,0:T(8,128)S(1)} %fusion.17) | copy-start | bytes 3145732
  185.5 5.1 %collective-permute-start.24 = (f32[8,1,256]{2,1,0:T(1,128)S(1)}, f32[8,1,256]{2,1,0:T(1,128)S(1)}, u32[]{:S(2)}, u32[]{:S(2)}) collective-permute-start(f32[8,1,256]{2,1,0:T(1,128)S(1)} %get-tuple-element.30), channel_id=1, source_target_pairs={{0,1},{1,4},{4,5},{5,8},{8,9},{9,12},{12,13},{2,3},{3,6},{6,7},{7,... | collective-permute-start | bytes 24584 | tf_op jit(solution)/shard_map/ppermute | solution.py:32
  188.6 5.0 %collective-permute-start.25 = (f32[8,1,256]{2,1,0:T(1,128)S(1)}, f32[8,1,256]{2,1,0:T(1,128)S(1)}, u32[]{:S(2)}, u32[]{:S(2)}) collective-permute-start(f32[8,1,256]{2,1,0:T(1,128)S(1)} %get-tuple-element.31), channel_id=1, source_target_pairs={{1,0},{4,1},{5,4},{8,5},{9,8},{12,9},{13,12},{3,2},{6,3},{7,6},{10... | collective-permute-start | bytes 24584 | tf_op jit(solution)/shard_map/ppermute | solution.py:34
  196.3 4.1 %collective-permute-start.26 = (f32[8,130,1]{1,0,2:T(8,128)S(1)}, f32[8,130,1]{1,0,2:T(8,128)S(1)}, u32[]{:S(2)}, u32[]{:S(2)}) collective-permute-start(f32[8,130,1]{1,0,2:T(8,128)S(1)} %copy.130), channel_id=1, source_target_pairs={{0,2},{1,3},{4,6},{5,7},{8,10},{9,11},{12,14},{13,15},{16,18},{17,... | collective-permute-start | bytes 12488 | tf_op jit(solution)/shard_map/ppermute | solution.py:32
  199.1 4.6 %collective-permute-start.27 = (f32[8,130,1]{1,0,2:T(8,128)S(1)}, f32[8,130,1]{1,0,2:T(8,128)S(1)}, u32[]{:S(2)}, u32[]{:S(2)}) collective-permute-start(f32[8,130,1]{1,0,2:T(8,128)S(1)} %copy.131), channel_id=1, source_target_pairs={{2,0},{3,1},{6,4},{7,5},{10,8},{11,9},{14,12},{15,13},{18,16},{19,... | collective-permute-start | bytes 12488 | tf_op jit(solution)/shard_map/ppermute | solution.py:34
  204.8 2.5 %copy-start.26 = (f32[8,130,1]{2,1,0:T(8,128)S(1)}, f32[8,130,1]{2,1,0:T(8,128)}, u32[]{:S(2)}) copy-start(f32[8,130,1]{2,1,0:T(8,128)} %copy.133) | copy-start | bytes 12484
  (15 other events, 30.1 us)
where the time goes:
time: 220 us; the launch traced here: 217 us
  starting transfers between devices  56.9 us (26%)
  local copies, waits for them, and re-layouts  54.1 us (25%)
  other arithmetic  46.5 us (21%)
  waiting for transfers between devices  40.6 us (18%)
  blocking collectives  17.1 us (8%)
    ppermute x12, waiting for transfers between devices, padded_2(): lax.ppermute(head, axis, [((i + 1) % count, i) for i in range(ends)])  29.4 us
    ppermute x12, starting transfers between devices, padded_2(): lax.ppermute(tail, axis, [(i, (i + 1) % count) for i in range(ends)])  29 us
    ppermute x12, starting transfers between devices, padded_2(): lax.ppermute(head, axis, [((i + 1) % count, i) for i in range(ends)])  19.7 us
    concatenate x12, other arithmetic, padded_2(): jnp.concatenate([lax.ppermute(tail, axis, [(i, (i + 1) % count) for i in...  19.7 us
    div x5, other arithmetic, sweep(): return total / denom  18.9 us
    slice x16, local copies, waits for them, and re-layouts, padded_2(): lax.slice_in_dim(cells, cells.shape[dim] - width, cells.shape[dim], axis=...  17 us
    ppermute x4, waiting for transfers between devices, from_behind(): lax.ppermute(value, axis, [(source, source + steps) for source in range(f...  11.2 us
    ppermute x4, starting transfers between devices, from_behind(): lax.ppermute(value, axis, [(source, source + steps) for source in range(f...  8.25 us
  transfers between devices with their start and end apart: 28, of which 13 were waited for; matrix products, arithmetic and copies ran while one was open for 15% of the time, Pallas kernels for 0%

commit v1 on v0

v1 whole, which is shorter than its diff:
```python
import functools

import jax
import jax.numpy as jnp
from jax import lax
from jax.experimental import pallas as pl
from jax.experimental.pallas import tpu as pltpu
from jax.sharding import PartitionSpec as P

RIM = 64
TILE = 64
STEPS = 2
SWEEPS = 3
COOLANT = 2.0

LANES = 128
WIDE = 6
LOCAL = 200
REGION = 144
EDGE = 72
ROWS_P = 2 * EDGE + 8 + 16
ROWS_G = EDGE + 16
ROWS_D = 40
F32 = jnp.float32
VMEM = pl.BlockSpec(memory_space=pltpu.VMEM)
SMEM = pl.BlockSpec(memory_space=pltpu.SMEM)
ANY = pl.BlockSpec(memory_space=pl.ANY)
PARAMS = pltpu.CompilerParams(vmem_limit_bytes=48 << 20)


def rows8(start):
    return pl.ds(pl.multiple_of(start, 8), 8)


def lane_ids():
    return lax.broadcasted_iota(jnp.int32, (8, LANES), 1)


def turn(value, shift):
    shift = shift % LANES
    return pltpu.roll(value, shift, 1) if shift else value


def decode_kernel(mantissa, exponent, own, sent, plain, own_sem, sent_sem):
    core = lax.axis_index("ta")
    depth, rows, _ = mantissa.shape
    tiles = rows // TILE
    wide_lane = lax.broadcasted_iota(jnp.int32, (16, LANES), 1)
    first = pl.multiple_of(core * 184, 8)
    other = pl.multiple_of(184 - core * 184, 8)

    def copies(layer):
        return (
            pltpu.make_async_copy(plain.at[layer, :, pl.ds(other, LOCAL), :], sent.at[layer], sent_sem.at[layer]),
            pltpu.make_async_copy(plain.at[layer, :, pl.ds(first, LOCAL), :], own.at[layer], own_sem.at[layer]),
        )

    for layer in range(depth):

        @pl.loop(0, tiles)
        def _(tile_row):
            for col in range(3):
                low = exponent[layer, tile_row, 2 * col]
                high = exponent[layer, tile_row, 2 * col + 1]
                scale = jnp.exp2(jnp.where(wide_lane < TILE, low, high).astype(F32))
                for part in range(TILE // 16):
                    where = pl.ds(pl.multiple_of(tile_row * TILE + part * 16, 16), 16)
                    cells = mantissa[layer, where, col * LANES : (col + 1) * LANES]
                    plain[layer, col, where, :] = cells.astype(F32) * scale

        for copy in copies(layer):
            copy.start()
    for layer in range(depth):
        for copy in copies(layer):
            copy.wait()


def pack_kernel(sides, own, other, t_own, t_other, *outs):
    core = lax.axis_index("ta")
    lane = lane_ids()
    low = lane < 64
    to_p, to_g, to_d = outs[0], outs[1 : 1 + len(sides)], outs[1 + len(sides) :]
    edge = core * 128
    region = 56 - core * 56
    t_row = core * 120
    t_edge = core * 248

    def place(total, value, source, target, width):
        moved = turn(value, target - source)
        return jnp.where((lane >= target) & (lane < target + width), moved, total)

    def one(src, t_src, index, layer):
        def cells(col, row):
            return src[index, col, rows8(row), :]

        def t_cells(col, row):
            return t_src[index, rows8(row), col * LANES : (col + 1) * LANES]

        extra = jnp.zeros((8, LANES), F32)
        for j in range(9):
            left, right = cells(0, edge + 8 * j), cells(2, edge + 8 * j)
            to_p[layer, 8 * j : 8 * j + 8, :] = cells(1, edge + 8 * j)
            to_p[layer, EDGE + 8 * j : EDGE + 8 * j + 8, :] = jnp.where(low, right, left)
            extra = place(extra, jnp.where(low, left, right), 64 - WIDE, 2 * WIDE * j, 2 * WIDE)
        to_p[layer, 2 * EDGE : 2 * EDGE + 8, :] = extra
        for col in range(2):
            start = 2 * EDGE + 8 + 8 * col
            to_p[layer, start : start + 8, :] = t_cells(col, t_edge)

        def side_parts(right, g_ref, d_ref):
            col, t_col = (2, 1) if right else (0, 0)
            at, t_at = (LANES - WIDE, LANES - WIDE) if right else (64, 0)

            def strip(row):
                value = cells(col, row)
                return turn(value, 64) if right else value

            extra = jnp.zeros((8, LANES), F32)
            for j in range(9):
                one_strip, two_strip = strip(region + 8 * j), strip(region + EDGE + 8 * j)
                g_ref[layer, 8 * j : 8 * j + 8, :] = jnp.where(low, one_strip, turn(two_strip, 64))
                extra = place(extra, one_strip, at, WIDE * j, WIDE)
                extra = place(extra, two_strip, at, WIDE * (j + 9), WIDE)
            g_ref[layer, EDGE : EDGE + 8, :] = extra
            extra = jnp.zeros((8, LANES), F32)
            for j in range(17):
                extra = place(extra, t_cells(t_col, t_row + 8 * j), t_at, WIDE * j, WIDE)
            g_ref[layer, EDGE + 8 : EDGE + 16, :] = extra
            strips = [strip(edge + 8 * j) for j in range(9)]
            for j in range(4):
                d_ref[layer, 8 * j : 8 * j + 8, :] = jnp.where(low, strips[j], turn(strips[j + 5], 64))
            extra = strips[4]
            for j in range(9):
                extra = place(extra, strips[j], at, 64 + WIDE * j, WIDE)
            extra = place(extra, t_cells(t_col, t_edge), t_at, 64 + 9 * WIDE, WIDE)
            d_ref[layer, 32:40, :] = extra

        for side, g_ref, d_ref in zip(sides, to_g, to_d):
            if side is None:
                first = lax.axis_index("gy") == 0
                pl.when(first)(functools.partial(side_parts, True, g_ref, d_ref))
                pl.when(jnp.logical_not(first))(functools.partial(side_parts, False, g_ref, d_ref))
            else:
                side_parts(side, g_ref, d_ref)

    depth = own.shape[0]

    @pl.loop(0, depth)
    def _(index):
        one(own, t_own, index, core * depth + index)
        one(other, t_other, index, (1 - core) * depth + index)


def solve_kernel(sides, bounds, *refs):
    count = len(sides)
    from_p, refs = refs[0], refs[1:]
    from_g, from_d, refs = refs[:count], refs[count : 2 * count], refs[2 * count :]
    own, other, t_own, t_other, flow, material, conductivity = refs[:7]
    t_out, h_out, sent = refs[7:10]
    heat, now, later, cond, f_up, f_down, f_right, f_above, inverse, base, t_stage, h_stage, sems = refs[10:]
    core = lax.axis_index("ta")
    lane = lane_ids()
    row_id = lax.broadcasted_iota(jnp.int32, (8, LANES), 0)
    low = lane < 64
    zero = jnp.zeros((8, LANES), F32)
    depth = own.shape[0]
    layers = 2 * depth
    region = 56 - core * 56
    edge = core * EDGE
    tiles = REGION // 8
    t_row = core * 120
    t_first = 8 - core * 8
    t_halo = core * (REGION - 8)
    row_start = lax.axis_index("gx") * 256 + core * 128 - 8
    col_start = lax.axis_index("gy") * 256 - 64

    def inside(row, col):
        rows = row_id + (row_start + row)
        cols = lane + (col_start + col * LANES)
        ok = (rows >= 0) & (rows < bounds[0]) & (cols >= 0) & (cols < bounds[1])
        return jnp.where(ok, 1.0, 0.0)

    def spread(t_left, t_right):
        one, two = turn(t_left, 64), turn(t_right, 64)
        return jnp.where(low, zero, one), jnp.where(low, one, two), jnp.where(low, two, zero)

    def gather(src, t_src, index, layer):
        for j in range(tiles):
            for col in range(3):
                heat[layer * 3 + col, 8 * j : 8 * j + 8, :] = src[index, col, rows8(region + 8 * j), :]
        for j in range(17):
            row = rows8(t_row + 8 * j)
            parts = spread(t_src[index, row, :LANES], t_src[index, row, LANES:])
            for col in range(3):
                now[layer * 3 + col, rows8(8 + t_first + 8 * j), :] = parts[col]

    @pl.loop(0, depth)
    def _(index):
        gather(own, t_own, index, core * depth + index)
        gather(other, t_other, index, (1 - core) * depth + index)

    def add_side(layer, right, g_ref, d_ref):
        col = 2 if right else 0
        target = 64 if right else 64 - WIDE

        def put(ref, row, value):
            ref[layer * 3 + col, row, :] = ref[layer * 3 + col, row, :] + value

        def merge(main, extra, at):
            moved = turn(extra, target - at)
            if right:
                return jnp.where(low, main, jnp.where(lane < 64 + WIDE, moved, 0.0))
            return jnp.where(low, jnp.where(lane >= 64 - WIDE, moved, 0.0), main)

        def only(extra, at):
            moved = turn(extra, target - at)
            return jnp.where((lane >= target) & (lane < target + WIDE), moved, 0.0)

        extra = g_ref[layer, EDGE : EDGE + 8, :]
        for j in range(9):
            main = g_ref[layer, 8 * j : 8 * j + 8, :]
            turned = turn(main, 64)
            one, two = (main, turned) if right else (turned, main)
            put(heat, pl.ds(8 * j, 8), merge(one, extra, WIDE * j))
            put(heat, pl.ds(EDGE + 8 * j, 8), merge(two, extra, WIDE * (j + 9)))
        extra = g_ref[layer, EDGE + 8 : EDGE + 16, :]
        for j in range(17):
            put(now, rows8(8 + t_first + 8 * j), only(extra, WIDE * j))
        extra = d_ref[layer, 32:40, :]
        for j in range(9):
            main = d_ref[layer, 8 * (j % 5) : 8 * (j % 5) + 8, :]
            if (j < 5) != right:
                main = turn(main, 64)
            put(heat, rows8(edge + 8 * j), merge(main, extra, 64 + WIDE * j))
        put(now, rows8(8 + t_halo), only(extra, 64 + 9 * WIDE))

    @pl.loop(0, layers)
    def _(layer):
        extra = from_p[layer, 2 * EDGE : 2 * EDGE + 8, :]
        for j in range(9):
            row = rows8(edge + 8 * j)
            middle = from_p[layer, 8 * j : 8 * j + 8, :]
            ends = from_p[layer, EDGE + 8 * j : EDGE + 8 * j + 8, :]
            moved = turn(extra, 64 - WIDE - 2 * WIDE * j)
            left = jnp.where(low, jnp.where(lane >= 64 - WIDE, moved, 0.0), ends)
            right = jnp.where(low, ends, jnp.where(lane < 64 + WIDE, moved, 0.0))
            for col, value in enumerate((left, middle, right)):
                heat[layer * 3 + col, row, :] = heat[layer * 3 + col, row, :] + value
        start = 2 * EDGE + 8
        parts = spread(from_p[layer, start : start + 8, :], from_p[layer, start + 8 : start + 16, :])
        for col in range(3):
            now[layer * 3 + col, rows8(8 + t_halo), :] = parts[col]
            for ref in (now, later, cond):
                ref[layer * 3 + col, 0:8, :] = zero
                ref[layer * 3 + col, REGION + 8 : REGION + 16, :] = zero
        for side, g_ref, d_ref in zip(sides, from_g, from_d):
            if side is None:
                first = lax.axis_index("gy") == 0
                pl.when(first)(functools.partial(add_side, layer, True, g_ref, d_ref))
                pl.when(jnp.logical_not(first))(functools.partial(add_side, layer, False, g_ref, d_ref))
            else:
                add_side(layer, side, g_ref, d_ref)

    def to_stage(stage, layer, row, parts):
        turned = [turn(part, 64) for part in parts]
        for col in range(2):
            value = jnp.where(low, turned[col], turned[col + 1])
            stage[layer, rows8(row), col * LANES : (col + 1) * LANES] = value

    def outputs(stage, which, out):
        mine = stage.at[pl.ds(core * depth, depth)]
        theirs = stage.at[pl.ds((1 - core) * depth, depth)]
        half = stage.shape[1]
        place = pl.ds(pl.multiple_of(core * half, half), half)
        return (
            pltpu.make_async_copy(theirs, sent.at[which], sems.at[which, 0]),
            pltpu.make_async_copy(mine, out.at[:, place, :], sems.at[which, 1]),
        )

    @pl.loop(0, 16)
    def _(tile):
        for layer in range(layers):
            to_stage(h_stage, layer, 8 * tile, [heat[layer * 3 + col, rows8(8 + 8 * tile), :] for col in range(3)])

    for copy in outputs(h_stage, 1, h_out):
        copy.start()

    def neighbours_right(values):
        moved = [turn(value, -1) for value in values]
        last = lane == LANES - 1
        return [jnp.where(last, moved[col + 1], moved[col]) if col < 2 else moved[col] for col in range(3)]

    def neighbours_left(values):
        moved = [turn(value, 1) for value in values]
        first = lane == 0
        return [jnp.where(first, moved[col - 1], moved[col]) if col > 0 else moved[col] for col in range(3)]

    def conductances():
        @pl.loop(0, tiles)
        def _(tile):
            masks = [inside(8 * tile, col) for col in range(3)]
            row = rows8(8 + 8 * tile)
            for layer in range(layers):
                scale = conductivity[material[layer]]
                for col in range(3):
                    n = layer * 3 + col
                    cond[n, row, :] = scale * (1.0 + 0.5 * jnp.tanh(now[n, row, :])) * masks[col]

    def coefficients():
        @pl.loop(0, tiles)
        def _(tile):
            masks = [inside(8 * tile, col) for col in range(3)]
            row, inner = rows8(8 + 8 * tile), rows8(8 * tile)
            below = [zero] * 3
            here = [cond[col, row, :] for col in range(3)]
            for layer in range(layers):
                if layer + 1 < layers:
                    above = [cond[layer * 3 + 3 + col, row, :] for col in range(3)]
                else:
                    above = [zero] * 3
                rights, lefts = neighbours_right(here), neighbours_left(here)
                for col in range(3):
                    n = layer * 3 + col
                    centre = here[col]
                    up = 0.5 * (centre + cond[n, pl.ds(8 * tile + 7, 8), :]) + flow[n : n + 1, :]
                    down = 0.5 * (centre + cond[n, pl.ds(8 * tile + 9, 8), :])
                    right = 0.5 * (centre + rights[col])
                    left = 0.5 * (centre + lefts[col])
                    over = centre + above[col]
                    under = centre + below[col]
                    total = 1.0 + up + down + right + left + over + under
                    f_up[n, inner, :] = up
                    f_down[n, inner, :] = down
                    f_right[n, inner, :] = right
                    f_above[n, inner, :] = over
                    inverse[n, inner, :] = masks[col] / total
                    base[n, inner, :] = now[n, row, :] + heat[n, inner, :]
                below, here = here, above

    def sweep(src, dst):
        @pl.loop(0, tiles)
        def _(tile):
            row, inner = rows8(8 + 8 * tile), rows8(8 * tile)
            below, f_below = None, None
            here = [src[col, row, :] for col in range(3)]
            for layer in range(layers):
                f_over = [f_above[layer * 3 + col, inner, :] for col in range(3)]
                above = None
                if layer + 1 < layers:
                    above = [src[layer * 3 + 3 + col, row, :] for col in range(3)]
                f_side = [f_right[layer * 3 + col, inner, :] for col in range(3)]
                rights = neighbours_right(here)
                lefts = neighbours_left([f * v for f, v in zip(f_side, here)])
                for col in range(3):
                    n = layer * 3 + col
                    total = base[n, inner, :] + f_up[n, inner, :] * src[n, pl.ds(8 * tile + 7, 8), :]
                    total = total + f_down[n, inner, :] * src[n, pl.ds(8 * tile + 9, 8), :]
                    total = total + (f_side[col] * rights[col] + lefts[col])
                    if above is not None:
                        total = total + f_over[col] * above[col]
                    if below is not None:
                        total = total + f_below[col] * below[col]
                    dst[n, row, :] = total * inverse[n, inner, :]
                below, here, f_below = here, above, f_over

    refs_now, refs_later = now, later
    for step in range(STEPS):
        if step:
            now = refs_now
        conductances()
        coefficients()
        for _ in range(SWEEPS):
            sweep(refs_now, refs_later)
            refs_now, refs_later = refs_later, refs_now

    @pl.loop(0, 16)
    def _(tile):
        for layer in range(layers):
            to_stage(t_stage, layer, 8 * tile, [refs_now[layer * 3 + col, rows8(16 + 8 * tile), :] for col in range(3)])

    for copy in outputs(t_stage, 0, t_out):
        copy.start()
    for copy in outputs(h_stage, 1, h_out) + outputs(t_stage, 0, t_out):
        copy.wait()


def place_kernel(received, t_in, h_in, t_out, h_out, sems):
    core = lax.axis_index("ta")
    half = received.shape[2]
    place = pl.ds(pl.multiple_of((1 - core) * half, half), half)
    copies = [
        pltpu.make_async_copy(received.at[which], out.at[:, place, :], sems.at[which])
        for which, out in enumerate((t_out, h_out))
    ]
    for copy in copies:
        copy.start()
    for copy in copies:
        copy.wait()


def on_device(t_initial, power_mantissa, tile_exponent, channel_mask, material, conductivity):
    depth, rows, cols = t_initial.shape
    layers = 2 * depth
    n_gx, n_gy = lax.axis_size("gx"), lax.axis_size("gy")
    array = jax.ShapeDtypeStruct
    swap = [(0, 1), (1, 0)]

    t_other = lax.ppermute(t_initial, "ta", swap)
    local = array((depth, 3, LOCAL, LANES), F32)
    own, sent = pl.pallas_call(
        decode_kernel,
        out_shape=(local, local),
        in_specs=[VMEM, SMEM],
        out_specs=(ANY, ANY),
        scratch_shapes=[
            pltpu.VMEM((depth, 3, rows + 2 * RIM, LANES), F32),
            pltpu.SemaphoreType.DMA((depth,)),
            pltpu.SemaphoreType.DMA((depth,)),
        ],
        compiler_params=PARAMS,
        name="decode",
    )(power_mantissa, tile_exponent)
    other = lax.ppermute(sent, "ta", swap)

    out_sides = [None] if n_gy == 2 else [True, False]
    count = len(out_sides)
    packed = pl.pallas_call(
        functools.partial(pack_kernel, out_sides),
        out_shape=(array((layers, ROWS_P, LANES), F32),)
        + (array((layers, ROWS_G, LANES), F32),) * count
        + (array((layers, ROWS_D, LANES), F32),) * count,
        in_specs=[VMEM] * 4,
        out_specs=(VMEM,) * (1 + 2 * count),
        compiler_params=PARAMS,
        name="pack",
    )(own, other, t_initial, t_other)

    def moves(shift):
        pairs = []
        for z in range(n_gx):
            for x in range(n_gy):
                for c in range(2):
                    to_z = z + 2 * c - 1
                    to_x = x ^ 1 if shift is None else x + shift
                    if 0 <= to_z < n_gx and 0 <= to_x < n_gy:
                        pairs.append(((z * n_gy + x) * 2 + c, (to_z * n_gy + to_x) * 2 + 1 - c))
        return pairs

    along = ("gx", "gy", "ta")
    shifts = [None] if n_gy == 2 else [1, -1]
    from_g = []
    for shift, value in zip(shifts, packed[1 : 1 + count]):
        pairs = swap if shift is None else [(x, x + shift) for x in range(n_gy) if 0 <= x + shift < n_gy]
        from_g.append(lax.ppermute(value, "gy", pairs))
    from_d = [lax.ppermute(value, along, moves(shift)) for shift, value in zip(shifts, packed[1 + count :])]
    from_p = lax.ppermute(packed[0], along, moves(0))
    in_sides = [None] if n_gy == 2 else [False, True]

    wide = jnp.pad(channel_mask, ((0, 0), (RIM, RIM)))
    mask = lax.dynamic_slice_in_dim(wide, lax.axis_index("gy") * cols, cols + 2 * RIM, 1)
    flow = COOLANT * mask.astype(F32).reshape(layers * 3, LANES)

    whole = array((depth, rows, cols), F32)
    half = array((2, depth, rows // 2, cols), F32)
    inner = pltpu.VMEM((layers * 3, REGION, LANES), F32)
    outer = pltpu.VMEM((layers * 3, REGION + 16, LANES), F32)
    stage = pltpu.VMEM((layers, rows // 2, cols), F32)
    t_part, h_part, sent = pl.pallas_call(
        functools.partial(solve_kernel, in_sides, (n_gx * rows, n_gy * cols)),
        out_shape=(whole, whole, half),
        in_specs=[VMEM] * (1 + 2 * count + 5) + [SMEM, SMEM],
        out_specs=(ANY, ANY, ANY),
        scratch_shapes=[inner, outer, outer, outer] + [inner] * 6 + [stage, stage, pltpu.SemaphoreType.DMA((2, 2))],
        compiler_params=PARAMS,
        name="solve",
    )(from_p, *from_g, *from_d, own, other, t_initial, t_other, flow, material, conductivity)
    received = lax.ppermute(sent, "ta", swap)
    return pl.pallas_call(
        place_kernel,
        out_shape=(whole, whole),
        in_specs=[ANY, ANY, ANY],
        out_specs=(ANY, ANY),
        scratch_shapes=[pltpu.SemaphoreType.DMA((2,))],
        input_output_aliases={1: 0, 2: 1},
        compiler_params=PARAMS,
        name="place",
    )(received, t_part, h_part)


def solution(mesh):
    cells = P("ta", ("group", "gx"), "gy")
    return jax.shard_map(
        on_device,
        mesh=mesh,
        in_specs=(cells, cells, cells, P(), P(), P()),
        out_specs=(cells, cells),
        check_vma=False,
    )
```

time: 220 us -> 66.6 us (0.30); the launches traced: 217 us -> 66.3 us
  starting transfers between devices: 56.9 us -> 8.17 us
  local copies, waits for them, and re-layouts: 54.1 us -> 6.99 us
  other arithmetic: 46.5 us -> 0.08 us
  Pallas kernels: 0 us -> 34 us
  waiting for transfers between devices: 40.6 us -> 16.3 us
  blocking collectives: 17.1 us -> 0 us
    ppermute x28 -> x6, starting transfers between devices: 56.9 us -> 8.17 us  [the longest x1 3.45 us: on_device(): from_p = lax.ppermute(packed[0], along, moves(0))]
    pallas_call x0 -> x4, Pallas kernels: none -> 34 us  [the longest x1 28.2 us: on_device(): pl.pallas_call(functools.partial(solve_kernel, in_sides, (n_gx * rows, n_...]
    slice x24 -> x0, local copies, waits for them, and re-layouts: 24.9 us -> none  [the longest x16 17 us: padded_2(): lax.slice_in_dim(cells, cells.shape[dim] - width, cells.shape[dim], axis=...]
    ppermute x28 -> x6, waiting for transfers between devices: 40.6 us -> 16.3 us  [the longest x1 8.96 us: on_device(): lax.ppermute(value, along, moves(shift))]
    concatenate x12 -> x0, other arithmetic: 19.7 us -> none  [padded_2(): jnp.concatenate([lax.ppermute(tail, axis, [(i, (i + 1) % count) for i in...]
    div x5 -> x0, other arithmetic: 18.9 us -> none  [sweep(): return total / denom]
    all_to_all x3 -> x0, blocking collectives: 17.1 us -> none  [the longest x1 7.65 us: on_device(): lax.all_to_all(power, 'ta', split_axis=1, concat_axis=0, tiled=True)]
    ppermute x12 -> x0, local copies, waits for them, and re-layouts: 12.4 us -> none  [the longest x6 7.24 us: padded_2(): lax.ppermute(head, axis, [((i + 1) % count, i) for i in range(ends)])]
  transfers between devices with their start and end apart: 28 -> 6, of which waited for: 13 -> 4; matrix products, arithmetic and copies ran while one was open for 15% -> 0% of each run, Pallas kernels for 0% -> 0%
where the time goes in v1:
time: 66.6 us; the launch traced here: 66.3 us
  Pallas kernels  34 us (51%)
  waiting for transfers between devices  16.3 us (24%)
  starting transfers between devices  8.17 us (12%)
  local copies, waits for them, and re-layouts  6.99 us (10%)
  between operations  0.73 us (1%)
    pallas_call x1, Pallas kernels, on_device(): pl.pallas_call(functools.partial(solve_kernel, in_sides, (n_gx * rows, n_...  28.2 us
    ppermute x1, waiting for transfers between devices, on_device(): lax.ppermute(value, along, moves(shift))  8.96 us
    unnamed x25, local copies, waits for them, and re-layouts  6.98 us
    ppermute x1, waiting for transfers between devices, on_device(): t_other = lax.ppermute(t_initial, 'ta', swap)  4.18 us
    ppermute x1, starting transfers between devices, on_device(): from_p = lax.ppermute(packed[0], along, moves(0))  3.45 us
    pallas_call x1, Pallas kernels, on_device(): pl.pallas_call(functools.partial(pack_kernel, out_sides), out_shape=(arra...  3.32 us
    ppermute x1, starting transfers between devices, on_device(): lax.ppermute(value, along, moves(shift))  2.87 us
    ppermute x1, waiting for transfers between devices, on_device(): received = lax.ppermute(sent, 'ta', swap)  2.44 us
  transfers between devices with their start and end apart: 6, of which 4 were waited for; matrix products, arithmetic and copies ran while one was open for 0% of the time, Pallas kernels for 0%

profile of v1, /device:TPU:21, one launch (start us, length us, event | category | flops | bytes accessed | tf_op | source)
XLA Modules:
  0.0 66.3 jit_solution(14997901489003732655)
XLA Ops:
  0.6 0.0 copy-start.1
  0.6 0.8 %copy.10.exponent = s32[4,6,6]{2,1,0:T(8,128)S(1)} copy(s32[4,6,6]{2,0,1:T(4,128)} %param.8) | data formatting | bytes 1152 | tf_op args[2]
  1.4 0.0 copy-start.4
  1.4 1.3 %copy-done.4 = bf16[4,384,384]{2,1,0:T(8,128)(2,1)S(1)} copy-done((bf16[4,384,384]{2,1,0:T(8,128)(2,1)S(1)}, bf16[4,384,384]{2,1,0:T(8,128)(2,1)}, u32[]{:S(2)}) %copy-start.4) | copy-done | bytes 1179672
  2.7 1.6 %decode.1 = (f32[4,3,200,128]{3,2,1,0:T(8,128)S(1)}, f32[4,3,200,128]{3,2,1,0:T(8,128)S(1)}) custom-call(bf16[4,384,384]{2,1,0:T(8,128)(2,1)S(1)} %copy-done.4, s32[4,6,6]{2,1,0:T(8,128)S(1)} %copy.10.exponent), custom_call_target="tpu_custom_call" | custom-call | tf_op jit(solution)/shard_map/decode/pallas_call | solution.py:410
  4.3 0.7 %collective-permute-start = (f32[4,3,200,128]{3,2,1,0:T(8,128)S(1)}, f32[4,3,200,128]{3,2,1,0:T(8,128)S(1)}, u32[]{:S(2)}, u32[]{:S(2)}) collective-permute-start(f32[4,3,200,128]{3,2,1,0:T(8,128)S(1)} %get-tuple-element.11), channel_id=1, source_target_pairs={{0,1},{1,0},{2,3},{3,2},{4,5},{5,4},{6,7},{7,6},{8,9},{9,8},{10,11... | collective-permute-start | bytes 3686408 | tf_op jit(solution)/shard_map/ppermute | solution.py:423
  5.0 0.1 collective-permute-start.1
  5.1 4.2 %collective-permute-done.1.t_other.refs_6_ = f32[4,256,256]{2,1,0:T(8,128)S(1)} collective-permute-done((f32[4,256,256]{2,1,0:T(8,128)}, f32[4,256,256]{2,1,0:T(8,128)S(1)}, u32[]{:S(2)}, u32[]{:S(2)}) %collective-permute-start.1) | collective-permute-done | bytes 1048608 | tf_op jit(solution)/shard_map/ppermute | solution.py:408
  9.3 0.0 copy-start.2
  9.3 0.0 collective-permute-done.other.refs_4_
  9.3 0.0 copy-start
  9.3 0.0 copy-done.1
  9.3 0.0 copy-start.11
  9.3 0.0 copy-start.9
  9.3 0.0 copy-start.10
  9.3 3.3 %pack.1 = (f32[8,168,128]{2,1,0:T(8,128)}, f32[8,88,128]{2,1,0:T(8,128)}, f32[8,40,128]{2,1,0:T(8,128)}) custom-call(f32[4,3,200,128]{3,2,1,0:T(8,128)S(1)} %get-tuple-element.10.own.refs_3_, f32[4,3,200,128]{3,2,1,0:T(8,128)S(1)} %collective-permute-done.other.refs_4_, f32[4,256,256]{2,1,0:T(8,128)S(1)} %copy-done.1, ...), custom_call_target="tpu_custom_call" | custom-call | tf_op jit(solution)/shard_map/pack/pallas_call | solution.py:427
  12.7 0.0 copy-done.2
  12.7 0.0 copy-done
  12.7 3.5 %collective-permute-start.2 = (f32[8,168,128]{2,1,0:T(8,128)}, f32[8,168,128]{2,1,0:T(8,128)S(1)}, u32[]{:S(2)}, u32[]{:S(2)}) collective-permute-start(f32[8,168,128]{2,1,0:T(8,128)} %get-tuple-element.12), channel_id=1, source_target_pairs={{1,4},{3,6},{4,1},{5,8},{6,3},{7,10},{8,5},{9,12},{10,7},{11,14},{... | collective-permute-start | bytes 2064392 | tf_op jit(solution)/shard_map/ppermute | solution.py:456
  16.1 0.7 %collective-permute-start.3 = (f32[8,88,128]{2,1,0:T(8,128)}, f32[8,88,128]{2,1,0:T(8,128)S(1)}, u32[]{:S(2)}, u32[]{:S(2)}) collective-permute-start(f32[8,88,128]{2,1,0:T(8,128)} %get-tuple-element.13), channel_id=1, source_target_pairs={{0,2},{2,0},{1,3},{3,1},{4,6},{6,4},{5,7},{7,5},{8,10},{10,8},{9,1... | collective-permute-start | bytes 1081352 | tf_op jit(solution)/shard_map/ppermute | solution.py:454
  16.9 2.9 %collective-permute-start.4 = (f32[8,40,128]{2,1,0:T(8,128)}, f32[8,40,128]{2,1,0:T(8,128)S(1)}, u32[]{:S(2)}, u32[]{:S(2)}) collective-permute-start(f32[8,40,128]{2,1,0:T(8,128)} %get-tuple-element.14), channel_id=1, source_target_pairs={{1,6},{3,4},{4,3},{5,10},{6,1},{7,8},{8,7},{9,14},{10,5},{11,12},{... | collective-permute-start | bytes 491528 | tf_op jit(solution)/shard_map/ppermute | solution.py:455
  19.8 0.0 copy-done.11
  19.8 0.1 fusion.1
  19.9 9.0 %collective-permute-done.4.refs_2_ = f32[8,40,128]{2,1,0:T(8,128)S(1)} collective-permute-done((f32[8,40,128]{2,1,0:T(8,128)}, f32[8,40,128]{2,1,0:T(8,128)S(1)}, u32[]{:S(2)}, u32[]{:S(2)}) %collective-permute-start.4) | collective-permute-done | bytes 163872 | tf_op jit(solution)/shard_map/ppermute | solution.py:455
  28.8 0.7 %collective-permute-done.3.refs_1_ = f32[8,88,128]{2,1,0:T(8,128)S(1)} collective-permute-done((f32[8,88,128]{2,1,0:T(8,128)}, f32[8,88,128]{2,1,0:T(8,128)S(1)}, u32[]{:S(2)}, u32[]{:S(2)}) %collective-permute-start.3) | collective-permute-done | bytes 360480 | tf_op jit(solution)/shard_map/ppermute | solution.py:454
  29.5 0.0 copy-start.7
  29.5 0.7 %copy-done.7 = f32[8,88,128]{2,1,0:T(8,128)} copy-done((f32[8,88,128]{2,1,0:T(8,128)}, f32[8,88,128]{2,1,0:T(8,128)S(1)}, u32[]{:S(2)}) %copy-start.7) | copy-done | bytes 360472
  30.3 0.0 collective-permute-done.2.refs_0_
  30.3 0.0 copy-start.5
  30.3 0.8 %copy-done.5 = f32[8,168,128]{2,1,0:T(8,128)} copy-done((f32[8,168,128]{2,1,0:T(8,128)}, f32[8,168,128]{2,1,0:T(8,128)S(1)}, u32[]{:S(2)}) %copy-start.5) | copy-done | bytes 688152
  31.1 0.0 copy-done.9
  31.1 0.0 copy-done.10
  31.1 0.0 copy-start.3
  31.1 1.2 %copy-done.3 = f32[4,256,256]{2,1,0:T(8,128)S(1)} copy-done((f32[4,256,256]{2,1,0:T(8,128)S(1)}, f32[4,256,256]{2,1,0:T(8,128)}, u32[]{:S(2)}) %copy-start.3) | copy-done | bytes 1048600
  32.3 0.0 copy-start.6
  32.3 1.1 %copy-done.6 = f32[8,168,128]{2,1,0:T(8,128)S(1)} copy-done((f32[8,168,128]{2,1,0:T(8,128)S(1)}, f32[8,168,128]{2,1,0:T(8,128)}, u32[]{:S(2)}) %copy-start.6) | copy-done | bytes 688152
  33.4 0.0 copy-start.8
  33.4 1.0 %copy-done.8 = f32[8,88,128]{2,1,0:T(8,128)S(1)} copy-done((f32[8,88,128]{2,1,0:T(8,128)S(1)}, f32[8,88,128]{2,1,0:T(8,128)}, u32[]{:S(2)}) %copy-start.8) | copy-done | bytes 360472
  34.4 28.2 %solve.1 = (f32[4,256,256]{2,1,0:T(8,128)}, f32[4,256,256]{2,1,0:T(8,128)}, f32[2,4,128,256]{3,2,1,0:T(8,128)S(1)}) custom-call(f32[8,168,128]{2,1,0:T(8,128)S(1)} %copy-done.6, f32[8,88,128]{2,1,0:T(8,128)S(1)} %copy-done.8, f32[8,40,128]{2,1,0:T(8,128)S(1)} %collective-permute-done.4.refs_2_, f32[4,3,200,128]{3,2,1,0:T(8,128)S(1)} %get-tuple-element.10.own.refs_3_, ...), custom_call_target="tpu_custom_call" | custom-call | tf_op jit(solution)/shard_map/solve/pallas_call | solution.py:468
  62.6 0.3 collective-permute-start.5
  62.9 2.4 %collective-permute-done.5.received = f32[2,4,128,256]{3,2,1,0:T(8,128)S(1)} collective-permute-done((f32[2,4,128,256]{3,2,1,0:T(8,128)S(1)}, f32[2,4,128,256]{3,2,1,0:T(8,128)S(1)}, u32[]{:S(2)}, u32[]{:S(2)}) %collective-permute-start.5) | collective-permute-done | bytes 1048608 | tf_op jit(solution)/shard_map/ppermute | solution.py:477
  65.3 1.0 %place.1 = (f32[4,256,256]{2,1,0:T(8,128)}, f32[4,256,256]{2,1,0:T(8,128)}) custom-call(f32[2,4,128,256]{3,2,1,0:T(8,128)S(1)} %collective-permute-done.5.received, f32[4,256,256]{2,1,0:T(8,128)} %get-tuple-element.16.t_in, f32[4,256,256]{2,1,0:T(8,128)} %get-tuple-element.17.h_in), custom_call_target="tpu_custom_call", output_to_operand_aliasing={{0}: (1, {}), {1}: (2, {})} | custom-call | tf_op jit(solution)/shard_map/place/pallas_call | solution.py:478
  (1 shorter events, 0.0 us)
Async XLA Ops:
  0.6 8.7 %copy-start.1 = (f32[4,256,256]{2,1,0:T(8,128)S(1)}, f32[4,256,256]{2,1,0:T(8,128)}, u32[]{:S(2)}) copy-start(f32[4,256,256]{2,1,0:T(8,128)} %refs_5_.1) | copy-start | bytes 3145732
  1.4 1.3 %copy-start.4 = (bf16[4,384,384]{2,1,0:T(8,128)(2,1)S(1)}, bf16[4,384,384]{2,1,0:T(8,128)(2,1)}, u32[]{:S(2)}) copy-start(bf16[4,384,384]{2,1,0:T(8,128)(2,1)} %mantissa.1) | copy-start | bytes 3538948
  4.3 5.0 %collective-permute-start = (f32[4,3,200,128]{3,2,1,0:T(8,128)S(1)}, f32[4,3,200,128]{3,2,1,0:T(8,128)S(1)}, u32[]{:S(2)}, u32[]{:S(2)}) collective-permute-start(f32[4,3,200,128]{3,2,1,0:T(8,128)S(1)} %get-tuple-element.11), channel_id=1, source_target_pairs={{0,1},{1,0},{2,3},{3,2},{4,5},{5,4},{6,7},{7,6},{8,9},{9,8},{10,11... | collective-permute-start | bytes 3686408 | tf_op jit(solution)/shard_map/ppermute | solution.py:423
  5.0 4.3 %collective-permute-start.1 = (f32[4,256,256]{2,1,0:T(8,128)}, f32[4,256,256]{2,1,0:T(8,128)S(1)}, u32[]{:S(2)}, u32[]{:S(2)}) collective-permute-start(f32[4,256,256]{2,1,0:T(8,128)} %refs_5_.1), channel_id=1, source_target_pairs={{0,1},{1,0},{2,3},{3,2},{4,5},{5,4},{6,7},{7,6},{8,9},{9,8},{10,11... | collective-permute-start | bytes 3145736 | tf_op jit(solution)/shard_map/ppermute | solution.py:408
  9.3 3.4 %copy-start.2 = (f32[4,256,256]{2,1,0:T(8,128)}, f32[4,256,256]{2,1,0:T(8,128)S(1)}, u32[]{:S(2)}) copy-start(f32[4,256,256]{2,1,0:T(8,128)S(1)} %collective-permute-done.1.t_other.refs_6_) | copy-start | bytes 3145732
  9.3 3.4 %copy-start = (f32[4,3,200,128]{3,2,1,0:T(8,128)}, f32[4,3,200,128]{3,2,1,0:T(8,128)S(1)}, u32[]{:S(2)}) copy-start(f32[4,3,200,128]{3,2,1,0:T(8,128)S(1)} %collective-permute-done.other.refs_4_) | copy-start | bytes 3686404
  9.3 10.5 %copy-start.11 = (s32[8,512]{1,0:T(8,128)S(1)}, s32[8,512]{1,0:T(8,128)}, u32[]{:S(2)}) copy-start(s32[8,512]{1,0:T(8,128)} %param.9) | copy-start | bytes 49156
  9.3 21.8 %copy-start.9 = (s32[8]{0:T(128)S(1)}, s32[8]{0:T(128)}, u32[]{:S(2)}) copy-start(s32[8]{0:T(128)} %refs_8_.1) | copy-start | bytes 100
  9.3 21.8 %copy-start.10 = (f32[4]{0:T(128)S(1)}, f32[4]{0:T(128)}, u32[]{:S(2)}) copy-start(f32[4]{0:T(128)} %refs_9_.1) | copy-start | bytes 52
  12.7 17.6 %collective-permute-start.2 = (f32[8,168,128]{2,1,0:T(8,128)}, f32[8,168,128]{2,1,0:T(8,128)S(1)}, u32[]{:S(2)}, u32[]{:S(2)}) collective-permute-start(f32[8,168,128]{2,1,0:T(8,128)} %get-tuple-element.12), channel_id=1, source_target_pairs={{1,4},{3,6},{4,1},{5,8},{6,3},{7,10},{8,5},{9,12},{10,7},{11,14},{... | collective-permute-start | bytes 2064392 | tf_op jit(solution)/shard_map/ppermute | solution.py:456
  16.1 13.4 %collective-permute-start.3 = (f32[8,88,128]{2,1,0:T(8,128)}, f32[8,88,128]{2,1,0:T(8,128)S(1)}, u32[]{:S(2)}, u32[]{:S(2)}) collective-permute-start(f32[8,88,128]{2,1,0:T(8,128)} %get-tuple-element.13), channel_id=1, source_target_pairs={{0,2},{2,0},{1,3},{3,1},{4,6},{6,4},{5,7},{7,5},{8,10},{10,8},{9,1... | collective-permute-start | bytes 1081352 | tf_op jit(solution)/shard_map/ppermute | solution.py:454
  16.9 11.9 %collective-permute-start.4 = (f32[8,40,128]{2,1,0:T(8,128)}, f32[8,40,128]{2,1,0:T(8,128)S(1)}, u32[]{:S(2)}, u32[]{:S(2)}) collective-permute-start(f32[8,40,128]{2,1,0:T(8,128)} %get-tuple-element.14), channel_id=1, source_target_pairs={{1,6},{3,4},{4,3},{5,10},{6,1},{7,8},{8,7},{9,14},{10,5},{11,12},{... | collective-permute-start | bytes 491528 | tf_op jit(solution)/shard_map/ppermute | solution.py:455
  29.5 0.7 %copy-start.7 = (f32[8,88,128]{2,1,0:T(8,128)}, f32[8,88,128]{2,1,0:T(8,128)S(1)}, u32[]{:S(2)}) copy-start(f32[8,88,128]{2,1,0:T(8,128)S(1)} %collective-permute-done.3.refs_1_) | copy-start | bytes 1081348
  30.3 0.8 %copy-start.5 = (f32[8,168,128]{2,1,0:T(8,128)}, f32[8,168,128]{2,1,0:T(8,128)S(1)}, u32[]{:S(2)}) copy-start(f32[8,168,128]{2,1,0:T(8,128)S(1)} %collective-permute-done.2.refs_0_) | copy-start | bytes 2064388
  31.1 1.2 %copy-start.3 = (f32[4,256,256]{2,1,0:T(8,128)S(1)}, f32[4,256,256]{2,1,0:T(8,128)}, u32[]{:S(2)}) copy-start(f32[4,256,256]{2,1,0:T(8,128)} %copy-done.2) | copy-start | bytes 3145732
  32.3 1.1 %copy-start.6 = (f32[8,168,128]{2,1,0:T(8,128)S(1)}, f32[8,168,128]{2,1,0:T(8,128)}, u32[]{:S(2)}) copy-start(f32[8,168,128]{2,1,0:T(8,128)} %copy-done.5) | copy-start | bytes 2064388
  33.4 1.0 %copy-start.8 = (f32[8,88,128]{2,1,0:T(8,128)S(1)}, f32[8,88,128]{2,1,0:T(8,128)}, u32[]{:S(2)}) copy-start(f32[8,88,128]{2,1,0:T(8,128)} %copy-done.7) | copy-start | bytes 1081348
  62.6 2.7 %collective-permute-start.5 = (f32[2,4,128,256]{3,2,1,0:T(8,128)S(1)}, f32[2,4,128,256]{3,2,1,0:T(8,128)S(1)}, u32[]{:S(2)}, u32[]{:S(2)}) collective-permute-start(f32[2,4,128,256]{3,2,1,0:T(8,128)S(1)} %get-tuple-element.15), channel_id=1, source_target_pairs={{0,1},{1,0},{2,3},{3,2},{4,5},{5,4},{6,7},{7,6},{8,9},{9,8},{10,11... | collective-permute-start | bytes 3145736 | tf_op jit(solution)/shard_map/ppermute | solution.py:477

commit v2 on v1

v2 whole, which is shorter than its diff:
```python
import functools

import jax
import jax.numpy as jnp
from jax import lax
from jax.experimental import pallas as pl
from jax.experimental.pallas import tpu as pltpu
from jax.sharding import PartitionSpec as P

RIM = 64
TILE = 64
STEPS = 2
SWEEPS = 3
COOLANT = 2.0

LANES = 128
WIDE = 6
LOCAL = 200
REGION = 144
EDGE = 72
ROWS_P = 2 * EDGE + 8 + 16
ROWS_G = EDGE + 16
ROWS_D = 40
F32 = jnp.float32
VMEM = pl.BlockSpec(memory_space=pltpu.VMEM)
SMEM = pl.BlockSpec(memory_space=pltpu.SMEM)
ANY = pl.BlockSpec(memory_space=pl.ANY)
PARAMS = pltpu.CompilerParams(vmem_limit_bytes=48 << 20)


def rows8(start):
    return pl.ds(pl.multiple_of(start, 8), 8)


def lane_ids():
    return lax.broadcasted_iota(jnp.int32, (8, LANES), 1)


def turn(value, shift):
    shift = shift % LANES
    return pltpu.roll(value, shift, 1) if shift else value


def decode_kernel(mantissa, exponent, own, sent, plain, own_sem, sent_sem):
    core = lax.axis_index("ta")
    depth, rows, _ = mantissa.shape
    tiles = rows // TILE
    wide_lane = lax.broadcasted_iota(jnp.int32, (16, LANES), 1)
    first = pl.multiple_of(core * 184, 8)
    other = pl.multiple_of(184 - core * 184, 8)

    def copies(layer):
        return (
            pltpu.make_async_copy(plain.at[layer, :, pl.ds(other, LOCAL), :], sent.at[layer], sent_sem.at[layer]),
            pltpu.make_async_copy(plain.at[layer, :, pl.ds(first, LOCAL), :], own.at[layer], own_sem.at[layer]),
        )

    for layer in range(depth):

        @pl.loop(0, tiles)
        def _(tile_row):
            for col in range(3):
                low = exponent[layer, tile_row, 2 * col]
                high = exponent[layer, tile_row, 2 * col + 1]
                scale = jnp.exp2(jnp.where(wide_lane < TILE, low, high).astype(F32))
                for part in range(TILE // 16):
                    where = pl.ds(pl.multiple_of(tile_row * TILE + part * 16, 16), 16)
                    cells = mantissa[layer, where, col * LANES : (col + 1) * LANES]
                    plain[layer, col, where, :] = cells.astype(F32) * scale

        for copy in copies(layer):
            copy.start()
    for layer in range(depth):
        for copy in copies(layer):
            copy.wait()


def pack_kernel(sides, own, other, t_own, t_other, *outs):
    core = lax.axis_index("ta")
    lane = lane_ids()
    low = lane < 64
    to_p, to_g, to_d = outs[0], outs[1 : 1 + len(sides)], outs[1 + len(sides) :]
    edge = core * 128
    region = 56 - core * 56
    t_row = core * 120
    t_edge = core * 248

    def place(total, value, source, target, width):
        moved = turn(value, target - source)
        return jnp.where((lane >= target) & (lane < target + width), moved, total)

    def one(src, t_src, index, layer):
        def cells(col, row):
            return src[index, col, rows8(row), :]

        def t_cells(col, row):
            return t_src[index, rows8(row), col * LANES : (col + 1) * LANES]

        extra = jnp.zeros((8, LANES), F32)
        for j in range(9):
            left, middle, right = (cells(col, edge + 8 * j) for col in range(3))
            one, two, three = turn(left, 64), turn(middle, 64), turn(right, 64)
            to_p[layer, 8 * j : 8 * j + 8, :] = jnp.where(low, one, two)
            to_p[layer, EDGE + 8 * j : EDGE + 8 * j + 8, :] = jnp.where(low, two, three)
            extra = place(extra, jnp.where(low, left, right), 64 - WIDE, 2 * WIDE * j, 2 * WIDE)
        to_p[layer, 2 * EDGE : 2 * EDGE + 8, :] = extra
        for col in range(2):
            start = 2 * EDGE + 8 + 8 * col
            to_p[layer, start : start + 8, :] = t_cells(col, t_edge)

        def side_parts(right, g_ref, d_ref):
            col, t_col = (2, 1) if right else (0, 0)
            at, t_at = (LANES - WIDE, LANES - WIDE) if right else (64, 0)

            def strip(row):
                value = cells(col, row)
                return turn(value, 64) if right else value

            extra = jnp.zeros((8, LANES), F32)
            for j in range(9):
                one_strip, two_strip = strip(region + 8 * j), strip(region + EDGE + 8 * j)
                g_ref[layer, 8 * j : 8 * j + 8, :] = jnp.where(low, one_strip, turn(two_strip, 64))
                extra = place(extra, one_strip, at, WIDE * j, WIDE)
                extra = place(extra, two_strip, at, WIDE * (j + 9), WIDE)
            g_ref[layer, EDGE : EDGE + 8, :] = extra
            extra = jnp.zeros((8, LANES), F32)
            for j in range(17):
                extra = place(extra, t_cells(t_col, t_row + 8 * j), t_at, WIDE * j, WIDE)
            g_ref[layer, EDGE + 8 : EDGE + 16, :] = extra
            strips = [strip(edge + 8 * j) for j in range(9)]
            for j in range(4):
                d_ref[layer, 8 * j : 8 * j + 8, :] = jnp.where(low, strips[j], turn(strips[j + 5], 64))
            extra = strips[4]
            for j in range(9):
                extra = place(extra, strips[j], at, 64 + WIDE * j, WIDE)
            extra = place(extra, t_cells(t_col, t_edge), t_at, 64 + 9 * WIDE, WIDE)
            d_ref[layer, 32:40, :] = extra

        for side, g_ref, d_ref in zip(sides, to_g, to_d):
            if side is None:
                first = lax.axis_index("gy") == 0
                pl.when(first)(functools.partial(side_parts, True, g_ref, d_ref))
                pl.when(jnp.logical_not(first))(functools.partial(side_parts, False, g_ref, d_ref))
            else:
                side_parts(side, g_ref, d_ref)

    depth = own.shape[0]

    @pl.loop(0, depth)
    def _(index):
        one(own, t_own, index, core * depth + index)
        one(other, t_other, index, (1 - core) * depth + index)


def stack_kernel(own, other, t_own, t_other, heat, now, cells, t_cells, sems, t_sems):
    core = lax.axis_index("ta")
    low = lane_ids() < 64
    zero = jnp.zeros((8, LANES), F32)
    depth, rows, _ = t_own.shape
    layers = 2 * depth
    height = own.shape[0] // depth
    t_height = REGION - 8
    copies = []
    for which, (src, t_src) in enumerate(((own, t_own), (other, t_other))):
        base = core * depth if which == 0 else (1 - core) * depth
        start = pl.multiple_of(base * height, 8)
        copies.append(pltpu.make_async_copy(src, cells.at[pl.ds(start, depth * height), :], sems.at[which]))
        for layer in range(depth):
            for col in range(2):
                row = pl.multiple_of(core * 120, 8)
                start = pl.multiple_of((base + layer) * t_height, 8)
                copies.append(
                    pltpu.make_async_copy(
                        t_src.at[layer, pl.ds(row, t_height), col * LANES : (col + 1) * LANES],
                        t_cells.at[col, pl.ds(start, t_height), :],
                        t_sems.at[which, layer, col],
                    )
                )
    for copy in copies:
        copy.start()
    for copy in copies:
        copy.wait()
    region = 56 - core * 56
    t_first = 8 - core * 8
    t_halo = core * t_height

    @pl.loop(0, REGION // 4)
    def _(block):
        for step in range(4):
            row = block * 4 + step
            parts = [turn(cells[pl.ds(region + row + col * LOCAL, layers, stride=height), :], 64) for col in range(3)]
            for col in range(3):
                heat[rows8(row * 24 + 8 * col), :] = jnp.where(low, parts[col], parts[(col + 1) % 3])

    @pl.loop(0, t_height // 4)
    def _(block):
        for step in range(4):
            row = block * 4 + step
            for col in range(2):
                part = t_cells[col, pl.ds(row, layers, stride=t_height), :]
                now[rows8((t_first + row) * 24 + 8 * col), :] = part
            now[rows8((t_first + row) * 24 + 16), :] = zero

    @pl.loop(0, 8)
    def _(row):
        for col in range(3):
            now[rows8((t_halo + row) * 24 + 8 * col), :] = zero


def solve_kernel(sides, bounds, *refs):
    count = len(sides)
    from_p, refs = refs[0], refs[1:]
    from_g, from_d, refs = refs[:count], refs[count : 2 * count], refs[2 * count :]
    heat_in, now_in, flow, material, conductivity = refs[:5]
    t_out, h_out, sent = refs[5:8]
    heat, now, later, cond, f_down, f_right, f_above, inverse, base, t_stage, h_stage, sems = refs[8:]
    core = lax.axis_index("ta")
    gx, gy = lax.axis_index("gx"), lax.axis_index("gy")
    lane = lane_ids()
    level = lax.broadcasted_iota(jnp.int32, (8, LANES), 0)
    low = lane < 64
    layers = 8
    depth = layers // 2
    edge = core * EDGE
    t_first = 8 - core * 8
    t_halo = core * (REGION - 8)

    def at(row, col):
        return rows8(row * 24 + 8 * col)

    def across(ref, row, height):
        return ref[pl.ds(row, layers, stride=height), :]

    def add(ref, row, col, value):
        ref[at(row, col), :] = ref[at(row, col), :] + value

    @pl.loop(0, REGION // 4)
    def _(block):
        for step in range(4):
            for col in range(3):
                where = at(block * 4 + step, col)
                heat[where, :] = heat_in[where, :]
                now[where, :] = now_in[where, :]

    def add_side(right, g_ref, d_ref):
        col = 1 if right else 0
        target = 0 if right else LANES - WIDE
        halo = (lane < WIDE) if right else (lane >= LANES - WIDE)
        main = (lane >= 64) if right else low

        @pl.loop(0, 8)
        def _(i):
            extra = across(g_ref, EDGE + i, ROWS_G)
            t_extra = across(g_ref, EDGE + 8 + i, ROWS_G)
            for j in range(9):
                value = across(g_ref, 8 * j + i, ROWS_G)
                turned = turn(value, 64)
                one, two = (turned, value) if right else (value, turned)
                add(heat, 8 * j + i, col, jnp.where(main, one, 0.0))
                add(heat, EDGE + 8 * j + i, col, jnp.where(main, two, 0.0))
            for j in range(18):
                add(heat, 8 * j + i, 2, jnp.where(halo, turn(extra, target - WIDE * j), 0.0))
            for j in range(17):
                add(now, t_first + 8 * j + i, 2, jnp.where(halo, turn(t_extra, target - WIDE * j), 0.0))
            extra = across(d_ref, 32 + i, ROWS_D)
            for j in range(9):
                value = across(d_ref, 8 * (j % 5) + i, ROWS_D)
                if (j < 5) == right:
                    value = turn(value, 64)
                add(heat, edge + 8 * j + i, col, jnp.where(main, value, 0.0))
                add(heat, edge + 8 * j + i, 2, jnp.where(halo, turn(extra, target - 64 - WIDE * j), 0.0))
            add(now, t_halo + i, 2, jnp.where(halo, turn(extra, target - 64 - 9 * WIDE), 0.0))

    halos = (lane < WIDE) | (lane >= LANES - WIDE)

    @pl.loop(0, 8)
    def _(i):
        extra = across(from_p, 2 * EDGE + i, ROWS_P)
        for j in range(9):
            row = edge + 8 * j + i
            for col in range(2):
                add(heat, row, col, across(from_p, col * EDGE + 8 * j + i, ROWS_P))
            add(heat, row, 2, jnp.where(halos, turn(extra, LANES - WIDE - 2 * WIDE * j), 0.0))
        for col in range(2):
            now[at(t_halo + i, col), :] = across(from_p, 2 * EDGE + 8 + 8 * col + i, ROWS_P)

    for side, g_ref, d_ref in zip(sides, from_g, from_d):
        if side is None:
            pl.when(gy == 0)(functools.partial(add_side, True, g_ref, d_ref))
            pl.when(gy > 0)(functools.partial(add_side, False, g_ref, d_ref))
        else:
            add_side(side, g_ref, d_ref)

    def to_stage(stage, src):
        @pl.loop(0, 16)
        def _(tile):
            for layer in range(layers):
                for col in range(2):
                    start = (8 + 8 * tile) * 24 + 8 * col + layer
                    value = src[pl.ds(start, 8, stride=24), :]
                    stage[layer, rows8(8 * tile), col * LANES : (col + 1) * LANES] = value

    def outputs(stage, which, out):
        mine = stage.at[pl.ds(core * depth, depth)]
        theirs = stage.at[pl.ds((1 - core) * depth, depth)]
        half = stage.shape[1]
        place = pl.ds(pl.multiple_of(core * half, half), half)
        return (
            pltpu.make_async_copy(theirs, sent.at[which], sems.at[which, 0]),
            pltpu.make_async_copy(mine, out.at[:, place, :], sems.at[which, 1]),
        )

    to_stage(h_stage, heat)
    for copy in outputs(h_stage, 1, h_out):
        copy.start()

    def to_right(values):
        moved = [turn(value, -1) for value in values]
        last = lane == LANES - 1
        return [jnp.where(last, moved[(col + 1) % 3], moved[col]) for col in range(3)]

    def to_left(values):
        moved = [turn(value, 1) for value in values]
        first = lane == 0
        return [jnp.where(first, moved[(col + 2) % 3], moved[col]) for col in range(3)]

    def upper(value):
        return pltpu.roll(value, 7, 0)

    def lower(value):
        return pltpu.roll(value, 1, 0)

    has_right = (gy + 1) * 256 < bounds[1]
    right_lanes = (lane < WIDE) & has_right
    left_lanes = (lane >= LANES - WIDE) & (gy > 0)
    one = jnp.full((8, LANES), 1.0, F32)
    col_masks = [one, one, jnp.where(right_lanes | left_lanes, 1.0, 0.0)]
    scale = jnp.full((8, LANES), conductivity[material[0]], F32)
    for layer in range(1, layers):
        scale = jnp.where(level == layer, conductivity[material[layer]], scale)
    scales = [scale * mask for mask in col_masks]
    not_top = jnp.where(level < layers - 1, 1.0, 0.0)
    not_bottom = jnp.where(level > 0, 1.0, 0.0)
    flows = [flow[:, col * LANES : (col + 1) * LANES] for col in range(3)]
    first_row = gx * 256 + core * 128 - 8

    def row_mask(row):
        place = first_row + row
        return jnp.where((place >= 0) & (place < bounds[0]), 1.0, 0.0)

    for ref in (now, later, cond, f_down):
        for row in (0, 1, REGION - 2, REGION - 1):
            for col in range(3):
                if ref is not now:
                    ref[at(row, col), :] = jnp.zeros((8, LANES), F32)

    def conductances(src, start, stop):
        @pl.loop(0, (stop - start) // 4)
        def _(block):
            for step in range(4):
                row = start + block * 4 + step
                mask = row_mask(row)
                for col in range(3):
                    where = at(row, col)
                    cond[where, :] = (scales[col] * mask) * (1.0 + 0.5 * jnp.tanh(src[where, :]))

    def coefficients(src, start, stop):
        @pl.loop(0, (stop - start) // 2)
        def _(block):
            first = start + block * 2
            lines = [[cond[at(first + step, col), :] for col in range(3)] for step in range(-1, 3)]
            for step in range(2):
                row = first + step
                up, here, down = lines[step], lines[step + 1], lines[step + 2]
                mask = row_mask(row)
                rights, lefts = to_right(here), to_left(here)
                for col in range(3):
                    where = at(row, col)
                    centre = here[col]
                    over = centre + upper(centre) * not_top
                    under = centre + lower(centre) * not_bottom
                    face_down = 0.5 * (centre + down[col])
                    face_right = 0.5 * (centre + rights[col])
                    total = (1.0 + flows[col]) + 0.5 * (centre + up[col]) + face_down
                    total = total + face_right + 0.5 * (centre + lefts[col]) + over + under
                    f_down[where, :] = face_down
                    f_right[where, :] = face_right
                    f_above[where, :] = over * not_top
                    inverse[where, :] = (mask * col_masks[col]) / total
                    base[where, :] = src[where, :] + heat[where, :]
            del lines

        for col in range(3):
            centre, down = cond[at(start - 1, col), :], cond[at(start, col), :]
            f_down[at(start - 1, col), :] = 0.5 * (centre + down)

    def sweep(src, dst, start, stop):
        @pl.loop(0, (stop - start) // 4)
        def _(block):
            first = start + block * 4
            lines = [[src[at(first + step, col), :] for col in range(3)] for step in range(-1, 5)]
            faces = [[f_down[at(first + step, col), :] for col in range(3)] for step in range(-1, 4)]
            for step in range(4):
                up, here, down = lines[step], lines[step + 1], lines[step + 2]
                sides_right = [f_right[at(first + step, col), :] for col in range(3)]
                rights = to_right(here)
                lefts = to_left([face * value for face, value in zip(sides_right, here)])
                for col in range(3):
                    where = at(first + step, col)
                    face_above = f_above[where, :]
                    total = base[where, :] + (faces[step][col] + flows[col]) * up[col]
                    total = total + faces[step + 1][col] * down[col]
                    total = total + (sides_right[col] * rights[col] + lefts[col])
                    total = total + (face_above * upper(here[col]) + lower(face_above * here[col]))
                    dst[where, :] = total * inverse[where, :]

    conductances(now, 2, 142)
    coefficients(now, 2, 142)
    sweep(now, later, 2, 142)
    sweep(later, now, 2, 142)
    sweep(now, later, 4, 140)
    conductances(later, 4, 140)
    coefficients(later, 6, 138)
    sweep(later, now, 6, 138)
    sweep(now, later, 6, 138)
    sweep(later, now, 8, 136)

    to_stage(t_stage, now)
    for copy in outputs(t_stage, 0, t_out):
        copy.start()
    for copy in outputs(h_stage, 1, h_out) + outputs(t_stage, 0, t_out):
        copy.wait()


def place_kernel(received, t_in, h_in, t_out, h_out, sems):
    core = lax.axis_index("ta")
    half = received.shape[2]
    place = pl.ds(pl.multiple_of((1 - core) * half, half), half)
    copies = [
        pltpu.make_async_copy(received.at[which], out.at[:, place, :], sems.at[which])
        for which, out in enumerate((t_out, h_out))
    ]
    for copy in copies:
        copy.start()
    for copy in copies:
        copy.wait()


def on_device(t_initial, power_mantissa, tile_exponent, channel_mask, material, conductivity):
    depth, rows, cols = t_initial.shape
    layers = 2 * depth
    n_gx, n_gy = lax.axis_size("gx"), lax.axis_size("gy")
    array = jax.ShapeDtypeStruct
    swap = [(0, 1), (1, 0)]

    t_other = lax.ppermute(t_initial, "ta", swap)
    local = array((depth, 3, LOCAL, LANES), F32)
    own, sent = pl.pallas_call(
        decode_kernel,
        out_shape=(local, local),
        in_specs=[VMEM, SMEM],
        out_specs=(ANY, ANY),
        scratch_shapes=[
            pltpu.VMEM((depth, 3, rows + 2 * RIM, LANES), F32),
            pltpu.SemaphoreType.DMA((depth,)),
            pltpu.SemaphoreType.DMA((depth,)),
        ],
        compiler_params=PARAMS,
        name="decode",
    )(power_mantissa, tile_exponent)
    other = lax.ppermute(sent, "ta", swap)

    out_sides = [None] if n_gy == 2 else [True, False]
    count = len(out_sides)
    packed = pl.pallas_call(
        functools.partial(pack_kernel, out_sides),
        out_shape=(array((layers, ROWS_P, LANES), F32),)
        + (array((layers, ROWS_G, LANES), F32),) * count
        + (array((layers, ROWS_D, LANES), F32),) * count,
        in_specs=[VMEM] * 4,
        out_specs=(VMEM,) * (1 + 2 * count),
        compiler_params=PARAMS,
        name="pack",
    )(own, other, t_initial, t_other)

    def moves(shift):
        pairs = []
        for z in range(n_gx):
            for x in range(n_gy):
                for c in range(2):
                    to_z = z + 2 * c - 1
                    to_x = x ^ 1 if shift is None else x + shift
                    if 0 <= to_z < n_gx and 0 <= to_x < n_gy:
                        pairs.append(((z * n_gy + x) * 2 + c, (to_z * n_gy + to_x) * 2 + 1 - c))
        return pairs

    along = ("gx", "gy", "ta")
    shifts = [None] if n_gy == 2 else [1, -1]
    from_g = []
    for shift, value in zip(shifts, packed[1 : 1 + count]):
        pairs = swap if shift is None else [(x, x + shift) for x in range(n_gy) if 0 <= x + shift < n_gy]
        from_g.append(lax.ppermute(value, "gy", pairs))
    from_d = [lax.ppermute(value, along, moves(shift)) for shift, value in zip(shifts, packed[1 + count :])]
    from_p = lax.ppermute(packed[0], along, moves(0))
    in_sides = [None] if n_gy == 2 else [False, True]

    wide = jnp.pad(channel_mask, ((0, 0), (RIM, RIM)))
    mask = lax.dynamic_slice_in_dim(wide, lax.axis_index("gy") * cols, cols + 2 * RIM, 1)
    flow = COOLANT * jnp.concatenate([mask[:, RIM:], mask[:, :RIM]], axis=1).astype(F32)

    stacked = array((REGION * 24, LANES), F32)
    heat, now = pl.pallas_call(
        stack_kernel,
        out_shape=(stacked, stacked),
        in_specs=[ANY] * 4,
        out_specs=(VMEM, VMEM),
        scratch_shapes=[
            pltpu.VMEM((layers * 3 * LOCAL, LANES), F32),
            pltpu.VMEM((2, layers * (REGION - 8), LANES), F32),
            pltpu.SemaphoreType.DMA((2,)),
            pltpu.SemaphoreType.DMA((2, depth, 2)),
        ],
        compiler_params=PARAMS,
        name="stack",
    )(own.reshape(-1, LANES), other.reshape(-1, LANES), t_initial, t_other)

    whole = array((depth, rows, cols), F32)
    half = array((2, depth, rows // 2, cols), F32)
    inner = pltpu.VMEM((REGION * 24, LANES), F32)
    stage = pltpu.VMEM((layers, rows // 2, cols), F32)

    def flat(value):
        return value.reshape(-1, LANES)

    t_part, h_part, sent = pl.pallas_call(
        functools.partial(solve_kernel, in_sides, (n_gx * rows, n_gy * cols)),
        out_shape=(whole, whole, half),
        in_specs=[VMEM] * (1 + 2 * count + 3) + [SMEM, SMEM],
        out_specs=(ANY, ANY, ANY),
        scratch_shapes=[inner] * 9 + [stage, stage, pltpu.SemaphoreType.DMA((2, 2))],
        compiler_params=PARAMS,
        name="solve",
    )(flat(from_p), *map(flat, from_g), *map(flat, from_d), heat, now, flow, material, conductivity)
    received = lax.ppermute(sent, "ta", swap)
    return pl.pallas_call(
        place_kernel,
        out_shape=(whole, whole),
        in_specs=[ANY, ANY, ANY],
        out_specs=(ANY, ANY),
        scratch_shapes=[pltpu.SemaphoreType.DMA((2,))],
        input_output_aliases={1: 0, 2: 1},
        compiler_params=PARAMS,
        name="place",
    )(received, t_part, h_part)


def solution(mesh):
    cells = P("ta", ("group", "gx"), "gy")
    return jax.shard_map(
        on_device,
        mesh=mesh,
        in_specs=(cells, cells, cells, P(), P(), P()),
        out_specs=(cells, cells),
        check_vma=False,
    )
```

time: 66.6 us -> 76.3 us (1.15)
  Pallas kernels: 34 us -> 50.9 us
  waiting for transfers between devices: 16.3 us -> 9.11 us
    pallas_call x1, Pallas kernels: 28.2 us -> 38.9 us  [on_device(): pl.pallas_call(functools.partial(solve_kernel, in_sides, (n_gx * rows, n_...]
    ppermute x1, waiting for transfers between devices: 8.96 us -> 1.66 us  [on_device(): lax.ppermute(value, along, moves(shift))]
    pallas_call x0 -> x1, Pallas kernels: none -> 5.99 us  [on_device(): pl.pallas_call(stack_kernel, out_shape=(stacked, stacked), in_specs=[ANY]...]
    unnamed x25 -> x21, local copies, waits for them, and re-layouts: 6.98 us -> 6.91 us
  transfers between devices with their start and end apart: 6 -> 6, of which waited for: 4 -> 4; matrix products, arithmetic and copies ran while one was open for 0% -> 0% of each run, Pallas kernels for 0% -> 8%
where the time goes in v2:
time: 76.3 us; the launch traced here: 76 us
  Pallas kernels  50.9 us (67%)
  waiting for transfers between devices  9.11 us (12%)
  starting transfers between devices  8.16 us (11%)
  local copies, waits for them, and re-layouts  7 us (9%)
    pallas_call x1, Pallas kernels, on_device(): pl.pallas_call(functools.partial(solve_kernel, in_sides, (n_gx * rows, n_...  38.9 us
    unnamed x21, local copies, waits for them, and re-layouts  6.91 us
    pallas_call x1, Pallas kernels, on_device(): pl.pallas_call(stack_kernel, out_shape=(stacked, stacked), in_specs=[ANY]...  5.99 us
    ppermute x1, waiting for transfers between devices, on_device(): t_other = lax.ppermute(t_initial, 'ta', swap)  4.18 us
    pallas_call x1, Pallas kernels, on_device(): pl.pallas_call(functools.partial(pack_kernel, out_sides), out_shape=(arra...  3.47 us
    ppermute x1, starting transfers between devices, on_device(): from_p = lax.ppermute(packed[0], along, moves(0))  3.46 us
    ppermute x1, starting transfers between devices, on_device(): lax.ppermute(value, along, moves(shift))  2.88 us
    ppermute x1, waiting for transfers between devices, on_device(): received = lax.ppermute(sent, 'ta', swap)  2.46 us
  transfers between devices with their start and end apart: 6, of which 4 were waited for; matrix products, arithmetic and copies ran while one was open for 0% of the time, Pallas kernels for 8%

profile of v2, /device:TPU:21, one launch (start us, length us, event | category | flops | bytes accessed | tf_op | source)
XLA Modules:
  0.0 76.0 jit_solution(14394563847521164009)
XLA Ops:
  0.6 0.0 copy-start
  0.6 0.8 %copy.10.exponent = s32[4,6,6]{2,1,0:T(8,128)S(1)} copy(s32[4,6,6]{2,0,1:T(4,128)} %param.8) | data formatting | bytes 1152 | tf_op args[2]
  1.4 0.0 copy-start.5
  1.4 1.3 %copy-done.5 = bf16[4,384,384]{2,1,0:T(8,128)(2,1)S(1)} copy-done((bf16[4,384,384]{2,1,0:T(8,128)(2,1)S(1)}, bf16[4,384,384]{2,1,0:T(8,128)(2,1)}, u32[]{:S(2)}) %copy-start.5) | copy-done | bytes 1179672
  2.7 1.6 %decode.1 = (f32[4,3,200,128]{3,2,1,0:T(8,128)S(1)}, f32[4,3,200,128]{3,2,1,0:T(8,128)S(1)}) custom-call(bf16[4,384,384]{2,1,0:T(8,128)(2,1)S(1)} %copy-done.5, s32[4,6,6]{2,1,0:T(8,128)S(1)} %copy.10.exponent), custom_call_target="tpu_custom_call" | custom-call | tf_op jit(solution)/shard_map/decode/pallas_call | solution.py:458
  4.3 0.7 collective-permute-start
  5.0 0.1 collective-permute-start.1
  5.1 4.2 %collective-permute-done.1.t_other = f32[4,256,256]{2,1,0:T(8,128)S(1)} collective-permute-done((f32[4,256,256]{2,1,0:T(8,128)}, f32[4,256,256]{2,1,0:T(8,128)S(1)}, u32[]{:S(2)}, u32[]{:S(2)}) %collective-permute-start.1) | collective-permute-done | bytes 1048608 | tf_op jit(solution)/shard_map/ppermute | solution.py:456
  9.3 0.0 copy-start.1
  9.3 0.0 collective-permute-done.other
  9.3 0.0 copy-done
  9.3 0.0 copy-start.9
  9.3 3.5 %pack.1 = (f32[8,168,128]{2,1,0:T(8,128)}, f32[8,88,128]{2,1,0:T(8,128)}, f32[8,40,128]{2,1,0:T(8,128)S(1)}) custom-call(f32[4,3,200,128]{3,2,1,0:T(8,128)S(1)} %get-tuple-element.12.own, f32[4,3,200,128]{3,2,1,0:T(8,128)S(1)} %collective-permute-done.other, f32[4,256,256]{2,1,0:T(8,128)S(1)} %copy-done, f32[4,256,256]{2,1,0:T(8,128)S(1)} %collective-permute-done.1.t_other), custom_call_target="tpu_custom_call" | custom-call | tf_op jit(solution)/shard_map/pack/pallas_call | solution.py:475
  12.8 0.0 copy-done.1
  12.8 0.0 copy-start.8
  12.8 0.7 copy-done.8
  13.4 3.5 %collective-permute-start.2 = (f32[8,168,128]{2,1,0:T(8,128)}, f32[8,168,128]{2,1,0:T(8,128)}, u32[]{:S(2)}, u32[]{:S(2)}) collective-permute-start(f32[8,168,128]{2,1,0:T(8,128)} %get-tuple-element.14), channel_id=1, source_target_pairs={{1,4},{3,6},{4,1},{5,8},{6,3},{7,10},{8,5},{9,12},{10,7},{11,14},{... | collective-permute-start | bytes 2064392 | tf_op jit(solution)/shard_map/ppermute | solution.py:504
  16.9 0.7 collective-permute-start.3
  17.6 0.0 copy-done.9
  17.7 2.9 %collective-permute-start.4 = (f32[8,40,128]{2,1,0:T(8,128)}, f32[8,40,128]{2,1,0:T(8,128)S(1)}, u32[]{:S(2)}, u32[]{:S(2)}) collective-permute-start(f32[8,40,128]{2,1,0:T(8,128)} %copy-done.8), channel_id=1, source_target_pairs={{1,6},{3,4},{4,3},{5,10},{6,1},{7,8},{8,7},{9,14},{10,5},{11,12},{... | collective-permute-start | bytes 491528 | tf_op jit(solution)/shard_map/ppermute | solution.py:503
  20.5 0.1 pad_dynamic-slice_fusion.1
  20.6 0.1 fusion.refs_5_
  20.7 0.0 copy-start.2
  20.7 1.2 %copy-done.2 = f32[4,256,256]{2,1,0:T(8,128)S(1)} copy-done((f32[4,256,256]{2,1,0:T(8,128)S(1)}, f32[4,256,256]{2,1,0:T(8,128)}, u32[]{:S(2)}) %copy-start.2) | copy-done | bytes 1048600
  21.9 0.0 copy-start.6
  21.9 0.0 copy-start.7
  21.9 6.0 %stack.1 = (f32[3456,128]{1,0:T(8,128)}, f32[3456,128]{1,0:T(8,128)}) custom-call(f32[2400,128]{1,0:T(8,128)S(1)} %bitcast.5, f32[2400,128]{1,0:T(8,128)S(1)} %bitcast.6, f32[4,256,256]{2,1,0:T(8,128)S(1)} %copy-done, f32[4,256,256]{2,1,0:T(8,128)S(1)} %copy-done.2), custom_call_target="tpu_custom_call" | custom-call | tf_op jit(solution)/shard_map/stack/pallas_call | solution.py:512
  27.9 1.7 %collective-permute-done.4 = f32[8,40,128]{2,1,0:T(8,128)S(1)} collective-permute-done((f32[8,40,128]{2,1,0:T(8,128)}, f32[8,40,128]{2,1,0:T(8,128)S(1)}, u32[]{:S(2)}, u32[]{:S(2)}) %collective-permute-start.4) | collective-permute-done | bytes 163872 | tf_op jit(solution)/shard_map/ppermute | solution.py:503
  29.6 0.8 %collective-permute-done.3 = f32[8,88,128]{2,1,0:T(8,128)} collective-permute-done((f32[8,88,128]{2,1,0:T(8,128)}, f32[8,88,128]{2,1,0:T(8,128)}, u32[]{:S(2)}, u32[]{:S(2)}) %collective-permute-start.3) | collective-permute-done | bytes 360480 | tf_op jit(solution)/shard_map/ppermute | solution.py:502
  30.4 0.0 collective-permute-done.2
  30.4 0.0 copy-done.6
  30.4 0.0 copy-done.7
  30.4 0.0 copy-start.3
  30.4 1.5 %copy-done.3 = f32[3456,128]{1,0:T(8,128)S(1)} copy-done((f32[3456,128]{1,0:T(8,128)S(1)}, f32[3456,128]{1,0:T(8,128)}, u32[]{:S(2)}) %copy-start.3) | copy-done | bytes 1769496
  31.9 0.0 copy-start.4
  31.9 1.5 %copy-done.4 = f32[3456,128]{1,0:T(8,128)S(1)} copy-done((f32[3456,128]{1,0:T(8,128)S(1)}, f32[3456,128]{1,0:T(8,128)}, u32[]{:S(2)}) %copy-start.4) | copy-done | bytes 1769496
  33.4 38.9 %solve.1 = (f32[4,256,256]{2,1,0:T(8,128)}, f32[4,256,256]{2,1,0:T(8,128)}, f32[2,4,128,256]{3,2,1,0:T(8,128)S(1)}) custom-call(f32[1344,128]{1,0:T(8,128)} %bitcast.refs_0_, f32[704,128]{1,0:T(8,128)} %bitcast.1.refs_1_, f32[320,128]{1,0:T(8,128)S(1)} %bitcast.7, f32[3456,128]{1,0:T(8,128)S(1)} %copy-done.3, f32[3456,128]{1,0:T(8,128)S(1)} %copy-done.4, ...), custom_call_target="tpu_custom_call" | custom-call | tf_op jit(solution)/shard_map/solve/pallas_call | solution.py:535
  72.3 0.3 collective-permute-start.5
  72.6 2.5 %collective-permute-done.5.received = f32[2,4,128,256]{3,2,1,0:T(8,128)S(1)} collective-permute-done((f32[2,4,128,256]{3,2,1,0:T(8,128)S(1)}, f32[2,4,128,256]{3,2,1,0:T(8,128)S(1)}, u32[]{:S(2)}, u32[]{:S(2)}) %collective-permute-start.5) | collective-permute-done | bytes 1048608 | tf_op jit(solution)/shard_map/ppermute | solution.py:544
  75.0 1.0 %place.1 = (f32[4,256,256]{2,1,0:T(8,128)}, f32[4,256,256]{2,1,0:T(8,128)}) custom-call(f32[2,4,128,256]{3,2,1,0:T(8,128)S(1)} %collective-permute-done.5.received, f32[4,256,256]{2,1,0:T(8,128)} %get-tuple-element.20.t_in, f32[4,256,256]{2,1,0:T(8,128)} %get-tuple-element.21.h_in), custom_call_target="tpu_custom_call", output_to_operand_aliasing={{0}: (1, {}), {1}: (2, {})} | custom-call | tf_op jit(solution)/shard_map/place/pallas_call | solution.py:545
  (1 shorter events, 0.0 us)
Async XLA Ops:
  0.6 8.7 %copy-start = (f32[4,256,256]{2,1,0:T(8,128)S(1)}, f32[4,256,256]{2,1,0:T(8,128)}, u32[]{:S(2)}) copy-start(f32[4,256,256]{2,1,0:T(8,128)} %t_own.3) | copy-start | bytes 3145732
  1.4 1.3 %copy-start.5 = (bf16[4,384,384]{2,1,0:T(8,128)(2,1)S(1)}, bf16[4,384,384]{2,1,0:T(8,128)(2,1)}, u32[]{:S(2)}) copy-start(bf16[4,384,384]{2,1,0:T(8,128)(2,1)} %mantissa.1) | copy-start | bytes 3538948
  4.3 5.0 %collective-permute-start = (f32[4,3,200,128]{3,2,1,0:T(8,128)S(1)}, f32[4,3,200,128]{3,2,1,0:T(8,128)S(1)}, u32[]{:S(2)}, u32[]{:S(2)}) collective-permute-start(f32[4,3,200,128]{3,2,1,0:T(8,128)S(1)} %get-tuple-element.13), channel_id=1, source_target_pairs={{0,1},{1,0},{2,3},{3,2},{4,5},{5,4},{6,7},{7,6},{8,9},{9,8},{10,11... | collective-permute-start | bytes 3686408 | tf_op jit(solution)/shard_map/ppermute | solution.py:471
  5.0 4.3 %collective-permute-start.1 = (f32[4,256,256]{2,1,0:T(8,128)}, f32[4,256,256]{2,1,0:T(8,128)S(1)}, u32[]{:S(2)}, u32[]{:S(2)}) collective-permute-start(f32[4,256,256]{2,1,0:T(8,128)} %t_own.3), channel_id=1, source_target_pairs={{0,1},{1,0},{2,3},{3,2},{4,5},{5,4},{6,7},{7,6},{8,9},{9,8},{10,11... | collective-permute-start | bytes 3145736 | tf_op jit(solution)/shard_map/ppermute | solution.py:456
  9.3 3.5 %copy-start.1 = (f32[4,256,256]{2,1,0:T(8,128)}, f32[4,256,256]{2,1,0:T(8,128)S(1)}, u32[]{:S(2)}) copy-start(f32[4,256,256]{2,1,0:T(8,128)S(1)} %collective-permute-done.1.t_other) | copy-start | bytes 3145732
  9.3 8.3 %copy-start.9 = (s32[8,512]{1,0:T(8,128)S(1)}, s32[8,512]{1,0:T(8,128)}, u32[]{:S(2)}) copy-start(s32[8,512]{1,0:T(8,128)} %param.9) | copy-start | bytes 49156
  12.8 0.7 copy-start.8
  13.4 17.0 %collective-permute-start.2 = (f32[8,168,128]{2,1,0:T(8,128)}, f32[8,168,128]{2,1,0:T(8,128)}, u32[]{:S(2)}, u32[]{:S(2)}) collective-permute-start(f32[8,168,128]{2,1,0:T(8,128)} %get-tuple-element.14), channel_id=1, source_target_pairs={{1,4},{3,6},{4,1},{5,8},{6,3},{7,10},{8,5},{9,12},{10,7},{11,14},{... | collective-permute-start | bytes 2064392 | tf_op jit(solution)/shard_map/ppermute | solution.py:504
  16.9 13.5 %collective-permute-start.3 = (f32[8,88,128]{2,1,0:T(8,128)}, f32[8,88,128]{2,1,0:T(8,128)}, u32[]{:S(2)}, u32[]{:S(2)}) collective-permute-start(f32[8,88,128]{2,1,0:T(8,128)} %get-tuple-element.15), channel_id=1, source_target_pairs={{0,2},{2,0},{1,3},{3,1},{4,6},{6,4},{5,7},{7,5},{8,10},{10,8},{9,1... | collective-permute-start | bytes 1081352 | tf_op jit(solution)/shard_map/ppermute | solution.py:502
  17.7 11.9 %collective-permute-start.4 = (f32[8,40,128]{2,1,0:T(8,128)}, f32[8,40,128]{2,1,0:T(8,128)S(1)}, u32[]{:S(2)}, u32[]{:S(2)}) collective-permute-start(f32[8,40,128]{2,1,0:T(8,128)} %copy-done.8), channel_id=1, source_target_pairs={{1,6},{3,4},{4,3},{5,10},{6,1},{7,8},{8,7},{9,14},{10,5},{11,12},{... | collective-permute-start | bytes 491528 | tf_op jit(solution)/shard_map/ppermute | solution.py:503
  20.7 1.2 %copy-start.2 = (f32[4,256,256]{2,1,0:T(8,128)S(1)}, f32[4,256,256]{2,1,0:T(8,128)}, u32[]{:S(2)}) copy-start(f32[4,256,256]{2,1,0:T(8,128)} %copy-done.1) | copy-start | bytes 3145732
  21.9 8.5 %copy-start.6 = (s32[8]{0:T(128)S(1)}, s32[8]{0:T(128)}, u32[]{:S(2)}) copy-start(s32[8]{0:T(128)} %refs_6_.1) | copy-start | bytes 100
  21.9 8.5 %copy-start.7 = (f32[4]{0:T(128)S(1)}, f32[4]{0:T(128)}, u32[]{:S(2)}) copy-start(f32[4]{0:T(128)} %refs_7_.1) | copy-start | bytes 52
  30.4 1.5 %copy-start.3 = (f32[3456,128]{1,0:T(8,128)S(1)}, f32[3456,128]{1,0:T(8,128)}, u32[]{:S(2)}) copy-start(f32[3456,128]{1,0:T(8,128)} %get-tuple-element.17.refs_3_) | copy-start | bytes 5308420
  31.9 1.5 %copy-start.4 = (f32[3456,128]{1,0:T(8,128)S(1)}, f32[3456,128]{1,0:T(8,128)}, u32[]{:S(2)}) copy-start(f32[3456,128]{1,0:T(8,128)} %get-tuple-element.18.refs_4_) | copy-start | bytes 5308420
  72.3 2.7 %collective-permute-start.5 = (f32[2,4,128,256]{3,2,1,0:T(8,128)S(1)}, f32[2,4,128,256]{3,2,1,0:T(8,128)S(1)}, u32[]{:S(2)}, u32[]{:S(2)}) collective-permute-start(f32[2,4,128,256]{3,2,1,0:T(8,128)S(1)} %get-tuple-element.19), channel_id=1, source_target_pairs={{0,1},{1,0},{2,3},{3,2},{4,5},{5,4},{6,7},{7,6},{8,9},{9,8},{10,11... | collective-permute-start | bytes 3145736 | tf_op jit(solution)/shard_map/ppermute | solution.py:544

commit v3 on v2

--- a/solution.py
+++ b/solution.py
@@ -16,7 +16,10 @@
 LANES = 128
 WIDE = 6
 LOCAL = 200
-REGION = 144
+REGION = 140
+STEP_ROWS = 70
+BLOCK = 10
+SPAN = 5
 EDGE = 72
 ROWS_P = 2 * EDGE + 8 + 16
 ROWS_G = EDGE + 16
@@ -152,14 +155,65 @@
         one(other, t_other, index, (1 - core) * depth + index)
 
 
-def stack_kernel(own, other, t_own, t_other, heat, now, cells, t_cells, sems, t_sems):
+def permutation(inverse):
+    rows = lax.broadcasted_iota(jnp.int32, (256, 256), 0)
+    cols = lax.broadcasted_iota(jnp.int32, (256, 256), 1)
+    if inverse:
+        rows, cols = cols, rows
+    return jnp.where(rows == 4 * (cols % 64) + cols // 64, 1.0, 0.0).astype(jnp.bfloat16)
+
+
+def permuted(value, matrix):
+    total = None
+    for _ in range(3):
+        part = value.astype(jnp.bfloat16)
+        value = value - part.astype(F32)
+        moved = jnp.dot(part, matrix, preferred_element_type=F32)
+        total = moved if total is None else total + moved
+    return total
+
+
+def to_groups(first, second):
+    low = lane_ids() < 64
+    out = []
+    for half in range(2):
+        one = first[:, half * LANES : (half + 1) * LANES]
+        two = second[:, half * LANES : (half + 1) * LANES]
+        out += [jnp.where(low, one, turn(two, 64)), jnp.where(low, turn(one, 64), two)]
+    return out
+
+
+def to_rows(parts):
+    low = lane_ids() < 64
+    one, two = [], []
+    for half in range(2):
+        left, right = parts[2 * half], parts[2 * half + 1]
+        one.append(jnp.where(low, left, turn(right, 64)))
+        two.append(jnp.where(low, turn(left, 64), right))
+    return jnp.concatenate(one, axis=1), jnp.concatenate(two, axis=1)
+
+
+def group_cells(src, dst, matrix, stop=None):
+    @pl.loop(0, STEP_ROWS // BLOCK)
+    def _(block):
+        values = []
+        for group in range(2):
+            where = pl.ds(pl.multiple_of((group * STEP_ROWS + block * BLOCK) * 8, 8), BLOCK * 8)
+            values.append(permuted(jnp.concatenate([src[0, where, :], src[1, where, :]], axis=1), matrix))
+        for step in range(BLOCK):
+            parts = to_groups(*(value[8 * step : 8 * step + 8] for value in values))
+            for col in range(4):
+                dst[rows8((block * BLOCK + step + 1) * 40 + 8 * col), :] = parts[col]
+
+
+def stack_kernel(own, other, t_own, t_other, heat, heat_halo, now, cells, t_cells, t_rows, sems, t_sems):
     core = lax.axis_index("ta")
     low = lane_ids() < 64
     zero = jnp.zeros((8, LANES), F32)
     depth, rows, _ = t_own.shape
     layers = 2 * depth
     height = own.shape[0] // depth
-    t_height = REGION - 8
+    t_height = 136
     copies = []
     for which, (src, t_src) in enumerate(((own, t_own), (other, t_other))):
         base = core * depth if which == 0 else (1 - core) * depth
@@ -180,73 +234,64 @@
         copy.start()
     for copy in copies:
         copy.wait()
-    region = 56 - core * 56
-    t_first = 8 - core * 8
-    t_halo = core * t_height
+    region = 58 - core * 56
 
     @pl.loop(0, REGION // 4)
     def _(block):
         for step in range(4):
             row = block * 4 + step
             parts = [turn(cells[pl.ds(region + row + col * LOCAL, layers, stride=height), :], 64) for col in range(3)]
-            for col in range(3):
-                heat[rows8(row * 24 + 8 * col), :] = jnp.where(low, parts[col], parts[(col + 1) % 3])
-
-    @pl.loop(0, t_height // 4)
+            for col in range(2):
+                heat[col, rows8(row * 8), :] = jnp.where(low, parts[col], parts[col + 1])
+            heat_halo[rows8(row * 8), :] = jnp.where(low, parts[2], parts[0])
+
+    @pl.loop(0, (REGION - 6) // 2)
     def _(block):
-        for step in range(4):
-            row = block * 4 + step
+        for step in range(2):
+            row = block * 2 + step
             for col in range(2):
-                part = t_cells[col, pl.ds(row, layers, stride=t_height), :]
-                now[rows8((t_first + row) * 24 + 8 * col), :] = part
-            now[rows8((t_first + row) * 24 + 16), :] = zero
-
-    @pl.loop(0, 8)
-    def _(row):
-        for col in range(3):
-            now[rows8((t_halo + row) * 24 + 8 * col), :] = zero
+                part = t_cells[col, pl.ds(2 * core + row, layers, stride=t_height), :]
+                t_rows[col, rows8((6 - 6 * core + row) * 8), :] = part
+
+    for row in range(6):
+        for col in range(2):
+            t_rows[col, rows8((134 * core + row) * 8), :] = zero
+    group_cells(t_rows, now, permutation(False))
+
+    @pl.loop(0, STEP_ROWS + 2)
+    def _(step):
+        now[rows8(step * 40 + 32), :] = zero
 
 
 def solve_kernel(sides, bounds, *refs):
     count = len(sides)
     from_p, refs = refs[0], refs[1:]
     from_g, from_d, refs = refs[:count], refs[count : 2 * count], refs[2 * count :]
-    heat_in, now_in, flow, material, conductivity = refs[:5]
-    t_out, h_out, sent = refs[5:8]
-    heat, now, later, cond, f_down, f_right, f_above, inverse, base, t_stage, h_stage, sems = refs[8:]
+    heat_in, halo_in, now_in, flow, material, conductivity = refs[:6]
+    t_out, h_out, sent = refs[6:9]
+    rows_heat, rows_halo, rows_t, t_halo, heat, now, later, cond = refs[9:17]
+    f_down, f_right, f_above, inverse, base, t_stage, h_stage, sems = refs[17:]
     core = lax.axis_index("ta")
     gx, gy = lax.axis_index("gx"), lax.axis_index("gy")
     lane = lane_ids()
     level = lax.broadcasted_iota(jnp.int32, (8, LANES), 0)
     low = lane < 64
+    zero = jnp.zeros((8, LANES), F32)
     layers = 8
     depth = layers // 2
-    edge = core * EDGE
-    t_first = 8 - core * 8
-    t_halo = core * (REGION - 8)
-
-    def at(row, col):
-        return rows8(row * 24 + 8 * col)
+
+    def at(step, col):
+        return rows8(step * 40 + 8 * col)
 
     def across(ref, row, height):
         return ref[pl.ds(row, layers, stride=height), :]
 
-    def add(ref, row, col, value):
-        ref[at(row, col), :] = ref[at(row, col), :] + value
-
-    @pl.loop(0, REGION // 4)
-    def _(block):
-        for step in range(4):
-            for col in range(3):
-                where = at(block * 4 + step, col)
-                heat[where, :] = heat_in[where, :]
-                now[where, :] = now_in[where, :]
-
-    def add_side(right, g_ref, d_ref):
+    def add_side(right, fresh, g_ref, d_ref):
         col = 1 if right else 0
         target = 0 if right else LANES - WIDE
         halo = (lane < WIDE) if right else (lane >= LANES - WIDE)
         main = (lane >= 64) if right else low
+        heat_from, halo_from = (heat_in, halo_in) if fresh else (rows_heat, rows_halo)
 
         @pl.loop(0, 8)
         def _(i):
@@ -255,49 +300,90 @@
             for j in range(9):
                 value = across(g_ref, 8 * j + i, ROWS_G)
                 turned = turn(value, 64)
-                one, two = (turned, value) if right else (value, turned)
-                add(heat, 8 * j + i, col, jnp.where(main, one, 0.0))
-                add(heat, EDGE + 8 * j + i, col, jnp.where(main, two, 0.0))
-            for j in range(18):
-                add(heat, 8 * j + i, 2, jnp.where(halo, turn(extra, target - WIDE * j), 0.0))
+                for k, part in ((j, turned if right else value), (j + 9, value if right else turned)):
+                    row = 8 * k + i - 2
+
+                    def put():
+                        where = rows8(row * 8)
+                        rows_heat[col, where, :] = heat_from[col, where, :] + jnp.where(main, part, 0.0)
+                        if fresh:
+                            rows_heat[1 - col, where, :] = heat_from[1 - col, where, :]
+                        moved = turn(extra, target - WIDE * k)
+                        rows_halo[where, :] = halo_from[where, :] + jnp.where(halo, moved, 0.0)
+
+                    if k == 0:
+                        pl.when(i >= 2)(put)
+                    elif k == 17:
+                        pl.when(i < 6)(put)
+                    else:
+                        put()
             for j in range(17):
-                add(now, t_first + 8 * j + i, 2, jnp.where(halo, turn(t_extra, target - WIDE * j), 0.0))
+                row = 8 * j + i
+                where = rows8((row + 8 - 8 * core) * 8)
+                t_halo[where, :] = t_halo[where, :] + jnp.where(halo, turn(t_extra, target - WIDE * j), 0.0)
+            extra = across(d_ref, 32 + i, ROWS_D)
+            where = rows8((core * 136 + i) * 8)
+            t_halo[where, :] = t_halo[where, :] + jnp.where(halo, turn(extra, target - 64 - 9 * WIDE), 0.0)
+
+        @pl.loop(0, 8)
+        def _(i):
             extra = across(d_ref, 32 + i, ROWS_D)
             for j in range(9):
                 value = across(d_ref, 8 * (j % 5) + i, ROWS_D)
                 if (j < 5) == right:
                     value = turn(value, 64)
-                add(heat, edge + 8 * j + i, col, jnp.where(main, value, 0.0))
-                add(heat, edge + 8 * j + i, 2, jnp.where(halo, turn(extra, target - 64 - WIDE * j), 0.0))
-            add(now, t_halo + i, 2, jnp.where(halo, turn(extra, target - 64 - 9 * WIDE), 0.0))
+
+                def put():
+                    where = rows8((edge + 8 * j + i) * 8)
+                    rows_heat[col, where, :] = rows_heat[col, where, :] + jnp.where(main, value, 0.0)
+                    moved = turn(extra, target - 64 - WIDE * j)
+                    rows_halo[where, :] = rows_halo[where, :] + jnp.where(halo, moved, 0.0)
+
+                edge_row(i, j, put)
 
     halos = (lane < WIDE) | (lane >= LANES - WIDE)
+    edge = core * EDGE - 2
+
+    def edge_row(i, j, put):
+        row = edge + 8 * j + i
+        if j in (0, 8):
+            pl.when((row >= 0) & (row < REGION))(put)
+        else:
+            put()
+
+    @pl.loop(0, 144 // 4)
+    def _(block):
+        for step in range(4):
+            t_halo[rows8((block * 4 + step) * 8), :] = zero
+
+    for place, (side, g_ref, d_ref) in enumerate(zip(sides, from_g, from_d)):
+        if side is None:
+            pl.when(gy == 0)(functools.partial(add_side, True, True, g_ref, d_ref))
+            pl.when(gy > 0)(functools.partial(add_side, False, True, g_ref, d_ref))
+        else:
+            add_side(side, place == 0, g_ref, d_ref)
 
     @pl.loop(0, 8)
     def _(i):
         extra = across(from_p, 2 * EDGE + i, ROWS_P)
         for j in range(9):
-            row = edge + 8 * j + i
-            for col in range(2):
-                add(heat, row, col, across(from_p, col * EDGE + 8 * j + i, ROWS_P))
-            add(heat, row, 2, jnp.where(halos, turn(extra, LANES - WIDE - 2 * WIDE * j), 0.0))
-        for col in range(2):
-            now[at(t_halo + i, col), :] = across(from_p, 2 * EDGE + 8 + 8 * col + i, ROWS_P)
-
-    for side, g_ref, d_ref in zip(sides, from_g, from_d):
-        if side is None:
-            pl.when(gy == 0)(functools.partial(add_side, True, g_ref, d_ref))
-            pl.when(gy > 0)(functools.partial(add_side, False, g_ref, d_ref))
-        else:
-            add_side(side, g_ref, d_ref)
+
+            def put():
+                where = rows8((edge + 8 * j + i) * 8)
+                for col in range(2):
+                    part = across(from_p, col * EDGE + 8 * j + i, ROWS_P)
+                    rows_heat[col, where, :] = rows_heat[col, where, :] + part
+                moved = turn(extra, LANES - WIDE - 2 * WIDE * j)
+                rows_halo[where, :] = rows_halo[where, :] + jnp.where(halos, moved, 0.0)
+
+            edge_row(i, j, put)
 
     def to_stage(stage, src):
         @pl.loop(0, 16)
         def _(tile):
             for layer in range(layers):
                 for col in range(2):
-                    start = (8 + 8 * tile) * 24 + 8 * col + layer
-                    value = src[pl.ds(start, 8, stride=24), :]
+                    value = src[col, pl.ds((6 + 8 * tile) * 8 + layer, 8, stride=8), :]
                     stage[layer, rows8(8 * tile), col * LANES : (col + 1) * LANES] = value
 
     def outputs(stage, which, out):
@@ -310,19 +396,71 @@
             pltpu.make_async_copy(mine, out.at[:, place, :], sems.at[which, 1]),
         )
 
-    to_stage(h_stage, heat)
+    to_stage(h_stage, rows_heat)
     for copy in outputs(h_stage, 1, h_out):
         copy.start()
 
+    matrix = permutation(False)
+    group_cells(rows_heat, heat, matrix)
+
+    def spread_halo(first, second):
+        moved = jnp.where(lane < 64 + WIDE, turn(first, 64), first)
+        other = jnp.where(lane < WIDE, second, turn(second, 64))
+        value = jnp.where(low, other, moved)
+        keep = (lane < WIDE) | ((lane >= 64 - WIDE) & (lane < 64 + WIDE)) | (lane >= LANES - WIDE)
+        return jnp.where(keep, value, 0.0)
+
+    t_edge = jnp.concatenate(
+        [
+            jnp.concatenate([across(from_p, 2 * EDGE + 8 + 8 * col + i, ROWS_P) for i in range(8)], axis=0)
+            for col in range(2)
+        ],
+        axis=1,
+    )
+    t_edge = permuted(t_edge, matrix)
+
+    @pl.loop(0, STEP_ROWS // 2)
+    def _(block):
+        for part in range(2):
+            step = block * 2 + part
+            first, second = rows8(step * 8), rows8((step + STEP_ROWS) * 8)
+            heat[at(step + 1, 4), :] = spread_halo(rows_halo[first, :], rows_halo[second, :])
+            first, second = rows8((step + 2) * 8), rows8((step + STEP_ROWS + 2) * 8)
+            now[at(step + 1, 4), :] = spread_halo(t_halo[first, :], t_halo[second, :])
+            for col in range(4):
+                now[at(step + 1, col), :] = now_in[at(step + 1, col), :]
+
+    @pl.when(core == 0)
+    def _():
+        for row in range(6):
+            value = t_edge[8 * row + 16 : 8 * row + 24]
+            parts = to_groups(value, value)
+            for col in range(4):
+                now[at(row + 1, col), :] = jnp.where(low, parts[col], now[at(row + 1, col), :])
+
+    @pl.when(core == 1)
+    def _():
+        for row in range(6):
+            value = t_edge[8 * row : 8 * row + 8]
+            parts = to_groups(value, value)
+            for col in range(4):
+                now[at(row + 65, col), :] = jnp.where(low, now[at(row + 65, col), :], parts[col])
+
+    def ghosts(ref):
+        for col in range(5):
+            ref[at(0, col), :] = turn(ref[at(STEP_ROWS, col), :], 64)
+            ref[at(STEP_ROWS + 1, col), :] = turn(ref[at(1, col), :], 64)
+
+    last = (lane == 63) | (lane == 127)
+    first = (lane == 0) | (lane == 64)
+
     def to_right(values):
-        moved = [turn(value, -1) for value in values]
-        last = lane == LANES - 1
-        return [jnp.where(last, moved[(col + 1) % 3], moved[col]) for col in range(3)]
+        inner, outer = turn(values[0], -1), turn(values[4], -1)
+        return values[1:4] + [jnp.where(last, outer, inner), jnp.where(last, inner, outer)]
 
     def to_left(values):
-        moved = [turn(value, 1) for value in values]
-        first = lane == 0
-        return [jnp.where(first, moved[(col + 2) % 3], moved[col]) for col in range(3)]
+        inner, outer = turn(values[3], 1), turn(values[4], 1)
+        return [jnp.where(first, outer, inner)] + values[:3] + [jnp.where(first, inner, outer)]
 
     def upper(value):
         return pltpu.roll(value, 7, 0)
@@ -331,51 +469,48 @@
         return pltpu.roll(value, 1, 0)
 
     has_right = (gy + 1) * 256 < bounds[1]
-    right_lanes = (lane < WIDE) & has_right
-    left_lanes = (lane >= LANES - WIDE) & (gy > 0)
-    one = jnp.full((8, LANES), 1.0, F32)
-    col_masks = [one, one, jnp.where(right_lanes | left_lanes, 1.0, 0.0)]
+    half_lane = jnp.where(low, lane, lane - 64)
+    keep = ((half_lane < WIDE) & has_right) | ((half_lane >= 64 - WIDE) & (gy > 0))
+    halo_mask = jnp.where(keep, 1.0, 0.0)
     scale = jnp.full((8, LANES), conductivity[material[0]], F32)
     for layer in range(1, layers):
         scale = jnp.where(level == layer, conductivity[material[layer]], scale)
-    scales = [scale * mask for mask in col_masks]
     not_top = jnp.where(level < layers - 1, 1.0, 0.0)
     not_bottom = jnp.where(level > 0, 1.0, 0.0)
-    flows = [flow[:, col * LANES : (col + 1) * LANES] for col in range(3)]
-    first_row = gx * 256 + core * 128 - 8
-
-    def row_mask(row):
-        place = first_row + row
-        return jnp.where((place >= 0) & (place < bounds[0]), 1.0, 0.0)
-
-    for ref in (now, later, cond, f_down):
-        for row in (0, 1, REGION - 2, REGION - 1):
-            for col in range(3):
-                if ref is not now:
-                    ref[at(row, col), :] = jnp.zeros((8, LANES), F32)
-
-    def conductances(src, start, stop):
-        @pl.loop(0, (stop - start) // 4)
+    flows = [flow[8 * col : 8 * col + 8, :] for col in range(5)]
+    first_row = gx * 256 + core * 128 - 6
+
+    def masks(step):
+        ones = []
+        for group in range(2):
+            row = first_row + step + group * STEP_ROWS
+            ones.append(jnp.where((row >= 0) & (row < bounds[0]), 1.0, 0.0))
+        inner = jnp.where(low, ones[0], ones[1])
+        return [inner] * 4 + [jnp.where(low, ones[1], ones[0]) * halo_mask]
+
+    def conductances(src):
+        @pl.loop(0, STEP_ROWS // 5)
         def _(block):
-            for step in range(4):
-                row = start + block * 4 + step
-                mask = row_mask(row)
-                for col in range(3):
-                    where = at(row, col)
-                    cond[where, :] = (scales[col] * mask) * (1.0 + 0.5 * jnp.tanh(src[where, :]))
-
-    def coefficients(src, start, stop):
-        @pl.loop(0, (stop - start) // 2)
+            for part in range(5):
+                step = block * 5 + part
+                mask = masks(step)
+                for col in range(5):
+                    where = at(step + 1, col)
+                    cond[where, :] = (scale * mask[col]) * (1.0 + 0.5 * jnp.tanh(src[where, :]))
+
+        ghosts(cond)
+
+    def coefficients(src):
+        @pl.loop(0, STEP_ROWS // 5)
         def _(block):
-            first = start + block * 2
-            lines = [[cond[at(first + step, col), :] for col in range(3)] for step in range(-1, 3)]
-            for step in range(2):
-                row = first + step
-                up, here, down = lines[step], lines[step + 1], lines[step + 2]
-                mask = row_mask(row)
+            start = block * 5
+            lines = [[cond[at(start + part, col), :] for col in range(5)] for part in range(7)]
+            for part in range(5):
+                up, here, down = lines[part], lines[part + 1], lines[part + 2]
+                mask = masks(start + part)
                 rights, lefts = to_right(here), to_left(here)
-                for col in range(3):
-                    where = at(row, col)
+                for col in range(5):
+                    where = at(start + part + 1, col)
                     centre = here[col]
                     over = centre + upper(centre) * not_top
                     under = centre + lower(centre) * not_bottom
@@ -386,46 +521,58 @@
                     f_down[where, :] = face_down
                     f_right[where, :] = face_right
                     f_above[where, :] = over * not_top
-                    inverse[where, :] = (mask * col_masks[col]) / total
+                    inverse[where, :] = mask[col] / total
                     base[where, :] = src[where, :] + heat[where, :]
-            del lines
-
-        for col in range(3):
-            centre, down = cond[at(start - 1, col), :], cond[at(start, col), :]
-            f_down[at(start - 1, col), :] = 0.5 * (centre + down)
-
-    def sweep(src, dst, start, stop):
-        @pl.loop(0, (stop - start) // 4)
+
+        for col in range(5):
+            f_down[at(0, col), :] = 0.5 * (cond[at(0, col), :] + cond[at(1, col), :])
+
+    def sweep(src, dst):
+        @pl.loop(0, STEP_ROWS // SPAN)
         def _(block):
-            first = start + block * 4
-            lines = [[src[at(first + step, col), :] for col in range(3)] for step in range(-1, 5)]
-            faces = [[f_down[at(first + step, col), :] for col in range(3)] for step in range(-1, 4)]
-            for step in range(4):
-                up, here, down = lines[step], lines[step + 1], lines[step + 2]
-                sides_right = [f_right[at(first + step, col), :] for col in range(3)]
+            start = block * SPAN
+            lines = [[src[at(start + part, col), :] for col in range(5)] for part in range(SPAN + 2)]
+            faces = [[f_down[at(start + part, col), :] for col in range(5)] for part in range(SPAN + 1)]
+            for part in range(SPAN):
+                up, here, down = lines[part], lines[part + 1], lines[part + 2]
+                face_right = [f_right[at(start + part + 1, col), :] for col in range(5)]
                 rights = to_right(here)
-                lefts = to_left([face * value for face, value in zip(sides_right, here)])
-                for col in range(3):
-                    where = at(first + step, col)
+                lefts = to_left([face * value for face, value in zip(face_right, here)])
+                for col in range(5):
+                    where = at(start + part + 1, col)
                     face_above = f_above[where, :]
-                    total = base[where, :] + (faces[step][col] + flows[col]) * up[col]
-                    total = total + faces[step + 1][col] * down[col]
-                    total = total + (sides_right[col] * rights[col] + lefts[col])
+                    total = base[where, :] + (faces[part][col] + flows[col]) * up[col]
+                    total = total + faces[part + 1][col] * down[col]
+                    total = total + (face_right[col] * rights[col] + lefts[col])
                     total = total + (face_above * upper(here[col]) + lower(face_above * here[col]))
                     dst[where, :] = total * inverse[where, :]
 
-    conductances(now, 2, 142)
-    coefficients(now, 2, 142)
-    sweep(now, later, 2, 142)
-    sweep(later, now, 2, 142)
-    sweep(now, later, 4, 140)
-    conductances(later, 4, 140)
-    coefficients(later, 6, 138)
-    sweep(later, now, 6, 138)
-    sweep(now, later, 6, 138)
-    sweep(later, now, 8, 136)
-
-    to_stage(t_stage, now)
+        ghosts(dst)
+
+    ghosts(now)
+    for _ in range(STEPS):
+        conductances(now)
+        coefficients(now)
+        for _ in range(SWEEPS):
+            sweep(now, later)
+            now, later = later, now
+
+    back = permutation(True)
+
+    @pl.loop(0, STEP_ROWS // BLOCK)
+    def _(block):
+        values = ([], [])
+        for part in range(BLOCK):
+            pair = to_rows([now[at(block * BLOCK + part + 1, col), :] for col in range(4)])
+            for group in range(2):
+                values[group].append(pair[group])
+        for group in range(2):
+            value = permuted(jnp.concatenate(values[group], axis=0), back)
+            where = pl.ds(pl.multiple_of((group * STEP_ROWS + block * BLOCK) * 8, 8), BLOCK * 8)
+            for col in range(2):
+                rows_t[col, where, :] = value[:, col * LANES : (col + 1) * LANES]
+
+    to_stage(t_stage, rows_t)
     for copy in outputs(t_stage, 0, t_out):
         copy.start()
     for copy in outputs(h_stage, 1, h_out) + outputs(t_stage, 0, t_out):
@@ -505,18 +652,25 @@
     in_sides = [None] if n_gy == 2 else [False, True]
 
     wide = jnp.pad(channel_mask, ((0, 0), (RIM, RIM)))
-    mask = lax.dynamic_slice_in_dim(wide, lax.axis_index("gy") * cols, cols + 2 * RIM, 1)
-    flow = COOLANT * jnp.concatenate([mask[:, RIM:], mask[:, :RIM]], axis=1).astype(F32)
-
-    stacked = array((REGION * 24, LANES), F32)
-    heat, now = pl.pallas_call(
+    mask = lax.dynamic_slice_in_dim(wide, lax.axis_index("gy") * cols, cols + 2 * RIM, 1).astype(F32) * COOLANT
+    inner = mask[:, RIM : RIM + cols].reshape(layers, 64, 4).transpose(2, 0, 1)
+    outer = jnp.zeros((layers, 64 - 2 * WIDE), F32)
+    outer = jnp.concatenate([mask[:, RIM + cols :][:, :WIDE], outer, mask[:, RIM - WIDE : RIM]], axis=1)
+    flow = jnp.concatenate([inner, outer[None]], axis=0).reshape(layers * 5, 64)
+    flow = jnp.concatenate([flow, flow], axis=1)
+
+    natural = array((2, REGION * 8, LANES), F32)
+    edge = array((REGION * 8, LANES), F32)
+    grouped = array(((STEP_ROWS + 2) * 40, LANES), F32)
+    heat, heat_halo, now = pl.pallas_call(
         stack_kernel,
-        out_shape=(stacked, stacked),
+        out_shape=(natural, edge, grouped),
         in_specs=[ANY] * 4,
-        out_specs=(VMEM, VMEM),
+        out_specs=(VMEM, VMEM, VMEM),
         scratch_shapes=[
             pltpu.VMEM((layers * 3 * LOCAL, LANES), F32),
-            pltpu.VMEM((2, layers * (REGION - 8), LANES), F32),
+            pltpu.VMEM((2, layers * 136, LANES), F32),
+            pltpu.VMEM(natural.shape, F32),
             pltpu.SemaphoreType.DMA((2,)),
             pltpu.SemaphoreType.DMA((2, depth, 2)),
         ],
@@ -526,7 +680,7 @@
 
     whole = array((depth, rows, cols), F32)
     half = array((2, depth, rows // 2, cols), F32)
-    inner = pltpu.VMEM((REGION * 24, LANES), F32)
+    work = pltpu.VMEM(grouped.shape, F32)
     stage = pltpu.VMEM((layers, rows // 2, cols), F32)
 
     def flat(value):
@@ -535,12 +689,19 @@
     t_part, h_part, sent = pl.pallas_call(
         functools.partial(solve_kernel, in_sides, (n_gx * rows, n_gy * cols)),
         out_shape=(whole, whole, half),
-        in_specs=[VMEM] * (1 + 2 * count + 3) + [SMEM, SMEM],
+        in_specs=[VMEM] * (1 + 2 * count + 4) + [SMEM, SMEM],
         out_specs=(ANY, ANY, ANY),
-        scratch_shapes=[inner] * 9 + [stage, stage, pltpu.SemaphoreType.DMA((2, 2))],
+        scratch_shapes=[
+            pltpu.VMEM(natural.shape, F32),
+            pltpu.VMEM(edge.shape, F32),
+            pltpu.VMEM(natural.shape, F32),
+            pltpu.VMEM((144 * 8, LANES), F32),
+        ]
+        + [work] * 9
+        + [stage, stage, pltpu.SemaphoreType.DMA((2, 2))],
         compiler_params=PARAMS,
         name="solve",
-    )(flat(from_p), *map(flat, from_g), *map(flat, from_d), heat, now, flow, material, conductivity)
+    )(flat(from_p), *map(flat, from_g), *map(flat, from_d), heat, heat_halo, now, flow, material, conductivity)
     received = lax.ppermute(sent, "ta", swap)
     return pl.pallas_call(
         place_kernel,

time: 76.3 us -> 67.3 us (0.88)
  Pallas kernels: 50.9 us -> 45.1 us
  waiting for transfers between devices: 9.11 us -> 6.96 us
  local copies, waits for them, and re-layouts: 7 us -> 5.29 us
    pallas_call x1, Pallas kernels: 38.9 us -> 27.4 us  [on_device(): pl.pallas_call(functools.partial(solve_kernel, in_sides, (n_gx * rows, n_...]
    pallas_call x1, Pallas kernels: 5.99 us -> 9.51 us  [on_device(): pl.pallas_call(stack_kernel, out_shape=(natural, edge, grouped), in_specs...]
    unnamed x21 -> x19, local copies, waits for them, and re-layouts: 6.91 us -> 4.86 us
    ppermute x1, waiting for transfers between devices: 1.66 us -> 0.01 us  [on_device(): lax.ppermute(value, along, moves(shift))]
    pallas_call x1, Pallas kernels: 3.47 us -> 5.02 us  [on_device(): pl.pallas_call(functools.partial(pack_kernel, out_sides), out_shape=(arra...]
  transfers between devices with their start and end apart: 6 -> 6, of which waited for: 4 -> 3; matrix products, arithmetic and copies ran while one was open for 0% -> 1% of each run, Pallas kernels for 8% -> 14%
where the time goes in v3:
time: 67.3 us; the launch traced here: 66.3 us
  Pallas kernels  45.1 us (67%)
  starting transfers between devices  7.99 us (12%)
  waiting for transfers between devices  6.96 us (10%)
  local copies, waits for them, and re-layouts  5.29 us (8%)
  between operations  0.74 us (1%)
    pallas_call x1, Pallas kernels, on_device(): pl.pallas_call(functools.partial(solve_kernel, in_sides, (n_gx * rows, n_...  27.4 us
    pallas_call x1, Pallas kernels, on_device(): pl.pallas_call(stack_kernel, out_shape=(natural, edge, grouped), in_specs...  9.51 us
    pallas_call x1, Pallas kernels, on_device(): pl.pallas_call(functools.partial(pack_kernel, out_sides), out_shape=(arra...  5.02 us
    unnamed x19, local copies, waits for them, and re-layouts  4.86 us
    ppermute x1, waiting for transfers between devices, on_device(): t_other = lax.ppermute(t_initial, 'ta', swap)  4.31 us
    ppermute x1, starting transfers between devices, on_device(): from_p = lax.ppermute(packed[0], along, moves(0))  3.45 us
    ppermute x1, starting transfers between devices, on_device(): lax.ppermute(value, along, moves(shift))  2.88 us
    ppermute x1, waiting for transfers between devices, on_device(): received = lax.ppermute(sent, 'ta', swap)  2.58 us
  transfers between devices with their start and end apart: 6, of which 3 were waited for; matrix products, arithmetic and copies ran while one was open for 1% of the time, Pallas kernels for 14%

profile of v3, /device:TPU:21, one launch (start us, length us, event | category | flops | bytes accessed | tf_op | source)
XLA Modules:
  0.0 66.3 jit_solution(4189396825742971630)
XLA Ops:
  0.6 0.0 copy-start.1
  0.6 0.8 %copy.15.exponent = s32[4,6,6]{2,1,0:T(8,128)S(1)} copy(s32[4,6,6]{2,0,1:T(4,128)} %param.8) | data formatting | bytes 1152 | tf_op args[2]
  1.4 0.0 copy-start.3
  1.4 1.3 %copy-done.3 = bf16[4,384,384]{2,1,0:T(8,128)(2,1)S(1)} copy-done((bf16[4,384,384]{2,1,0:T(8,128)(2,1)S(1)}, bf16[4,384,384]{2,1,0:T(8,128)(2,1)}, u32[]{:S(2)}) %copy-start.3) | copy-done | bytes 1179672
  2.7 2.2 %decode.1 = (f32[4,3,200,128]{3,2,1,0:T(8,128)S(1)}, f32[4,3,200,128]{3,2,1,0:T(8,128)}) custom-call(bf16[4,384,384]{2,1,0:T(8,128)(2,1)S(1)} %copy-done.3, s32[4,6,6]{2,1,0:T(8,128)S(1)} %copy.15.exponent), custom_call_target="tpu_custom_call" | custom-call | tf_op jit(solution)/shard_map/decode/pallas_call | solution.py:605
  4.9 0.7 %collective-permute-start = (f32[4,3,200,128]{3,2,1,0:T(8,128)}, f32[4,3,200,128]{3,2,1,0:T(8,128)S(1)}, u32[]{:S(2)}, u32[]{:S(2)}) collective-permute-start(f32[4,3,200,128]{3,2,1,0:T(8,128)} %get-tuple-element.14), channel_id=1, source_target_pairs={{0,1},{1,0},{2,3},{3,2},{4,5},{5,4},{6,7},{7,6},{8,9},{9,8},{10,11... | collective-permute-start | bytes 3686408 | tf_op jit(solution)/shard_map/ppermute | solution.py:618
  5.6 0.1 collective-permute-start.1
  5.7 4.3 %collective-permute-done.1.t_other = f32[4,256,256]{2,1,0:T(8,128)} collective-permute-done((f32[4,256,256]{2,1,0:T(8,128)}, f32[4,256,256]{2,1,0:T(8,128)}, u32[]{:S(2)}, u32[]{:S(2)}) %collective-permute-start.1) | collective-permute-done | bytes 1048608 | tf_op jit(solution)/shard_map/ppermute | solution.py:603
  10.0 0.0 collective-permute-done.other
  10.0 0.0 copy-start
  10.0 0.0 copy-done.1
  10.0 0.0 copy-start.8
  10.0 5.0 %pack.1 = (f32[8,168,128]{2,1,0:T(8,128)}, f32[8,88,128]{2,1,0:T(8,128)S(1)}, f32[8,40,128]{2,1,0:T(8,128)S(1)}) custom-call(f32[4,3,200,128]{3,2,1,0:T(8,128)S(1)} %get-tuple-element.13.own, f32[4,3,200,128]{3,2,1,0:T(8,128)S(1)} %collective-permute-done.other, f32[4,256,256]{2,1,0:T(8,128)S(1)} %copy-done.1, f32[4,256,256]{2,1,0:T(8,128)} %collective-permute-done.1.t_other), custom_call_target="tpu_custom_call" | custom-call | tf_op jit(solution)/shard_map/pack/pallas_call | solution.py:622
  15.1 0.0 copy-done
  15.1 0.0 copy-start.6
  15.1 0.7 %copy-done.6 = f32[8,88,128]{2,1,0:T(8,128)} copy-done((f32[8,88,128]{2,1,0:T(8,128)}, f32[8,88,128]{2,1,0:T(8,128)S(1)}, u32[]{:S(2)}) %copy-start.6) | copy-done | bytes 360472
  15.8 0.0 copy-start.7
  15.8 0.7 %copy-done.7 = f32[8,40,128]{2,1,0:T(8,128)} copy-done((f32[8,40,128]{2,1,0:T(8,128)}, f32[8,40,128]{2,1,0:T(8,128)S(1)}, u32[]{:S(2)}) %copy-start.7) | copy-done | bytes 163864
  16.5 3.5 %collective-permute-start.2 = (f32[8,168,128]{2,1,0:T(8,128)}, f32[8,168,128]{2,1,0:T(8,128)S(1)}, u32[]{:S(2)}, u32[]{:S(2)}) collective-permute-start(f32[8,168,128]{2,1,0:T(8,128)} %get-tuple-element.15), channel_id=1, source_target_pairs={{1,4},{3,6},{4,1},{5,8},{6,3},{7,10},{8,5},{9,12},{10,7},{11,14},{... | collective-permute-start | bytes 2064392 | tf_op jit(solution)/shard_map/ppermute | solution.py:651
  19.9 0.0 copy-done.8
  19.9 0.1 fusion.1
  20.0 0.1 slice.14
  20.1 0.1 copy.16
  20.2 0.1 copy.17
  20.3 0.1 pad.10.clone
  20.4 0.1 fusion.2
  20.5 0.7 %collective-permute-start.3 = (f32[8,88,128]{2,1,0:T(8,128)}, f32[8,88,128]{2,1,0:T(8,128)S(1)}, u32[]{:S(2)}, u32[]{:S(2)}) collective-permute-start(f32[8,88,128]{2,1,0:T(8,128)} %copy-done.6), channel_id=1, source_target_pairs={{0,2},{2,0},{1,3},{3,1},{4,6},{6,4},{5,7},{7,5},{8,10},{10,8},{9,1... | collective-permute-start | bytes 1081352 | tf_op jit(solution)/shard_map/ppermute | solution.py:649
  21.2 0.1 maximum_bitcast_fusion.1
  21.2 2.9 %collective-permute-start.4 = (f32[8,40,128]{2,1,0:T(8,128)}, f32[8,40,128]{2,1,0:T(8,128)S(1)}, u32[]{:S(2)}, u32[]{:S(2)}) collective-permute-start(f32[8,40,128]{2,1,0:T(8,128)} %copy-done.7), channel_id=1, source_target_pairs={{1,6},{3,4},{4,3},{5,10},{6,1},{7,8},{8,7},{9,14},{10,5},{11,12},{... | collective-permute-start | bytes 491528 | tf_op jit(solution)/shard_map/ppermute | solution.py:650
  24.1 0.1 pad_maximum_fusion.refs_6_
  24.2 0.0 copy-start.4
  24.2 0.0 copy-start.5
  24.2 9.5 %stack.1 = (f32[2,1120,128]{2,1,0:T(8,128)S(1)}, f32[1120,128]{1,0:T(8,128)S(1)}, f32[2880,128]{1,0:T(8,128)}) custom-call(f32[2400,128]{1,0:T(8,128)S(1)} %bitcast.12, f32[2400,128]{1,0:T(8,128)} %bitcast.13, f32[4,256,256]{2,1,0:T(8,128)S(1)} %copy-done.1, f32[4,256,256]{2,1,0:T(8,128)} %collective-permute-done.1.t_other), custom_call_target="tpu_custom_call" | custom-call | tf_op jit(solution)/shard_map/stack/pallas_call | solution.py:665
  33.7 0.0 collective-permute-done.4
  33.7 0.1 collective-permute-done.3
  33.8 0.0 collective-permute-done.2
  33.8 0.0 copy-done.4
  33.8 0.0 copy-done.5
  33.8 0.0 copy-start.2
  33.8 1.4 %copy-done.2 = f32[2880,128]{1,0:T(8,128)S(1)} copy-done((f32[2880,128]{1,0:T(8,128)S(1)}, f32[2880,128]{1,0:T(8,128)}, u32[]{:S(2)}) %copy-start.2) | copy-done | bytes 1474584
  35.2 27.4 %solve.1 = (f32[4,256,256]{2,1,0:T(8,128)}, f32[4,256,256]{2,1,0:T(8,128)}, f32[2,4,128,256]{3,2,1,0:T(8,128)S(1)}) custom-call(f32[1344,128]{1,0:T(8,128)S(1)} %bitcast.14, f32[704,128]{1,0:T(8,128)S(1)} %bitcast.15, f32[320,128]{1,0:T(8,128)S(1)} %bitcast.16, f32[2,1120,128]{2,1,0:T(8,128)S(1)} %get-tuple-element.18.refs_3_, ...), custom_call_target="tpu_custom_call" | custom-call | tf_op jit(solution)/shard_map/solve/pallas_call | solution.py:689
  62.6 0.1 collective-permute-start.5
  62.7 2.6 %collective-permute-done.5.received = f32[2,4,128,256]{3,2,1,0:T(8,128)S(1)} collective-permute-done((f32[2,4,128,256]{3,2,1,0:T(8,128)S(1)}, f32[2,4,128,256]{3,2,1,0:T(8,128)S(1)}, u32[]{:S(2)}, u32[]{:S(2)}) %collective-permute-start.5) | collective-permute-done | bytes 1048608 | tf_op jit(solution)/shard_map/ppermute | solution.py:705
  65.3 1.0 %place.1 = (f32[4,256,256]{2,1,0:T(8,128)}, f32[4,256,256]{2,1,0:T(8,128)}) custom-call(f32[2,4,128,256]{3,2,1,0:T(8,128)S(1)} %collective-permute-done.5.received, f32[4,256,256]{2,1,0:T(8,128)} %get-tuple-element.22.t_in, f32[4,256,256]{2,1,0:T(8,128)} %get-tuple-element.23.h_in), custom_call_target="tpu_custom_call", output_to_operand_aliasing={{0}: (1, {}), {1}: (2, {})} | custom-call | tf_op jit(solution)/shard_map/place/pallas_call | solution.py:706
  (2 shorter events, 0.0 us)
Async XLA Ops:
  0.6 9.4 %copy-start.1 = (f32[4,256,256]{2,1,0:T(8,128)S(1)}, f32[4,256,256]{2,1,0:T(8,128)}, u32[]{:S(2)}) copy-start(f32[4,256,256]{2,1,0:T(8,128)} %t_own.3) | copy-start | bytes 3145732
  1.4 1.3 %copy-start.3 = (bf16[4,384,384]{2,1,0:T(8,128)(2,1)S(1)}, bf16[4,384,384]{2,1,0:T(8,128)(2,1)}, u32[]{:S(2)}) copy-start(bf16[4,384,384]{2,1,0:T(8,128)(2,1)} %mantissa.1) | copy-start | bytes 3538948
  4.9 5.1 %collective-permute-start = (f32[4,3,200,128]{3,2,1,0:T(8,128)}, f32[4,3,200,128]{3,2,1,0:T(8,128)S(1)}, u32[]{:S(2)}, u32[]{:S(2)}) collective-permute-start(f32[4,3,200,128]{3,2,1,0:T(8,128)} %get-tuple-element.14), channel_id=1, source_target_pairs={{0,1},{1,0},{2,3},{3,2},{4,5},{5,4},{6,7},{7,6},{8,9},{9,8},{10,11... | collective-permute-start | bytes 3686408 | tf_op jit(solution)/shard_map/ppermute | solution.py:618
  5.6 4.4 %collective-permute-start.1 = (f32[4,256,256]{2,1,0:T(8,128)}, f32[4,256,256]{2,1,0:T(8,128)}, u32[]{:S(2)}, u32[]{:S(2)}) collective-permute-start(f32[4,256,256]{2,1,0:T(8,128)} %t_own.3), channel_id=1, source_target_pairs={{0,1},{1,0},{2,3},{3,2},{4,5},{5,4},{6,7},{7,6},{8,9},{9,8},{10,11... | collective-permute-start | bytes 3145736 | tf_op jit(solution)/shard_map/ppermute | solution.py:603
  10.0 5.0 %copy-start = (f32[4,3,200,128]{3,2,1,0:T(8,128)}, f32[4,3,200,128]{3,2,1,0:T(8,128)S(1)}, u32[]{:S(2)}) copy-start(f32[4,3,200,128]{3,2,1,0:T(8,128)S(1)} %collective-permute-done.other) | copy-start | bytes 3686404
  10.0 9.9 %copy-start.8 = (s32[8,512]{1,0:T(8,128)S(1)}, s32[8,512]{1,0:T(8,128)}, u32[]{:S(2)}) copy-start(s32[8,512]{1,0:T(8,128)} %param.9) | copy-start | bytes 49156
  15.1 0.7 %copy-start.6 = (f32[8,88,128]{2,1,0:T(8,128)}, f32[8,88,128]{2,1,0:T(8,128)S(1)}, u32[]{:S(2)}) copy-start(f32[8,88,128]{2,1,0:T(8,128)S(1)} %get-tuple-element.16) | copy-start | bytes 1081348
  15.8 0.7 %copy-start.7 = (f32[8,40,128]{2,1,0:T(8,128)}, f32[8,40,128]{2,1,0:T(8,128)S(1)}, u32[]{:S(2)}) copy-start(f32[8,40,128]{2,1,0:T(8,128)S(1)} %get-tuple-element.17) | copy-start | bytes 491524
  16.5 17.4 %collective-permute-start.2 = (f32[8,168,128]{2,1,0:T(8,128)}, f32[8,168,128]{2,1,0:T(8,128)S(1)}, u32[]{:S(2)}, u32[]{:S(2)}) collective-permute-start(f32[8,168,128]{2,1,0:T(8,128)} %get-tuple-element.15), channel_id=1, source_target_pairs={{1,4},{3,6},{4,1},{5,8},{6,3},{7,10},{8,5},{9,12},{10,7},{11,14},{... | collective-permute-start | bytes 2064392 | tf_op jit(solution)/shard_map/ppermute | solution.py:651
  20.5 13.3 %collective-permute-start.3 = (f32[8,88,128]{2,1,0:T(8,128)}, f32[8,88,128]{2,1,0:T(8,128)S(1)}, u32[]{:S(2)}, u32[]{:S(2)}) collective-permute-start(f32[8,88,128]{2,1,0:T(8,128)} %copy-done.6), channel_id=1, source_target_pairs={{0,2},{2,0},{1,3},{3,1},{4,6},{6,4},{5,7},{7,5},{8,10},{10,8},{9,1... | collective-permute-start | bytes 1081352 | tf_op jit(solution)/shard_map/ppermute | solution.py:649
  21.2 12.5 %collective-permute-start.4 = (f32[8,40,128]{2,1,0:T(8,128)}, f32[8,40,128]{2,1,0:T(8,128)S(1)}, u32[]{:S(2)}, u32[]{:S(2)}) collective-permute-start(f32[8,40,128]{2,1,0:T(8,128)} %copy-done.7), channel_id=1, source_target_pairs={{1,6},{3,4},{4,3},{5,10},{6,1},{7,8},{8,7},{9,14},{10,5},{11,12},{... | collective-permute-start | bytes 491528 | tf_op jit(solution)/shard_map/ppermute | solution.py:650
  24.2 9.6 %copy-start.4 = (s32[8]{0:T(128)S(1)}, s32[8]{0:T(128)}, u32[]{:S(2)}) copy-start(s32[8]{0:T(128)} %refs_7_.1) | copy-start | bytes 100
  24.2 9.6 %copy-start.5 = (f32[4]{0:T(128)S(1)}, f32[4]{0:T(128)}, u32[]{:S(2)}) copy-start(f32[4]{0:T(128)} %refs_8_.1) | copy-start | bytes 52
  33.8 1.4 %copy-start.2 = (f32[2880,128]{1,0:T(8,128)S(1)}, f32[2880,128]{1,0:T(8,128)}, u32[]{:S(2)}) copy-start(f32[2880,128]{1,0:T(8,128)} %get-tuple-element.20.refs_5_) | copy-start | bytes 4423684
  62.6 2.7 %collective-permute-start.5 = (f32[2,4,128,256]{3,2,1,0:T(8,128)S(1)}, f32[2,4,128,256]{3,2,1,0:T(8,128)S(1)}, u32[]{:S(2)}, u32[]{:S(2)}) collective-permute-start(f32[2,4,128,256]{3,2,1,0:T(8,128)S(1)} %get-tuple-element.21), channel_id=1, source_target_pairs={{0,1},{1,0},{2,3},{3,2},{4,5},{5,4},{6,7},{7,6},{8,9},{9,8},{10,11... | collective-permute-start | bytes 3145736 | tf_op jit(solution)/shard_map/ppermute | solution.py:705

commit v4 on v3

v4 whole, which is shorter than its diff:
```python
import functools

import jax
import jax.numpy as jnp
from jax import lax
from jax.experimental import pallas as pl
from jax.experimental.pallas import tpu as pltpu
from jax.sharding import PartitionSpec as P

RIM = 64
TILE = 64
STEPS = 2
SWEEPS = 3
COOLANT = 2.0

LANES = 128
WIDE = 6
REGION = 140
STEP_ROWS = 70
BLOCK = 35
SPAN = 5
SUM_ROWS = 272
HALF_ROWS = 144
SWAP = 3 * HALF_ROWS + 16
EDGE = 72
SLOTS = LANES // WIDE
ROWS_P = 2 * EDGE + 8 + 16
ROWS_G = SUM_ROWS // 2 + 16 + 16
ROWS_D = 40
F32 = jnp.float32
VMEM = pl.BlockSpec(memory_space=pltpu.VMEM)
SMEM = pl.BlockSpec(memory_space=pltpu.SMEM)
ANY = pl.BlockSpec(memory_space=pl.ANY)


def params(megabytes):
    return pltpu.CompilerParams(vmem_limit_bytes=megabytes << 20)


def rows8(start):
    return pl.ds(pl.multiple_of(start, 8), 8)


def lane_ids():
    return lax.broadcasted_iota(jnp.int32, (8, LANES), 1)


def turn(value, shift):
    shift = shift % LANES
    return pltpu.roll(value, shift, 1) if shift else value


def by_side(sides, body, *lists):
    for place, side in enumerate(sides):
        rest = [values[place] for values in lists]
        if side is None:
            first = lax.axis_index("gy") == 0
            pl.when(first)(functools.partial(body, True, place, *rest))
            pl.when(jnp.logical_not(first))(functools.partial(body, False, place, *rest))
        else:
            body(side, place, *rest)


def send_kernel(sides, mantissa, exponent, t_ref, *refs):
    count = len(sides)
    whole, to_up, to_down = refs[:3]
    to_g, to_d_up, to_d_down = refs[3 : 3 + count], refs[3 + count : 3 + 2 * count], refs[3 + 2 * count : 3 + 3 * count]
    plain, sems = refs[3 + 3 * count :]
    depth, rows, _ = mantissa.shape
    lane = lane_ids()
    low = lane < 64
    wide_lane = lax.broadcasted_iota(jnp.int32, (16, LANES), 1)

    def place(total, value, source, target, width):
        moved = turn(value, target - source)
        return jnp.where((lane >= target) & (lane < target + width), moved, total)

    def copy(layer):
        return pltpu.make_async_copy(plain.at[layer], whole.at[layer], sems.at[layer])

    def pack(layer):
        def cells(col, row):
            return plain[layer, col, row : row + 8, :]

        def t_cells(col, row):
            return t_ref[layer, row : row + 8, col * LANES : (col + 1) * LANES]

        for out, edge, t_edge in ((to_up, 0, 0), (to_down, rows - EDGE, rows - 2 * RIM - 8)):
            extra = jnp.zeros((8, LANES), F32)
            for j in range(9):
                left, right = cells(0, edge + 8 * j), cells(2, edge + 8 * j)
                out[layer, 8 * j : 8 * j + 8, :] = cells(1, edge + 8 * j)
                out[layer, EDGE + 8 * j : EDGE + 8 * j + 8, :] = jnp.where(low, right, left)
                extra = place(extra, jnp.where(low, left, right), 64 - WIDE, 2 * WIDE * j, 2 * WIDE)
            out[layer, 2 * EDGE : 2 * EDGE + 8, :] = extra
            for col in range(2):
                start = 2 * EDGE + 8 + 8 * col
                out[layer, start : start + 8, :] = t_cells(col, t_edge)

        def side(right, _, g_ref, up_ref, down_ref):
            col, t_col = (2, 1) if right else (0, 0)
            at, t_at = (64 - WIDE, LANES - WIDE) if right else (64, 0)
            half = SUM_ROWS // 2

            def both(one, two):
                return jnp.where(low, turn(two, 64), one) if right else jnp.where(low, one, turn(two, 64))

            for j in range(17):
                one, two = cells(col, RIM - 8 + 8 * j), cells(col, RIM - 8 + half + 8 * j)
                g_ref[layer, 8 * j : 8 * j + 8, :] = both(one, two)
            for first, parts, source in (
                (half, [cells(col, RIM - 8 + 8 * j) for j in range(34)], at),
                (half + 16, [t_cells(t_col, 8 * j) for j in range(32)], t_at),
            ):
                for part in range(2):
                    extra = jnp.zeros((8, LANES), F32)
                    for slot, value in enumerate(parts[part * SLOTS : (part + 1) * SLOTS]):
                        extra = place(extra, value, source, WIDE * slot, WIDE)
                    g_ref[layer, first + 8 * part : first + 8 * part + 8, :] = extra
            for out, edge, t_edge in ((up_ref, 0, 0), (down_ref, rows - EDGE, rows - 2 * RIM - 8)):
                strips = [cells(col, edge + 8 * j) for j in range(9)]
                for j in range(4):
                    out[layer, 8 * j : 8 * j + 8, :] = both(strips[j], strips[j + 5])
                start = 0 if right else 64
                extra = strips[4]
                for j in range(9):
                    extra = place(extra, strips[j], at, start + WIDE * j, WIDE)
                extra = place(extra, t_cells(t_col, t_edge), t_at, start + 9 * WIDE, WIDE)
                out[layer, 32:40, :] = extra

        by_side(sides, side, to_g, to_d_up, to_d_down)

    @pl.loop(0, depth)
    def _(layer):
        @pl.loop(0, rows // TILE)
        def _(tile_row):
            for col in range(3):
                left = exponent[tile_row, layer, 2 * col]
                right = exponent[tile_row, layer, 2 * col + 1]
                scale = jnp.exp2(jnp.where(wide_lane < TILE, left, right).astype(F32))
                for part in range(TILE // 16):
                    where = pl.ds(pl.multiple_of(tile_row * TILE + part * 16, 16), 16)
                    cells = mantissa[layer, where, col * LANES : (col + 1) * LANES]
                    plain[layer, col, where, :] = cells.astype(F32) * scale

        copy(layer).start()
        pack(layer)

    for layer in range(depth):
        copy(layer).wait()


def sum_kernel(sides, *refs):
    count = len(sides)
    plain, from_below, from_above = refs[:3]
    from_g, d_below, d_above = refs[3 : 3 + count], refs[3 + count : 3 + 2 * count], refs[3 + 2 * count : 3 + 3 * count]
    own, other, total, t_edge, sems = refs[3 + 3 * count :]
    depth = plain.shape[0]
    core = lax.axis_index("ta")
    lane = lane_ids()
    low = lane < 64
    half = SUM_ROWS // 2
    centre = (lane >= 64 - WIDE) & (lane < 64 + WIDE)

    def copies(side, out, index):
        row = pl.multiple_of(side * (SUM_ROWS - HALF_ROWS), 8)
        made = [
            pltpu.make_async_copy(
                total.at[:, col, pl.ds(row, HALF_ROWS), :],
                out.at[:, pl.ds(col * HALF_ROWS, HALF_ROWS), :],
                sems.at[index, col],
            )
            for col in range(3)
        ]
        made.append(pltpu.make_async_copy(t_edge.at[side], out.at[:, pl.ds(3 * HALF_ROWS, 16), :], sems.at[index, 3]))
        return made

    @pl.loop(0, depth)
    def _(layer):
        for j in range(SUM_ROWS // 8):
            row, where = RIM - 8 + 8 * j, pl.ds(8 * j, 8)
            left, right = plain[layer, 0, row : row + 8, :], plain[layer, 2, row : row + 8, :]
            total[layer, 0, where, :] = plain[layer, 1, row : row + 8, :]
            total[layer, 1, where, :] = jnp.where(low, right, left)
            total[layer, 2, where, :] = jnp.where(centre, jnp.where(low, left, right), 0.0)

        def add(col, row, value):
            total[layer, col, row : row + 8, :] = total[layer, col, row : row + 8, :] + value

        for edge, ref in ((0, from_above), (SUM_ROWS - EDGE, from_below)):
            extra = ref[layer, 2 * EDGE : 2 * EDGE + 8, :]
            for j in range(9):
                add(0, edge + 8 * j, ref[layer, 8 * j : 8 * j + 8, :])
                add(1, edge + 8 * j, ref[layer, EDGE + 8 * j : EDGE + 8 * j + 8, :])
                add(2, edge + 8 * j, jnp.where(centre, turn(extra, 64 - WIDE - 2 * WIDE * j), 0.0))
        t_edge[0, layer, :, :] = from_above[layer, 2 * EDGE + 8 :, :]
        t_edge[1, layer, :, :] = from_below[layer, 2 * EDGE + 8 :, :]

        def side(right, _, g_ref, below_ref, above_ref):
            main = low if right else jnp.logical_not(low)
            at, t_at = (64, 0) if right else (64 - WIDE, LANES - WIDE)

            def window(value, source, target):
                return jnp.where((lane >= target) & (lane < target + WIDE), turn(value, target - source), 0.0)

            for j in range(17):
                value = g_ref[layer, 8 * j : 8 * j + 8, :]
                add(1, 8 * j, jnp.where(main, value, 0.0))
                add(1, half + 8 * j, jnp.where(main, turn(value, 64), 0.0))
            extras = [g_ref[layer, half + 8 * j : half + 8 * j + 8, :] for j in range(4)]
            for j in range(34):
                value = window(extras[j // SLOTS], WIDE * (j % SLOTS), at)
                if 1 <= j <= 32:
                    k = j - 1
                    value = value + window(extras[2 + k // SLOTS], WIDE * (k % SLOTS), t_at)
                add(2, 8 * j, value)
            for edge, ref, t_row in ((0, above_ref, 0), (SUM_ROWS - EDGE, below_ref, SUM_ROWS - 8)):
                extra = ref[layer, 32:40, :]
                start = 64 if right else 0
                for j in range(9):
                    value = ref[layer, 8 * (j % 5) : 8 * (j % 5) + 8, :]
                    if j > 4:
                        value = turn(value, 64)
                    add(1, edge + 8 * j, jnp.where(main, value, 0.0))
                    add(2, edge + 8 * j, window(extra, start + WIDE * j, at))
                add(2, t_row, window(extra, start + 9 * WIDE, t_at))

        by_side(sides, side, from_g, d_below, d_above)

    made = copies(1 - core, other, 0) + copies(core, own, 1)
    for one in made:
        one.start()
    for one in made:
        one.wait()


def heat_kernel(own, other, out):
    depth = own.shape[0]
    core = lax.axis_index("ta")
    low = lane_ids() < 64

    def move(src, first):
        @pl.loop(0, depth)
        def _(layer):
            for j in range(16):
                one = turn(src[layer, 8 + 8 * j : 16 + 8 * j, :], 64)
                two = turn(src[layer, HALF_ROWS + 8 + 8 * j : HALF_ROWS + 16 + 8 * j, :], 64)
                out[layer, rows8(first + 8 * j), :LANES] = jnp.where(low, two, one)
                out[layer, rows8(first + 8 * j), LANES:] = jnp.where(low, one, two)

    move(own, core * 128)
    move(other, 128 - core * 128)


def permutation(inverse=False, shift=0):
    rows = lax.broadcasted_iota(jnp.int32, (256, 256), 0)
    cols = lax.broadcasted_iota(jnp.int32, (256, 256), 1)
    if inverse:
        rows, cols = cols, rows
    return jnp.where((rows + shift) % 256 == 4 * (cols % 64) + cols // 64, 1.0, 0.0).astype(jnp.bfloat16)


def permuted(value, matrix):
    parts = []
    for _ in range(3):
        part = value.astype(jnp.bfloat16)
        value = value - part.astype(F32)
        parts.append(part)
    moved = jnp.dot(jnp.concatenate(parts, axis=0), matrix, preferred_element_type=F32)
    high, middle, low = (moved[k * value.shape[0] : (k + 1) * value.shape[0]] for k in range(3))
    return high + (middle + low)


def to_groups(first, second):
    low = lane_ids() < 64
    out = []
    for half in range(2):
        one = first[:, half * LANES : (half + 1) * LANES]
        two = second[:, half * LANES : (half + 1) * LANES]
        out += [jnp.where(low, one, turn(two, 64)), jnp.where(low, turn(one, 64), two)]
    return out


def to_rows(parts):
    low = lane_ids() < 64
    one, two = [], []
    for half in range(2):
        left, right = parts[2 * half], parts[2 * half + 1]
        one.append(jnp.where(low, left, turn(right, 64)))
        two.append(jnp.where(low, turn(left, 64), right))
    return jnp.concatenate(one, axis=1), jnp.concatenate(two, axis=1)


def group_cells(load, dst, matrix):
    @pl.loop(0, STEP_ROWS // BLOCK)
    def _(block):
        rows = [group * STEP_ROWS + block * BLOCK + step for group in range(2) for step in range(BLOCK)]
        halves = [jnp.concatenate([load(row, half) for row in rows], axis=0) for half in range(2)]
        value = permuted(jnp.concatenate(halves, axis=1), matrix)
        for step in range(BLOCK):
            parts = to_groups(*(value[8 * at : 8 * at + 8] for at in (step, BLOCK + step)))
            for col in range(4):
                dst[rows8((block * BLOCK + step + 1) * 40 + 8 * col), :] = parts[col]


def stack_kernel(t_own, t_other, now, t_cells, t_sems):
    core = lax.axis_index("ta")
    depth, rows, _ = t_own.shape
    layers = 2 * depth
    copies = []
    for which, t_src in enumerate((t_own, t_other)):
        base = core * depth if which == 0 else (1 - core) * depth
        for layer in range(depth):
            for col in range(2):
                copies.append(
                    pltpu.make_async_copy(
                        t_src.at[layer, :, col * LANES : (col + 1) * LANES],
                        t_cells.at[col, base + layer, pl.ds(8, rows), :],
                        t_sems.at[which, layer, col],
                    )
                )
    for copy in copies:
        copy.start()
    zero = jnp.zeros((8, LANES), F32)
    for col in range(2):
        for layer in range(layers):
            t_cells[col, layer, 0:8, :] = zero
            t_cells[col, layer, rows + 8 : rows + 16, :] = zero

    @pl.loop(0, STEP_ROWS + 2)
    def _(step):
        now[rows8(step * 40 + 32), :] = zero

    for copy in copies:
        copy.wait()
    flat = t_cells.reshape(2, layers * (rows + 16), LANES)
    first = 2 + core * 128

    def load(row, half):
        return flat[half, pl.ds(first + row, layers, stride=rows + 16), :]

    group_cells(load, now, permutation())


def solve_kernel(bounds, own, other, now_in, flow, material, conductivity, t_out, sent, *refs):
    cells, rows_t, heat, now, later, cond, f_down, f_right, f_above, inverse, base, t_stage, in_sems, sems = refs
    core = lax.axis_index("ta")
    gx, gy = lax.axis_index("gx"), lax.axis_index("gy")
    lane = lane_ids()
    level = lax.broadcasted_iota(jnp.int32, (8, LANES), 0)
    low = lane < 64
    layers = 8
    depth = layers // 2

    def at(step, col):
        return rows8(step * 40 + 8 * col)

    incoming = [
        pltpu.make_async_copy(src, cells.at[pl.ds(first, depth)], in_sems.at[which])
        for which, (src, first) in enumerate(((own, core * depth), (other, (1 - core) * depth)))
    ]
    for copy in incoming:
        copy.start()
    for copy in incoming:
        copy.wait()
    flat = cells.reshape(layers * SWAP, LANES)

    def across(row):
        return flat[pl.ds(row, layers, stride=SWAP), :]

    def to_stage(stage, src):
        @pl.loop(0, 16)
        def _(tile):
            for layer in range(layers):
                for col in range(2):
                    value = src[col, pl.ds((6 + 8 * tile) * 8 + layer, 8, stride=8), :]
                    stage[layer, rows8(8 * tile), col * LANES : (col + 1) * LANES] = value

    def outputs():
        mine = t_stage.at[pl.ds(core * depth, depth)]
        theirs = t_stage.at[pl.ds((1 - core) * depth, depth)]
        half = t_stage.shape[1]
        place = pl.ds(pl.multiple_of(core * half, half), half)
        return (
            pltpu.make_async_copy(theirs, sent, sems.at[0]),
            pltpu.make_async_copy(mine, t_out.at[:, place, :], sems.at[1]),
        )

    group_cells(lambda row, half: across(half * HALF_ROWS + 2 + row), heat, permutation(shift=64))
    t_edge = jnp.concatenate(
        [
            jnp.concatenate([across(3 * HALF_ROWS + 8 * col + i) for i in range(8)], axis=0)
            for col in range(2)
        ],
        axis=1,
    )
    t_edge = permuted(t_edge, permutation())
    halo_lanes = (lane < WIDE) | ((lane >= 64 - WIDE) & (lane < 64 + WIDE)) | (lane >= LANES - WIDE)

    @pl.loop(0, STEP_ROWS // 5)
    def _(block):
        for part in range(5):
            step = block * 5 + part
            first, second = across(2 * HALF_ROWS + 2 + step), across(2 * HALF_ROWS + 2 + step + STEP_ROWS)
            first_turned, second_turned = turn(first, 64), turn(second, 64)
            upper_lanes = jnp.where(lane < 64 + WIDE, first, first_turned)
            lower_lanes = jnp.where(lane < WIDE, second_turned, second)
            heat[at(step + 1, 4), :] = jnp.where(halo_lanes, jnp.where(low, lower_lanes, upper_lanes), 0.0)
            upper_lanes = jnp.where(lane < 64 + WIDE, first_turned, first)
            lower_lanes = jnp.where(lane < WIDE, second, second_turned)
            now[at(step + 1, 4), :] = jnp.where(halo_lanes, jnp.where(low, lower_lanes, upper_lanes), 0.0)
            for col in range(4):
                now[at(step + 1, col), :] = now_in[at(step + 1, col), :]

    @pl.when(core == 0)
    def _():
        for row in range(6):
            value = t_edge[8 * row + 16 : 8 * row + 24]
            parts = to_groups(value, value)
            for col in range(4):
                now[at(row + 1, col), :] = jnp.where(low, parts[col], now[at(row + 1, col), :])

    @pl.when(core == 1)
    def _():
        for row in range(6):
            value = t_edge[8 * row : 8 * row + 8]
            parts = to_groups(value, value)
            for col in range(4):
                now[at(row + 65, col), :] = jnp.where(low, now[at(row + 65, col), :], parts[col])

    def ghosts(ref):
        for col in range(5):
            ref[at(0, col), :] = turn(ref[at(STEP_ROWS, col), :], 64)
            ref[at(STEP_ROWS + 1, col), :] = turn(ref[at(1, col), :], 64)

    last = (lane == 63) | (lane == 127)
    first = (lane == 0) | (lane == 64)

    def to_right(values):
        inner, outer = turn(values[0], -1), turn(values[4], -1)
        return values[1:4] + [jnp.where(last, outer, inner), jnp.where(last, inner, outer)]

    def to_left(values):
        inner, outer = turn(values[3], 1), turn(values[4], 1)
        return [jnp.where(first, outer, inner)] + values[:3] + [jnp.where(first, inner, outer)]

    def upper(value):
        return pltpu.roll(value, 7, 0)

    def lower(value):
        return pltpu.roll(value, 1, 0)

    has_right = (gy + 1) * 256 < bounds[1]
    half_lane = jnp.where(low, lane, lane - 64)
    keep = ((half_lane < WIDE) & has_right) | ((half_lane >= 64 - WIDE) & (gy > 0))
    halo_mask = jnp.where(keep, 1.0, 0.0)
    scale = jnp.full((8, LANES), conductivity[material[0]], F32)
    for layer in range(1, layers):
        scale = jnp.where(level == layer, conductivity[material[layer]], scale)
    not_top = jnp.where(level < layers - 1, 1.0, 0.0)
    not_bottom = jnp.where(level > 0, 1.0, 0.0)
    flows = [flow[8 * col : 8 * col + 8, :] for col in range(5)]
    first_row = gx * 256 + core * 128 - 6

    def masks(step):
        ones = []
        for group in range(2):
            row = first_row + step + group * STEP_ROWS
            ones.append(jnp.where((row >= 0) & (row < bounds[0]), 1.0, 0.0))
        inner = jnp.where(low, ones[0], ones[1])
        return [inner] * 4 + [jnp.where(low, ones[1], ones[0]) * halo_mask]

    def conductances(src):
        @pl.loop(0, STEP_ROWS // 5)
        def _(block):
            for part in range(5):
                step = block * 5 + part
                mask = masks(step)
                for col in range(5):
                    where = at(step + 1, col)
                    cond[where, :] = (scale * mask[col]) * (1.0 + 0.5 * jnp.tanh(src[where, :]))

        ghosts(cond)

    def coefficients(src):
        @pl.loop(0, STEP_ROWS // 5)
        def _(block):
            start = block * 5
            lines = [[cond[at(start + part, col), :] for col in range(5)] for part in range(7)]
            for part in range(5):
                up, here, down = lines[part], lines[part + 1], lines[part + 2]
                mask = masks(start + part)
                rights, lefts = to_right(here), to_left(here)
                for col in range(5):
                    where = at(start + part + 1, col)
                    centre = here[col]
                    over = centre + upper(centre) * not_top
                    under = centre + lower(centre) * not_bottom
                    face_down = 0.5 * (centre + down[col])
                    face_right = 0.5 * (centre + rights[col])
                    total = (1.0 + flows[col]) + 0.5 * (centre + up[col]) + face_down
                    total = total + face_right + 0.5 * (centre + lefts[col]) + over + under
                    f_down[where, :] = face_down
                    f_right[where, :] = face_right
                    f_above[where, :] = over * not_top
                    inverse[where, :] = mask[col] / total
                    base[where, :] = src[where, :] + heat[where, :]

        for col in range(5):
            f_down[at(0, col), :] = 0.5 * (cond[at(0, col), :] + cond[at(1, col), :])

    def sweep(src, dst):
        @pl.loop(0, STEP_ROWS // SPAN)
        def _(block):
            start = block * SPAN
            lines = [[src[at(start + part, col), :] for col in range(5)] for part in range(SPAN + 2)]
            faces = [[f_down[at(start + part, col), :] for col in range(5)] for part in range(SPAN + 1)]
            for part in range(SPAN):
                up, here, down = lines[part], lines[part + 1], lines[part + 2]
                face_right = [f_right[at(start + part + 1, col), :] for col in range(5)]
                rights = to_right(here)
                lefts = to_left([face * value for face, value in zip(face_right, here)])
                for col in range(5):
                    where = at(start + part + 1, col)
                    face_above = f_above[where, :]
                    total = base[where, :] + (faces[part][col] + flows[col]) * up[col]
                    total = total + faces[part + 1][col] * down[col]
                    total = total + (face_right[col] * rights[col] + lefts[col])
                    total = total + (face_above * upper(here[col]) + lower(face_above * here[col]))
                    dst[where, :] = total * inverse[where, :]

        ghosts(dst)

    ghosts(now)
    for _ in range(STEPS):
        conductances(now)
        coefficients(now)
        for _ in range(SWEEPS):
            sweep(now, later)
            now, later = later, now

    back = permutation(inverse=True)

    @pl.loop(0, STEP_ROWS // BLOCK)
    def _(block):
        pairs = [
            to_rows([now[at(block * BLOCK + part + 1, col), :] for col in range(4)]) for part in range(BLOCK)
        ]
        value = jnp.concatenate([pair[group] for group in range(2) for pair in pairs], axis=0)
        value = permuted(value, back)
        for group in range(2):
            where = pl.ds(pl.multiple_of((group * STEP_ROWS + block * BLOCK) * 8, 8), BLOCK * 8)
            for col in range(2):
                part = value[group * BLOCK * 8 : (group + 1) * BLOCK * 8, col * LANES : (col + 1) * LANES]
                rows_t[col, where, :] = part

    to_stage(t_stage, rows_t)
    for copy in outputs():
        copy.start()
    for copy in outputs():
        copy.wait()


def place_kernel(received, t_in, t_out, sem):
    core = lax.axis_index("ta")
    half = received.shape[1]
    place = pl.ds(pl.multiple_of((1 - core) * half, half), half)
    copy = pltpu.make_async_copy(received, t_out.at[:, place, :], sem)
    copy.start()
    copy.wait()


def on_device(t_initial, power_mantissa, tile_exponent, channel_mask, material, conductivity):
    depth, rows, cols = t_initial.shape
    layers = 2 * depth
    n_gx, n_gy = lax.axis_size("gx"), lax.axis_size("gy")
    array = jax.ShapeDtypeStruct
    swap = [(0, 1), (1, 0)]
    out_sides = [None] if n_gy == 2 else [True, False]
    in_sides = [None] if n_gy == 2 else [False, True]
    count = len(out_sides)

    t_other = lax.ppermute(t_initial, "ta", swap)
    plain_shape = array((depth, 3, rows + 2 * RIM, LANES), F32)
    along = array((depth, ROWS_P, LANES), F32)
    across = (array((depth, ROWS_G, LANES), F32),) * count
    corner = (array((depth, ROWS_D, LANES), F32),) * (2 * count)
    sent = pl.pallas_call(
        functools.partial(send_kernel, out_sides),
        out_shape=(plain_shape, along, along) + across + corner,
        in_specs=[VMEM, SMEM, VMEM],
        out_specs=(ANY,) + (VMEM,) * (2 + 3 * count),
        scratch_shapes=[pltpu.VMEM(plain_shape.shape, F32), pltpu.SemaphoreType.DMA((depth,))],
        compiler_params=params(12),
        name="send",
    )(power_mantissa, tile_exponent.transpose(1, 0, 2), t_initial)
    plain, up, down = sent[:3]
    to_g, to_d_up, to_d_down = sent[3 : 3 + count], sent[3 + count : 3 + 2 * count], sent[3 + 2 * count :]

    def move(value, step_z, step_x):
        pairs = []
        for z in range(n_gx):
            for x in range(n_gy):
                to_z, to_x = z + step_z, x ^ 1 if step_x is None else x + step_x
                if 0 <= to_z < n_gx and 0 <= to_x < n_gy:
                    pairs.append((z * n_gy + x, to_z * n_gy + to_x))
        return lax.ppermute(value, ("gx", "gy"), pairs)

    steps = [None] if n_gy == 2 else [1, -1]
    from_g = [move(value, 0, step) for value, step in zip(to_g, steps)]
    from_above = move(down, 1, 0)
    from_below = move(up, -1, 0)
    d_above = [move(value, 1, step) for value, step in zip(to_d_down, steps)]
    d_below = [move(value, -1, step) for value, step in zip(to_d_up, steps)]

    wide = jnp.pad(channel_mask, ((0, 0), (RIM, RIM)))
    mask = lax.dynamic_slice_in_dim(wide, lax.axis_index("gy") * cols, cols + 2 * RIM, 1).astype(F32) * COOLANT
    inner = mask[:, RIM : RIM + cols].reshape(layers, 64, 4).transpose(2, 0, 1)
    outer = jnp.zeros((layers, 64 - 2 * WIDE), F32)
    outer = jnp.concatenate([mask[:, RIM + cols :][:, :WIDE], outer, mask[:, RIM - WIDE : RIM]], axis=1)
    flow = jnp.concatenate([inner, outer[None]], axis=0).reshape(layers * 5, 64)
    flow = jnp.concatenate([flow, flow], axis=1)

    grouped = array(((STEP_ROWS + 2) * 40, LANES), F32)
    now = pl.pallas_call(
        stack_kernel,
        out_shape=grouped,
        in_specs=[ANY] * 2,
        out_specs=VMEM,
        scratch_shapes=[
            pltpu.VMEM((2, layers, rows + 16, LANES), F32),
            pltpu.SemaphoreType.DMA((2, depth, 2)),
        ],
        compiler_params=params(24),
        name="stack",
    )(t_initial, t_other)

    half = array((depth, SWAP, LANES), F32)
    own, other = pl.pallas_call(
        functools.partial(sum_kernel, in_sides),
        out_shape=(half, half),
        in_specs=[VMEM] * (3 + 3 * count),
        out_specs=(ANY, ANY),
        scratch_shapes=[
            pltpu.VMEM((depth, 3, SUM_ROWS, LANES), F32),
            pltpu.VMEM((2, depth, 16, LANES), F32),
            pltpu.SemaphoreType.DMA((2, 4)),
        ],
        compiler_params=params(12),
        name="sum",
    )(plain, from_below, from_above, *from_g, *d_below, *d_above)
    received = lax.ppermute(other, "ta", swap)
    whole = array((depth, rows, cols), F32)
    heat_source = pl.pallas_call(
        heat_kernel,
        out_shape=whole,
        in_specs=[VMEM] * 2,
        out_specs=VMEM,
        compiler_params=params(8),
        name="heat",
    )(own, other)

    work = pltpu.VMEM(grouped.shape, F32)
    t_part, sent = pl.pallas_call(
        functools.partial(solve_kernel, (n_gx * rows, n_gy * cols)),
        out_shape=(whole, array((depth, rows // 2, cols), F32)),
        in_specs=[ANY, ANY] + [VMEM] * 2 + [SMEM, SMEM],
        out_specs=(ANY, ANY),
        scratch_shapes=[
            pltpu.VMEM((layers, SWAP, LANES), F32),
            pltpu.VMEM((2, REGION * 8, LANES), F32),
        ]
        + [work] * 9
        + [
            pltpu.VMEM((layers, rows // 2, cols), F32),
            pltpu.SemaphoreType.DMA((2,)),
            pltpu.SemaphoreType.DMA((2,)),
        ],
        compiler_params=params(44),
        name="solve",
    )(own, received, now, flow, material, conductivity)
    received = lax.ppermute(sent, "ta", swap)
    temperature = pl.pallas_call(
        place_kernel,
        out_shape=whole,
        in_specs=[ANY, ANY],
        out_specs=ANY,
        scratch_shapes=[pltpu.SemaphoreType.DMA],
        input_output_aliases={1: 0},
        compiler_params=params(4),
        name="place",
    )(received, t_part)
    return temperature, heat_source


def solution(mesh):
    cells = P("ta", ("group", "gx"), "gy")
    return jax.shard_map(
        on_device,
        mesh=mesh,
        in_specs=(cells, cells, cells, P(), P(), P()),
        out_specs=(cells, cells),
        check_vma=False,
    )
```

time: 67.3 us -> 56.8 us (0.84)
  Pallas kernels: 45.1 us -> 30.2 us
  starting transfers between devices: 7.99 us -> 15.5 us
  local copies, waits for them, and re-layouts: 5.29 us -> 2.41 us
    pallas_call x5 -> x6, Pallas kernels: 45.1 us -> 30.2 us  [the longest x1 20.1 us: on_device(): pl.pallas_call(functools.partial(solve_kernel, (n_gx * rows, n_gy * cols)...]
    ppermute x4 -> x6, waiting for transfers between devices: 0.08 us -> 7.26 us  [the longest x5 7.25 us: move(): return lax.ppermute(value, ('gx', 'gy'), pairs)]
    ppermute x4 -> x6, starting transfers between devices: 7.76 us -> 13.5 us  [the longest x5 10.5 us: move(): return lax.ppermute(value, ('gx', 'gy'), pairs)]
    ppermute x1, waiting for transfers between devices: 4.31 us -> 0.01 us  [on_device(): t_other = lax.ppermute(t_initial, 'ta', swap)]
    unnamed x19 -> x10, local copies, waits for them, and re-layouts: 4.86 us -> 1.98 us
    ppermute x1, waiting for transfers between devices: 2.58 us -> 0.11 us  [on_device(): received = lax.ppermute(sent, 'ta', swap)]
    ppermute x1, starting transfers between devices: 0.08 us -> 1.86 us  [on_device(): t_other = lax.ppermute(t_initial, 'ta', swap)]
  transfers between devices with their start and end apart: 6 -> 8, of which waited for: 3 -> 3; matrix products, arithmetic and copies ran while one was open for 1% -> 1% of each run, Pallas kernels for 14% -> 10%
where the time goes in v4:
time: 56.8 us; the launch traced here: 56.4 us
  Pallas kernels  30.2 us (53%)
  starting transfers between devices  15.5 us (27%)
  waiting for transfers between devices  7.37 us (13%)
  local copies, waits for them, and re-layouts  2.41 us (4%)
  between operations  0.77 us (1%)
    pallas_call x1, Pallas kernels, on_device(): pl.pallas_call(functools.partial(solve_kernel, (n_gx * rows, n_gy * cols)...  20.1 us
    ppermute x5, starting transfers between devices, move(): return lax.ppermute(value, ('gx', 'gy'), pairs)  10.5 us
    ppermute x5, waiting for transfers between devices, move(): return lax.ppermute(value, ('gx', 'gy'), pairs)  7.25 us
    pallas_call x1, Pallas kernels, on_device(): pl.pallas_call(functools.partial(send_kernel, out_sides), out_shape=(plai...  3.44 us
    ppermute x1, starting transfers between devices, on_device(): received = lax.ppermute(other, 'ta', swap)  3.01 us
    pallas_call x1, Pallas kernels, on_device(): pl.pallas_call(stack_kernel, out_shape=grouped, in_specs=[ANY] * 2, out_s...  2.72 us
    unnamed x10, local copies, waits for them, and re-layouts  1.98 us
    ppermute x1, starting transfers between devices, on_device(): t_other = lax.ppermute(t_initial, 'ta', swap)  1.86 us
  transfers between devices with their start and end apart: 8, of which 3 were waited for; matrix products, arithmetic and copies ran while one was open for 1% of the time, Pallas kernels for 10%

profile of v4, /device:TPU:21, one launch (start us, length us, event | category | flops | bytes accessed | tf_op | source)
XLA Modules:
  0.0 56.4 jit_solution(12303269439449888353)
XLA Ops:
  0.6 0.0 copy-start
  0.6 1.3 %copy-done = bf16[4,384,384]{2,1,0:T(8,128)(2,1)S(1)} copy-done((bf16[4,384,384]{2,1,0:T(8,128)(2,1)S(1)}, bf16[4,384,384]{2,1,0:T(8,128)(2,1)}, u32[]{:S(2)}) %copy-start) | copy-done | bytes 1179672
  1.9 0.0 copy-start.1
  1.9 0.7 %copy-done.1 = s32[4,6,6]{2,0,1:T(4,128)S(1)} copy-done((s32[4,6,6]{2,0,1:T(4,128)S(1)}, s32[4,6,6]{2,0,1:T(4,128)}, u32[]{:S(2)}) %copy-start.1) | copy-done | bytes 600
  2.6 3.4 %send.1 = (f32[4,3,384,128]{3,2,1,0:T(8,128)S(1)}, f32[4,168,128]{2,1,0:T(8,128)S(1)}, f32[4,168,128]{2,1,0:T(8,128)S(1)}, f32[4,168,128]{2,1,0:T(8,128)S(1)}, f...) custom-call(bf16[4,384,384]{2,1,0:T(8,128)(2,1)S(1)} %copy-done, s32[6,4,6]{2,1,0:T(4,128)S(1)} %bitcast.8, ...), custom_call_target="tpu_custom_call" | custom-call | tf_op jit(solution)/shard_map/send/pallas_call | solution.py:588
  6.1 2.1 %collective-permute-start = (f32[4,168,128]{2,1,0:T(8,128)S(1)}, f32[4,168,128]{2,1,0:T(8,128)S(1)}, u32[]{:S(2)}, u32[]{:S(2)}) collective-permute-start(f32[4,168,128]{2,1,0:T(8,128)S(1)} %get-tuple-element.13), channel_id=1, source_target_pairs={{4,0},{6,2},{8,4},{10,6},{12,8},{14,10},{5,1},{7,3},{9,5},{11,7},{... | collective-permute-start | bytes 1032200 | tf_op jit(solution)/shard_map/ppermute | solution.py:607
  8.1 3.2 %collective-permute-start.1 = (f32[4,168,128]{2,1,0:T(8,128)S(1)}, f32[4,168,128]{2,1,0:T(8,128)S(1)}, u32[]{:S(2)}, u32[]{:S(2)}) collective-permute-start(f32[4,168,128]{2,1,0:T(8,128)S(1)} %get-tuple-element.14), channel_id=1, source_target_pairs={{0,4},{2,6},{4,8},{6,10},{8,12},{10,14},{1,5},{3,7},{5,9},{7,11},{... | collective-permute-start | bytes 1032200 | tf_op jit(solution)/shard_map/ppermute | solution.py:607
  11.4 1.3 %collective-permute-start.2 = (f32[4,168,128]{2,1,0:T(8,128)S(1)}, f32[4,168,128]{2,1,0:T(8,128)S(1)}, u32[]{:S(2)}, u32[]{:S(2)}) collective-permute-start(f32[4,168,128]{2,1,0:T(8,128)S(1)} %get-tuple-element.15), channel_id=1, source_target_pairs={{0,2},{2,0},{4,6},{6,4},{8,10},{10,8},{12,14},{14,12},{1,3},{3,1},... | collective-permute-start | bytes 1032200 | tf_op jit(solution)/shard_map/ppermute | solution.py:607
  12.6 2.0 %collective-permute-start.3 = (f32[4,40,128]{2,1,0:T(8,128)S(1)}, f32[4,40,128]{2,1,0:T(8,128)S(1)}, u32[]{:S(2)}, u32[]{:S(2)}) collective-permute-start(f32[4,40,128]{2,1,0:T(8,128)S(1)} %get-tuple-element.16), channel_id=1, source_target_pairs={{4,2},{6,0},{8,6},{10,4},{12,10},{14,8},{5,3},{7,1},{9,7},{11,5},{... | collective-permute-start | bytes 245768 | tf_op jit(solution)/shard_map/ppermute | solution.py:607
  14.7 1.9 %collective-permute-start.6 = (f32[4,256,256]{2,1,0:T(8,128)}, f32[4,256,256]{2,1,0:T(8,128)S(1)}, u32[]{:S(2)}, u32[]{:S(2)}) collective-permute-start(f32[4,256,256]{2,1,0:T(8,128)} %t_own.1), channel_id=1, source_target_pairs={{0,1},{1,0},{2,3},{3,2},{4,5},{5,4},{6,7},{7,6},{8,9},{9,8},{10,11... | collective-permute-start | bytes 3145736 | tf_op jit(solution)/shard_map/ppermute | solution.py:583
  16.5 3.1 %collective-permute-done.3.refs_4_ = f32[4,40,128]{2,1,0:T(8,128)S(1)} collective-permute-done((f32[4,40,128]{2,1,0:T(8,128)S(1)}, f32[4,40,128]{2,1,0:T(8,128)S(1)}, u32[]{:S(2)}, u32[]{:S(2)}) %collective-permute-start.3) | collective-permute-done | bytes 81952 | tf_op jit(solution)/shard_map/ppermute | solution.py:607
  19.6 1.9 %collective-permute-start.4 = (f32[4,40,128]{2,1,0:T(8,128)S(1)}, f32[4,40,128]{2,1,0:T(8,128)S(1)}, u32[]{:S(2)}, u32[]{:S(2)}) collective-permute-start(f32[4,40,128]{2,1,0:T(8,128)S(1)} %get-tuple-element.17), channel_id=1, source_target_pairs={{0,6},{2,4},{4,10},{6,8},{8,14},{10,12},{1,7},{3,5},{5,11},{7,9},{... | collective-permute-start | bytes 245768 | tf_op jit(solution)/shard_map/ppermute | solution.py:607
  21.5 4.2 %collective-permute-done.4.refs_5_ = f32[4,40,128]{2,1,0:T(8,128)S(1)} collective-permute-done((f32[4,40,128]{2,1,0:T(8,128)S(1)}, f32[4,40,128]{2,1,0:T(8,128)S(1)}, u32[]{:S(2)}, u32[]{:S(2)}) %collective-permute-start.4) | collective-permute-done | bytes 81952 | tf_op jit(solution)/shard_map/ppermute | solution.py:607
  25.7 0.0 collective-permute-done.refs_1_
  25.7 0.0 collective-permute-done.1.refs_2_
  25.7 0.0 collective-permute-done.2.refs_3_
  25.7 0.0 copy-start.4
  25.7 1.4 %sum.1 = (f32[4,448,128]{2,1,0:T(8,128)S(1)}, f32[4,448,128]{2,1,0:T(8,128)S(1)}) custom-call(f32[4,3,384,128]{3,2,1,0:T(8,128)S(1)} %get-tuple-element.12.refs_0_, f32[4,168,128]{2,1,0:T(8,128)S(1)} %collective-permute-done.refs_1_, f32[4,168,128]{2,1,0:T(8,128)S(1)} %collective-permute-done.1.refs_2_, f32[4,168,128]{2,1,0:T(8,128)S(1)} %collective-permute-done.2.refs_3_, ...), custom_call_target="tpu_custom_call" | custom-call | tf_op jit(solution)/shard_map/sum/pallas_call | solution.py:639
  27.1 3.0 %collective-permute-start.5 = (f32[4,448,128]{2,1,0:T(8,128)S(1)}, f32[4,448,128]{2,1,0:T(8,128)}, u32[]{:S(2)}, u32[]{:S(2)}) collective-permute-start(f32[4,448,128]{2,1,0:T(8,128)S(1)} %get-tuple-element.19.other), channel_id=1, source_target_pairs={{0,1},{1,0},{2,3},{3,2},{4,5},{5,4},{6,7},{7,6},{8,9},{9,8},{10,11... | collective-permute-start | bytes 2752520 | tf_op jit(solution)/shard_map/ppermute | solution.py:652
  30.1 0.0 copy-done.4
  30.1 0.1 fusion.1
  30.2 0.1 slice.14
  30.3 0.1 copy.12
  30.4 0.1 copy.13
  30.5 0.1 pad.10.clone
  30.6 0.1 fusion.2
  30.6 0.1 maximum_bitcast_fusion.1
  30.7 0.1 pad_maximum_fusion.flow
  30.8 0.0 copy-start.2
  30.8 0.0 copy-start.3
  30.8 0.0 collective-permute-done.6.t_other
  30.8 2.7 %stack.1.now_in = f32[2880,128]{1,0:T(8,128)S(1)} custom-call(f32[4,256,256]{2,1,0:T(8,128)} %t_own.1, f32[4,256,256]{2,1,0:T(8,128)S(1)} %collective-permute-done.6.t_other), custom_call_target="tpu_custom_call" | custom-call | tf_op jit(solution)/shard_map/stack/pallas_call | solution.py:625
  33.6 0.0 collective-permute-done.5.other
  33.6 0.0 copy-done.2
  33.6 0.0 copy-done.3
  33.6 20.1 %solve.1 = (f32[4,256,256]{2,1,0:T(8,128)}, f32[4,128,256]{2,1,0:T(8,128)S(1)}) custom-call(f32[4,448,128]{2,1,0:T(8,128)S(1)} %get-tuple-element.18.own, f32[4,448,128]{2,1,0:T(8,128)} %collective-permute-done.5.other, f32[2880,128]{1,0:T(8,128)S(1)} %stack.1.now_in, f32[40,128]{1,0:T(8,128)S(1)} %pad_maximum_fusion.flow, s32[8]{0:T(128)S(1)} %copy-done.2, ...), custom_call_target="tpu_custom_call" | custom-call | tf_op jit(solution)/shard_map/solve/pallas_call | solution.py:664
  53.7 0.1 collective-permute-start.7
  53.8 1.8 %heat.1 = f32[4,256,256]{2,1,0:T(8,128)} custom-call(f32[4,448,128]{2,1,0:T(8,128)S(1)} %get-tuple-element.18.own, f32[4,448,128]{2,1,0:T(8,128)S(1)} %get-tuple-element.19.other), custom_call_target="tpu_custom_call" | custom-call | tf_op jit(solution)/shard_map/heat/pallas_call | solution.py:654
  55.5 0.1 collective-permute-done.7.received
  55.6 0.8 %place.1 = f32[4,256,256]{2,1,0:T(8,128)} custom-call(f32[4,128,256]{2,1,0:T(8,128)S(1)} %collective-permute-done.7.received, f32[4,256,256]{2,1,0:T(8,128)} %get-tuple-element.21.t_in), custom_call_target="tpu_custom_call", output_to_operand_aliasing={{}: (1, {})} | custom-call | tf_op jit(solution)/shard_map/place/pallas_call | solution.py:683
  (2 shorter events, 0.0 us)
Async XLA Ops:
  0.6 1.3 %copy-start = (bf16[4,384,384]{2,1,0:T(8,128)(2,1)S(1)}, bf16[4,384,384]{2,1,0:T(8,128)(2,1)}, u32[]{:S(2)}) copy-start(bf16[4,384,384]{2,1,0:T(8,128)(2,1)} %mantissa.1) | copy-start | bytes 3538948
  1.9 0.7 %copy-start.1 = (s32[4,6,6]{2,0,1:T(4,128)S(1)}, s32[4,6,6]{2,0,1:T(4,128)}, u32[]{:S(2)}) copy-start(s32[4,6,6]{2,0,1:T(4,128)} %param.8) | copy-start | bytes 1732
  6.1 19.6 %collective-permute-start = (f32[4,168,128]{2,1,0:T(8,128)S(1)}, f32[4,168,128]{2,1,0:T(8,128)S(1)}, u32[]{:S(2)}, u32[]{:S(2)}) collective-permute-start(f32[4,168,128]{2,1,0:T(8,128)S(1)} %get-tuple-element.13), channel_id=1, source_target_pairs={{4,0},{6,2},{8,4},{10,6},{12,8},{14,10},{5,1},{7,3},{9,5},{11,7},{... | collective-permute-start | bytes 1032200 | tf_op jit(solution)/shard_map/ppermute | solution.py:607
  8.1 17.6 %collective-permute-start.1 = (f32[4,168,128]{2,1,0:T(8,128)S(1)}, f32[4,168,128]{2,1,0:T(8,128)S(1)}, u32[]{:S(2)}, u32[]{:S(2)}) collective-permute-start(f32[4,168,128]{2,1,0:T(8,128)S(1)} %get-tuple-element.14), channel_id=1, source_target_pairs={{0,4},{2,6},{4,8},{6,10},{8,12},{10,14},{1,5},{3,7},{5,9},{7,11},{... | collective-permute-start | bytes 1032200 | tf_op jit(solution)/shard_map/ppermute | solution.py:607
  11.4 14.3 %collective-permute-start.2 = (f32[4,168,128]{2,1,0:T(8,128)S(1)}, f32[4,168,128]{2,1,0:T(8,128)S(1)}, u32[]{:S(2)}, u32[]{:S(2)}) collective-permute-start(f32[4,168,128]{2,1,0:T(8,128)S(1)} %get-tuple-element.15), channel_id=1, source_target_pairs={{0,2},{2,0},{4,6},{6,4},{8,10},{10,8},{12,14},{14,12},{1,3},{3,1},... | collective-permute-start | bytes 1032200 | tf_op jit(solution)/shard_map/ppermute | solution.py:607
  12.6 7.0 %collective-permute-start.3 = (f32[4,40,128]{2,1,0:T(8,128)S(1)}, f32[4,40,128]{2,1,0:T(8,128)S(1)}, u32[]{:S(2)}, u32[]{:S(2)}) collective-permute-start(f32[4,40,128]{2,1,0:T(8,128)S(1)} %get-tuple-element.16), channel_id=1, source_target_pairs={{4,2},{6,0},{8,6},{10,4},{12,10},{14,8},{5,3},{7,1},{9,7},{11,5},{... | collective-permute-start | bytes 245768 | tf_op jit(solution)/shard_map/ppermute | solution.py:607
  14.7 16.1 %collective-permute-start.6 = (f32[4,256,256]{2,1,0:T(8,128)}, f32[4,256,256]{2,1,0:T(8,128)S(1)}, u32[]{:S(2)}, u32[]{:S(2)}) collective-permute-start(f32[4,256,256]{2,1,0:T(8,128)} %t_own.1), channel_id=1, source_target_pairs={{0,1},{1,0},{2,3},{3,2},{4,5},{5,4},{6,7},{7,6},{8,9},{9,8},{10,11... | collective-permute-start | bytes 3145736 | tf_op jit(solution)/shard_map/ppermute | solution.py:583
  19.6 6.1 %collective-permute-start.4 = (f32[4,40,128]{2,1,0:T(8,128)S(1)}, f32[4,40,128]{2,1,0:T(8,128)S(1)}, u32[]{:S(2)}, u32[]{:S(2)}) collective-permute-start(f32[4,40,128]{2,1,0:T(8,128)S(1)} %get-tuple-element.17), channel_id=1, source_target_pairs={{0,6},{2,4},{4,10},{6,8},{8,14},{10,12},{1,7},{3,5},{5,11},{7,9},{... | collective-permute-start | bytes 245768 | tf_op jit(solution)/shard_map/ppermute | solution.py:607
  25.7 4.4 %copy-start.4 = (s32[8,512]{1,0:T(8,128)S(1)}, s32[8,512]{1,0:T(8,128)}, u32[]{:S(2)}) copy-start(s32[8,512]{1,0:T(8,128)} %param.9) | copy-start | bytes 49156
  27.1 6.5 %collective-permute-start.5 = (f32[4,448,128]{2,1,0:T(8,128)S(1)}, f32[4,448,128]{2,1,0:T(8,128)}, u32[]{:S(2)}, u32[]{:S(2)}) collective-permute-start(f32[4,448,128]{2,1,0:T(8,128)S(1)} %get-tuple-element.19.other), channel_id=1, source_target_pairs={{0,1},{1,0},{2,3},{3,2},{4,5},{5,4},{6,7},{7,6},{8,9},{9,8},{10,11... | collective-permute-start | bytes 2752520 | tf_op jit(solution)/shard_map/ppermute | solution.py:652
  30.8 2.8 %copy-start.2 = (s32[8]{0:T(128)S(1)}, s32[8]{0:T(128)}, u32[]{:S(2)}) copy-start(s32[8]{0:T(128)} %material.1) | copy-start | bytes 100
  30.8 2.8 %copy-start.3 = (f32[4]{0:T(128)S(1)}, f32[4]{0:T(128)}, u32[]{:S(2)}) copy-start(f32[4]{0:T(128)} %conductivity.1) | copy-start | bytes 52
  53.7 2.0 %collective-permute-start.7 = (f32[4,128,256]{2,1,0:T(8,128)S(1)}, f32[4,128,256]{2,1,0:T(8,128)S(1)}, u32[]{:S(2)}, u32[]{:S(2)}) collective-permute-start(f32[4,128,256]{2,1,0:T(8,128)S(1)} %get-tuple-element.20), channel_id=1, source_target_pairs={{0,1},{1,0},{2,3},{3,2},{4,5},{5,4},{6,7},{7,6},{8,9},{9,8},{10,11... | collective-permute-start | bytes 1572872 | tf_op jit(solution)/shard_map/ppermute | solution.py:682

commit v5 on v4

--- a/solution.py
+++ b/solution.py
@@ -18,7 +18,7 @@
 REGION = 140
 STEP_ROWS = 70
 BLOCK = 35
-SPAN = 5
+SPAN = 35
 SUM_ROWS = 272
 HALF_ROWS = 144
 SWAP = 3 * HALF_ROWS + 16
@@ -31,6 +31,7 @@
 VMEM = pl.BlockSpec(memory_space=pltpu.VMEM)
 SMEM = pl.BlockSpec(memory_space=pltpu.SMEM)
 ANY = pl.BlockSpec(memory_space=pl.ANY)
+HBM = pl.BlockSpec(memory_space=pltpu.HBM)
 
 
 def params(megabytes):
@@ -61,11 +62,11 @@
             body(side, place, *rest)
 
 
-def send_kernel(sides, mantissa, exponent, t_ref, *refs):
+def send_kernel(sides, mantissa_in, exponent_in, t_in, *refs):
     count = len(sides)
-    whole, to_up, to_down = refs[:3]
-    to_g, to_d_up, to_d_down = refs[3 : 3 + count], refs[3 + count : 3 + 2 * count], refs[3 + 2 * count : 3 + 3 * count]
-    plain, sems = refs[3 + 3 * count :]
+    whole, to_first, to_second = refs[:3]
+    to_g, to_d_first, to_d_second = refs[3 : 3 + count], refs[3 + count : 3 + 2 * count], refs[3 + 2 * count : 3 + 3 * count]
+    plain, mantissa, exponent, t_ref, sems, in_sems, exponent_sem = refs[3 + 3 * count :]
     depth, rows, _ = mantissa.shape
     lane = lane_ids()
     low = lane < 64
@@ -75,17 +76,21 @@
         moved = turn(value, target - source)
         return jnp.where((lane >= target) & (lane < target + width), moved, total)
 
+    odd = lax.rem(lax.axis_index("gx"), 2)
+    edges = [which * (rows - EDGE) for which in (1 - odd, odd)]
+    t_edges = [which * (rows - 2 * RIM - 8) for which in (1 - odd, odd)]
+
     def copy(layer):
         return pltpu.make_async_copy(plain.at[layer], whole.at[layer], sems.at[layer])
 
     def pack(layer):
         def cells(col, row):
-            return plain[layer, col, row : row + 8, :]
+            return plain[layer, col, rows8(row), :]
 
         def t_cells(col, row):
-            return t_ref[layer, row : row + 8, col * LANES : (col + 1) * LANES]
-
-        for out, edge, t_edge in ((to_up, 0, 0), (to_down, rows - EDGE, rows - 2 * RIM - 8)):
+            return t_ref[layer, rows8(row), col * LANES : (col + 1) * LANES]
+
+        for out, edge, t_edge in ((to_first, edges[0], t_edges[0]), (to_second, edges[1], t_edges[1])):
             extra = jnp.zeros((8, LANES), F32)
             for j in range(9):
                 left, right = cells(0, edge + 8 * j), cells(2, edge + 8 * j)
@@ -97,7 +102,7 @@
                 start = 2 * EDGE + 8 + 8 * col
                 out[layer, start : start + 8, :] = t_cells(col, t_edge)
 
-        def side(right, _, g_ref, up_ref, down_ref):
+        def side(right, _, g_ref, first_ref, second_ref):
             col, t_col = (2, 1) if right else (0, 0)
             at, t_at = (64 - WIDE, LANES - WIDE) if right else (64, 0)
             half = SUM_ROWS // 2
@@ -117,7 +122,7 @@
                     for slot, value in enumerate(parts[part * SLOTS : (part + 1) * SLOTS]):
                         extra = place(extra, value, source, WIDE * slot, WIDE)
                     g_ref[layer, first + 8 * part : first + 8 * part + 8, :] = extra
-            for out, edge, t_edge in ((up_ref, 0, 0), (down_ref, rows - EDGE, rows - 2 * RIM - 8)):
+            for out, edge, t_edge in ((first_ref, edges[0], t_edges[0]), (second_ref, edges[1], t_edges[1])):
                 strips = [cells(col, edge + 8 * j) for j in range(9)]
                 for j in range(4):
                     out[layer, 8 * j : 8 * j + 8, :] = both(strips[j], strips[j + 5])
@@ -128,10 +133,26 @@
                 extra = place(extra, t_cells(t_col, t_edge), t_at, start + 9 * WIDE, WIDE)
                 out[layer, 32:40, :] = extra
 
-        by_side(sides, side, to_g, to_d_up, to_d_down)
+        by_side(sides, side, to_g, to_d_first, to_d_second)
+
+    def arrivals(layer):
+        return (
+            pltpu.make_async_copy(mantissa_in.at[layer], mantissa.at[layer], in_sems.at[0, layer]),
+            pltpu.make_async_copy(t_in.at[layer], t_ref.at[layer], in_sems.at[1, layer]),
+        )
+
+    scales = pltpu.make_async_copy(exponent_in, exponent, exponent_sem)
+    scales.start()
+    for layer in range(depth):
+        for one in arrivals(layer):
+            one.start()
+    scales.wait()
 
     @pl.loop(0, depth)
     def _(layer):
+        for one in arrivals(layer):
+            one.wait()
+
         @pl.loop(0, rows // TILE)
         def _(tile_row):
             for col in range(3):
@@ -152,11 +173,17 @@
 
 def sum_kernel(sides, *refs):
     count = len(sides)
-    plain, from_below, from_above = refs[:3]
-    from_g, d_below, d_above = refs[3 : 3 + count], refs[3 + count : 3 + 2 * count], refs[3 + 2 * count : 3 + 3 * count]
+    plain, payloads = refs[0], refs[1:]
+    from_g, payloads = payloads[:count], payloads[count:]
+    from_first, payloads = payloads[0], payloads[1:]
+    from_second, payloads = payloads[0], payloads[1:]
+    d_first, payloads = payloads[:count], payloads[count:]
+    d_second, payloads = payloads[:count], payloads[count:]
     own, other, total, t_edge, sems = refs[3 + 3 * count :]
     depth = plain.shape[0]
     core = lax.axis_index("ta")
+    odd = lax.rem(lax.axis_index("gx"), 2)
+    after = (1 - odd, odd)
     lane = lane_ids()
     low = lane < 64
     half = SUM_ROWS // 2
@@ -185,18 +212,18 @@
             total[layer, 2, where, :] = jnp.where(centre, jnp.where(low, left, right), 0.0)
 
         def add(col, row, value):
-            total[layer, col, row : row + 8, :] = total[layer, col, row : row + 8, :] + value
-
-        for edge, ref in ((0, from_above), (SUM_ROWS - EDGE, from_below)):
+            total[layer, col, rows8(row), :] = total[layer, col, rows8(row), :] + value
+
+        for which, ref in zip(after, (from_first, from_second)):
+            edge = which * (SUM_ROWS - EDGE)
+            t_edge[which, layer, :, :] = ref[layer, 2 * EDGE + 8 :, :]
             extra = ref[layer, 2 * EDGE : 2 * EDGE + 8, :]
             for j in range(9):
                 add(0, edge + 8 * j, ref[layer, 8 * j : 8 * j + 8, :])
                 add(1, edge + 8 * j, ref[layer, EDGE + 8 * j : EDGE + 8 * j + 8, :])
                 add(2, edge + 8 * j, jnp.where(centre, turn(extra, 64 - WIDE - 2 * WIDE * j), 0.0))
-        t_edge[0, layer, :, :] = from_above[layer, 2 * EDGE + 8 :, :]
-        t_edge[1, layer, :, :] = from_below[layer, 2 * EDGE + 8 :, :]
-
-        def side(right, _, g_ref, below_ref, above_ref):
+
+        def side(right, _, g_ref, first_ref, second_ref):
             main = low if right else jnp.logical_not(low)
             at, t_at = (64, 0) if right else (64 - WIDE, LANES - WIDE)
 
@@ -214,7 +241,8 @@
                     k = j - 1
                     value = value + window(extras[2 + k // SLOTS], WIDE * (k % SLOTS), t_at)
                 add(2, 8 * j, value)
-            for edge, ref, t_row in ((0, above_ref, 0), (SUM_ROWS - EDGE, below_ref, SUM_ROWS - 8)):
+            for which, ref in zip(after, (first_ref, second_ref)):
+                edge, t_row = which * (SUM_ROWS - EDGE), which * (SUM_ROWS - 8)
                 extra = ref[layer, 32:40, :]
                 start = 64 if right else 0
                 for j in range(9):
@@ -225,7 +253,7 @@
                     add(2, edge + 8 * j, window(extra, start + WIDE * j, at))
                 add(2, t_row, window(extra, start + 9 * WIDE, t_at))
 
-        by_side(sides, side, from_g, d_below, d_above)
+        by_side(sides, side, from_g, d_first, d_second)
 
     made = copies(1 - core, other, 0) + copies(core, own, 1)
     for one in made:
@@ -471,10 +499,10 @@
         return [inner] * 4 + [jnp.where(low, ones[1], ones[0]) * halo_mask]
 
     def conductances(src):
-        @pl.loop(0, STEP_ROWS // 5)
+        @pl.loop(0, STEP_ROWS // 14)
         def _(block):
-            for part in range(5):
-                step = block * 5 + part
+            for part in range(14):
+                step = block * 14 + part
                 mask = masks(step)
                 for col in range(5):
                     where = at(step + 1, col)
@@ -483,11 +511,11 @@
         ghosts(cond)
 
     def coefficients(src):
-        @pl.loop(0, STEP_ROWS // 5)
+        @pl.loop(0, STEP_ROWS // 10)
         def _(block):
-            start = block * 5
-            lines = [[cond[at(start + part, col), :] for col in range(5)] for part in range(7)]
-            for part in range(5):
+            start = block * 10
+            lines = [[cond[at(start + part, col), :] for col in range(5)] for part in range(12)]
+            for part in range(10):
                 up, here, down = lines[part], lines[part + 1], lines[part + 2]
                 mask = masks(start + part)
                 rights, lefts = to_right(here), to_left(here)
@@ -581,6 +609,7 @@
     count = len(out_sides)
 
     t_other = lax.ppermute(t_initial, "ta", swap)
+    exponents = tile_exponent.transpose(1, 0, 2)
     plain_shape = array((depth, 3, rows + 2 * RIM, LANES), F32)
     along = array((depth, ROWS_P, LANES), F32)
     across = (array((depth, ROWS_G, LANES), F32),) * count
@@ -588,30 +617,41 @@
     sent = pl.pallas_call(
         functools.partial(send_kernel, out_sides),
         out_shape=(plain_shape, along, along) + across + corner,
-        in_specs=[VMEM, SMEM, VMEM],
+        in_specs=[HBM, HBM, HBM],
         out_specs=(ANY,) + (VMEM,) * (2 + 3 * count),
-        scratch_shapes=[pltpu.VMEM(plain_shape.shape, F32), pltpu.SemaphoreType.DMA((depth,))],
+        scratch_shapes=[
+            pltpu.VMEM(plain_shape.shape, F32),
+            pltpu.VMEM(power_mantissa.shape, power_mantissa.dtype),
+            pltpu.SMEM(exponents.shape, jnp.int32),
+            pltpu.VMEM(t_initial.shape, F32),
+            pltpu.SemaphoreType.DMA((depth,)),
+            pltpu.SemaphoreType.DMA((2, depth)),
+            pltpu.SemaphoreType.DMA,
+        ],
         compiler_params=params(12),
         name="send",
-    )(power_mantissa, tile_exponent.transpose(1, 0, 2), t_initial)
-    plain, up, down = sent[:3]
-    to_g, to_d_up, to_d_down = sent[3 : 3 + count], sent[3 + count : 3 + 2 * count], sent[3 + 2 * count :]
-
-    def move(value, step_z, step_x):
+    )(*(pltpu.with_memory_space_constraint(value, pltpu.HBM) for value in (power_mantissa, exponents, t_initial)))
+    sent = tuple(sent[:1]) + tuple(lax.optimization_barrier(tuple(sent[1:]) + (t_other,)))
+    sent, t_other = sent[:-1], sent[-1]
+    plain, first, second = sent[:3]
+    to_g, to_d_first, to_d_second = sent[3 : 3 + count], sent[3 + count : 3 + 2 * count], sent[3 + 2 * count :]
+
+    def move(value, start, step_x):
         pairs = []
         for z in range(n_gx):
+            to_z = z if start is None else z + 1 if (z - start) % 2 == 0 else z - 1
             for x in range(n_gy):
-                to_z, to_x = z + step_z, x ^ 1 if step_x is None else x + step_x
+                to_x = x ^ 1 if step_x is None else x + step_x
                 if 0 <= to_z < n_gx and 0 <= to_x < n_gy:
                     pairs.append((z * n_gy + x, to_z * n_gy + to_x))
         return lax.ppermute(value, ("gx", "gy"), pairs)
 
     steps = [None] if n_gy == 2 else [1, -1]
-    from_g = [move(value, 0, step) for value, step in zip(to_g, steps)]
-    from_above = move(down, 1, 0)
-    from_below = move(up, -1, 0)
-    d_above = [move(value, 1, step) for value, step in zip(to_d_down, steps)]
-    d_below = [move(value, -1, step) for value, step in zip(to_d_up, steps)]
+    from_g = [move(value, None, step) for value, step in zip(to_g, steps)]
+    from_first = move(first, 0, 0)
+    from_second = move(second, 1, 0)
+    d_first = [move(value, 0, step) for value, step in zip(to_d_first, steps)]
+    d_second = [move(value, 1, step) for value, step in zip(to_d_second, steps)]
 
     wide = jnp.pad(channel_mask, ((0, 0), (RIM, RIM)))
     mask = lax.dynamic_slice_in_dim(wide, lax.axis_index("gy") * cols, cols + 2 * RIM, 1).astype(F32) * COOLANT
@@ -648,7 +688,7 @@
         ],
         compiler_params=params(12),
         name="sum",
-    )(plain, from_below, from_above, *from_g, *d_below, *d_above)
+    )(plain, *from_g, from_first, from_second, *d_first, *d_second)
     received = lax.ppermute(other, "ta", swap)
     whole = array((depth, rows, cols), F32)
     heat_source = pl.pallas_call(
@@ -676,7 +716,7 @@
             pltpu.SemaphoreType.DMA((2,)),
             pltpu.SemaphoreType.DMA((2,)),
         ],
-        compiler_params=params(44),
+        compiler_params=params(30),
         name="solve",
     )(own, received, now, flow, material, conductivity)
     received = lax.ppermute(sent, "ta", swap)

time: 56.8 us -> 46.7 us (0.82)
  starting transfers between devices: 15.5 us -> 10.6 us
  Pallas kernels: 30.2 us -> 27.3 us
  local copies, waits for them, and re-layouts: 2.41 us -> 0.45 us
    pallas_call x1, Pallas kernels: 20.1 us -> 16.1 us  [on_device(): pl.pallas_call(functools.partial(solve_kernel, (n_gx * rows, n_gy * cols)...]
    ppermute x5, starting transfers between devices: 10.5 us -> 7.9 us  [move(): return lax.ppermute(value, ('gx', 'gy'), pairs)]
    unnamed x10 -> x8, local copies, waits for them, and re-layouts: 1.98 us -> 0.02 us
    ppermute x1, starting transfers between devices: 3.01 us -> 1.8 us  [on_device(): received = lax.ppermute(other, 'ta', swap)]
    pallas_call x1, Pallas kernels: 1.78 us -> 2.95 us  [on_device(): pl.pallas_call(heat_kernel, out_shape=whole, in_specs=[VMEM] * 2, out_spe...]
    ppermute x1, starting transfers between devices: 1.86 us -> 0.74 us  [on_device(): t_other = lax.ppermute(t_initial, 'ta', swap)]
    pallas_call x1, Pallas kernels: 1.37 us -> 2.19 us  [on_device(): pl.pallas_call(functools.partial(sum_kernel, in_sides), out_shape=(half,...]
    pallas_call x1, Pallas kernels: 2.72 us -> 1.99 us  [on_device(): pl.pallas_call(stack_kernel, out_shape=grouped, in_specs=[ANY] * 2, out_s...]
  transfers between devices with their start and end apart: 8 -> 8, of which waited for: 3 -> 2; matrix products, arithmetic and copies ran while one was open for 1% -> 1% of each run, Pallas kernels for 10% -> 11%
where the time goes in v5:
time: 46.7 us; the launch traced here: 46.4 us
  Pallas kernels  27.3 us (58%)
  starting transfers between devices  10.6 us (23%)
  waiting for transfers between devices  7.03 us (15%)
  between operations  0.77 us (2%)
    pallas_call x1, Pallas kernels, on_device(): pl.pallas_call(functools.partial(solve_kernel, (n_gx * rows, n_gy * cols)...  16.1 us
    ppermute x5, starting transfers between devices, move(): return lax.ppermute(value, ('gx', 'gy'), pairs)  7.9 us
    ppermute x5, waiting for transfers between devices, move(): return lax.ppermute(value, ('gx', 'gy'), pairs)  7.02 us
    pallas_call x1, Pallas kernels, on_device(): pl.pallas_call(functools.partial(send_kernel, out_sides), out_shape=(plai...  3.34 us
    pallas_call x1, Pallas kernels, on_device(): pl.pallas_call(heat_kernel, out_shape=whole, in_specs=[VMEM] * 2, out_spe...  2.95 us
    pallas_call x1, Pallas kernels, on_device(): pl.pallas_call(functools.partial(sum_kernel, in_sides), out_shape=(half,...  2.19 us
    pallas_call x1, Pallas kernels, on_device(): pl.pallas_call(stack_kernel, out_shape=grouped, in_specs=[ANY] * 2, out_s...  1.99 us
    ppermute x1, starting transfers between devices, on_device(): received = lax.ppermute(other, 'ta', swap)  1.8 us
  transfers between devices with their start and end apart: 8, of which 2 were waited for; matrix products, arithmetic and copies ran while one was open for 1% of the time, Pallas kernels for 11%

profile of v5, /device:TPU:21, one launch (start us, length us, event | category | flops | bytes accessed | tf_op | source)
XLA Modules:
  0.0 46.4 jit_solution(8705660498309069774)
XLA Ops:
  0.6 0.7 %collective-permute-start = (f32[4,256,256]{2,1,0:T(8,128)}, f32[4,256,256]{2,1,0:T(8,128)S(1)}, u32[]{:S(2)}, u32[]{:S(2)}) collective-permute-start(f32[4,256,256]{2,1,0:T(8,128)} %t_own.1), channel_id=1, source_target_pairs={{0,1},{1,0},{2,3},{3,2},{4,5},{5,4},{6,7},{7,6},{8,9},{9,8},{10,11... | collective-permute-start | bytes 3145736 | tf_op jit(solution)/shard_map/ppermute | solution.py:611
  1.4 3.3 %send.1 = (f32[4,3,384,128]{3,2,1,0:T(8,128)S(1)}, f32[4,168,128]{2,1,0:T(8,128)S(1)}, f32[4,168,128]{2,1,0:T(8,128)S(1)}, f32[4,168,128]{2,1,0:T(8,128)S(1)}, f...) custom-call(bf16[4,384,384]{2,1,0:T(8,128)(2,1)} %mantissa_in.1, s32[6,4,6]{2,1,0:T(4,128)} %bitcast.9, ...), custom_call_target="tpu_custom_call" | custom-call | tf_op jit(solution)/shard_map/send/pallas_call | solution.py:617
  4.7 0.0 collective-permute-done.t_other
  4.7 1.3 %collective-permute-start.1 = (f32[4,168,128]{2,1,0:T(8,128)S(1)}, f32[4,168,128]{2,1,0:T(8,128)S(1)}, u32[]{:S(2)}, u32[]{:S(2)}) collective-permute-start(f32[4,168,128]{2,1,0:T(8,128)S(1)} %get-tuple-element.24), channel_id=1, source_target_pairs={{0,2},{2,0},{4,6},{6,4},{8,10},{10,8},{12,14},{14,12},{1,3},{3,1},... | collective-permute-start | bytes 1032200 | tf_op jit(solution)/shard_map/ppermute | solution.py:647
  6.0 1.3 %collective-permute-start.2 = (f32[4,168,128]{2,1,0:T(8,128)S(1)}, f32[4,168,128]{2,1,0:T(8,128)S(1)}, u32[]{:S(2)}, u32[]{:S(2)}) collective-permute-start(f32[4,168,128]{2,1,0:T(8,128)S(1)} %get-tuple-element.25), channel_id=1, source_target_pairs={{0,4},{2,6},{4,0},{6,2},{8,12},{10,14},{12,8},{14,10},{1,5},{3,7},... | collective-permute-start | bytes 1032200 | tf_op jit(solution)/shard_map/ppermute | solution.py:647
  7.3 1.9 %collective-permute-start.3 = (f32[4,168,128]{2,1,0:T(8,128)S(1)}, f32[4,168,128]{2,1,0:T(8,128)S(1)}, u32[]{:S(2)}, u32[]{:S(2)}) collective-permute-start(f32[4,168,128]{2,1,0:T(8,128)S(1)} %get-tuple-element.26), channel_id=1, source_target_pairs={{4,8},{6,10},{8,4},{10,6},{5,9},{7,11},{9,5},{11,7},{20,24},{22,26... | collective-permute-start | bytes 1032200 | tf_op jit(solution)/shard_map/ppermute | solution.py:647
  9.2 0.1 collective-permute-start.4
  9.3 3.4 %collective-permute-start.5 = (f32[4,40,128]{2,1,0:T(8,128)S(1)}, f32[4,40,128]{2,1,0:T(8,128)S(1)}, u32[]{:S(2)}, u32[]{:S(2)}) collective-permute-start(f32[4,40,128]{2,1,0:T(8,128)S(1)} %get-tuple-element.28), channel_id=1, source_target_pairs={{4,10},{6,8},{8,6},{10,4},{5,11},{7,9},{9,7},{11,5},{20,26},{22,24... | collective-permute-start | bytes 245768 | tf_op jit(solution)/shard_map/ppermute | solution.py:647
  12.7 4.4 %collective-permute-done.4.refs_4_ = f32[4,40,128]{2,1,0:T(8,128)S(1)} collective-permute-done((f32[4,40,128]{2,1,0:T(8,128)S(1)}, f32[4,40,128]{2,1,0:T(8,128)S(1)}, u32[]{:S(2)}, u32[]{:S(2)}) %collective-permute-start.4) | collective-permute-done | bytes 81952 | tf_op jit(solution)/shard_map/ppermute | solution.py:647
  17.1 2.6 %collective-permute-done.5.refs_5_ = f32[4,40,128]{2,1,0:T(8,128)S(1)} collective-permute-done((f32[4,40,128]{2,1,0:T(8,128)S(1)}, f32[4,40,128]{2,1,0:T(8,128)S(1)}, u32[]{:S(2)}, u32[]{:S(2)}) %collective-permute-start.5) | collective-permute-done | bytes 81952 | tf_op jit(solution)/shard_map/ppermute | solution.py:647
  19.7 0.0 collective-permute-done.1.refs_1_
  19.7 0.0 collective-permute-done.2.refs_2_
  19.7 0.0 collective-permute-done.3.refs_3_
  19.7 0.0 copy-start.3
  19.7 0.0 copy-start
  19.7 2.2 %sum.1 = (f32[4,448,128]{2,1,0:T(8,128)S(1)}, f32[4,448,128]{2,1,0:T(8,128)}) custom-call(f32[4,3,384,128]{3,2,1,0:T(8,128)S(1)} %get-tuple-element.18.refs_0_, f32[4,168,128]{2,1,0:T(8,128)S(1)} %collective-permute-done.1.refs_1_, f32[4,168,128]{2,1,0:T(8,128)S(1)} %collective-permute-done.2.refs_2_, f32[4,168,128]{2,1,0:T(8,128)S(1)} %collective-permute-done.3.refs_3_, ...), custom_call_target="tpu_custom_call" | custom-call | tf_op jit(solution)/shard_map/sum/pallas_call | solution.py:679
  21.9 1.8 %collective-permute-start.6 = (f32[4,448,128]{2,1,0:T(8,128)}, f32[4,448,128]{2,1,0:T(8,128)}, u32[]{:S(2)}, u32[]{:S(2)}) collective-permute-start(f32[4,448,128]{2,1,0:T(8,128)} %get-tuple-element.30.other), channel_id=1, source_target_pairs={{0,1},{1,0},{2,3},{3,2},{4,5},{5,4},{6,7},{7,6},{8,9},{9,8},{10,11... | collective-permute-start | bytes 2752520 | tf_op jit(solution)/shard_map/ppermute | solution.py:692
  23.7 0.0 copy-done.3
  23.7 0.1 fusion.1
  23.8 0.1 slice.14
  23.9 0.1 copy.12
  24.0 0.1 copy.13
  24.1 0.1 pad.10.clone
  24.2 0.1 fusion.2
  24.2 0.1 maximum_bitcast_fusion.1
  24.3 0.1 pad_maximum_fusion.flow
  24.4 0.0 copy-done
  24.4 0.0 copy-start.1
  24.4 0.0 copy-start.2
  24.4 2.0 %stack.1.now_in = f32[2880,128]{1,0:T(8,128)S(1)} custom-call(f32[4,256,256]{2,1,0:T(8,128)S(1)} %copy-done, f32[4,256,256]{2,1,0:T(8,128)S(1)} %collective-permute-done.t_other), custom_call_target="tpu_custom_call" | custom-call | tf_op jit(solution)/shard_map/stack/pallas_call | solution.py:665
  26.4 0.0 collective-permute-done.6.other
  26.4 0.0 copy-done.1
  26.5 0.0 copy-done.2
  26.5 16.1 %solve.1 = (f32[4,256,256]{2,1,0:T(8,128)}, f32[4,128,256]{2,1,0:T(8,128)S(1)}) custom-call(f32[4,448,128]{2,1,0:T(8,128)S(1)} %get-tuple-element.29.own, f32[4,448,128]{2,1,0:T(8,128)} %collective-permute-done.6.other, f32[2880,128]{1,0:T(8,128)S(1)} %stack.1.now_in, f32[40,128]{1,0:T(8,128)S(1)} %pad_maximum_fusion.flow, s32[8]{0:T(128)S(1)} %copy-done.1, ...), custom_call_target="tpu_custom_call" | custom-call | tf_op jit(solution)/shard_map/solve/pallas_call | solution.py:704
  42.5 0.1 collective-permute-start.7
  42.7 3.0 %heat.1 = f32[4,256,256]{2,1,0:T(8,128)} custom-call(f32[4,448,128]{2,1,0:T(8,128)S(1)} %get-tuple-element.29.own, f32[4,448,128]{2,1,0:T(8,128)} %get-tuple-element.30.other), custom_call_target="tpu_custom_call" | custom-call | tf_op jit(solution)/shard_map/heat/pallas_call | solution.py:694
  45.6 0.0 collective-permute-done.7.received
  45.6 0.8 %place.1 = f32[4,256,256]{2,1,0:T(8,128)} custom-call(f32[4,128,256]{2,1,0:T(8,128)S(1)} %collective-permute-done.7.received, f32[4,256,256]{2,1,0:T(8,128)} %get-tuple-element.33.t_in), custom_call_target="tpu_custom_call", output_to_operand_aliasing={{}: (1, {})} | custom-call | tf_op jit(solution)/shard_map/place/pallas_call | solution.py:723
  (2 shorter events, 0.0 us)
Async XLA Ops:
  0.6 4.1 %collective-permute-start = (f32[4,256,256]{2,1,0:T(8,128)}, f32[4,256,256]{2,1,0:T(8,128)S(1)}, u32[]{:S(2)}, u32[]{:S(2)}) collective-permute-start(f32[4,256,256]{2,1,0:T(8,128)} %t_own.1), channel_id=1, source_target_pairs={{0,1},{1,0},{2,3},{3,2},{4,5},{5,4},{6,7},{7,6},{8,9},{9,8},{10,11... | collective-permute-start | bytes 3145736 | tf_op jit(solution)/shard_map/ppermute | solution.py:611
  4.7 14.9 %collective-permute-start.1 = (f32[4,168,128]{2,1,0:T(8,128)S(1)}, f32[4,168,128]{2,1,0:T(8,128)S(1)}, u32[]{:S(2)}, u32[]{:S(2)}) collective-permute-start(f32[4,168,128]{2,1,0:T(8,128)S(1)} %get-tuple-element.24), channel_id=1, source_target_pairs={{0,2},{2,0},{4,6},{6,4},{8,10},{10,8},{12,14},{14,12},{1,3},{3,1},... | collective-permute-start | bytes 1032200 | tf_op jit(solution)/shard_map/ppermute | solution.py:647
  6.0 13.7 %collective-permute-start.2 = (f32[4,168,128]{2,1,0:T(8,128)S(1)}, f32[4,168,128]{2,1,0:T(8,128)S(1)}, u32[]{:S(2)}, u32[]{:S(2)}) collective-permute-start(f32[4,168,128]{2,1,0:T(8,128)S(1)} %get-tuple-element.25), channel_id=1, source_target_pairs={{0,4},{2,6},{4,0},{6,2},{8,12},{10,14},{12,8},{14,10},{1,5},{3,7},... | collective-permute-start | bytes 1032200 | tf_op jit(solution)/shard_map/ppermute | solution.py:647
  7.3 12.4 %collective-permute-start.3 = (f32[4,168,128]{2,1,0:T(8,128)S(1)}, f32[4,168,128]{2,1,0:T(8,128)S(1)}, u32[]{:S(2)}, u32[]{:S(2)}) collective-permute-start(f32[4,168,128]{2,1,0:T(8,128)S(1)} %get-tuple-element.26), channel_id=1, source_target_pairs={{4,8},{6,10},{8,4},{10,6},{5,9},{7,11},{9,5},{11,7},{20,24},{22,26... | collective-permute-start | bytes 1032200 | tf_op jit(solution)/shard_map/ppermute | solution.py:647
  9.2 7.9 %collective-permute-start.4 = (f32[4,40,128]{2,1,0:T(8,128)S(1)}, f32[4,40,128]{2,1,0:T(8,128)S(1)}, u32[]{:S(2)}, u32[]{:S(2)}) collective-permute-start(f32[4,40,128]{2,1,0:T(8,128)S(1)} %get-tuple-element.27), channel_id=1, source_target_pairs={{0,6},{2,4},{4,2},{6,0},{8,14},{10,12},{12,10},{14,8},{1,7},{3,5},... | collective-permute-start | bytes 245768 | tf_op jit(solution)/shard_map/ppermute | solution.py:647
  9.3 10.4 %collective-permute-start.5 = (f32[4,40,128]{2,1,0:T(8,128)S(1)}, f32[4,40,128]{2,1,0:T(8,128)S(1)}, u32[]{:S(2)}, u32[]{:S(2)}) collective-permute-start(f32[4,40,128]{2,1,0:T(8,128)S(1)} %get-tuple-element.28), channel_id=1, source_target_pairs={{4,10},{6,8},{8,6},{10,4},{5,11},{7,9},{9,7},{11,5},{20,26},{22,24... | collective-permute-start | bytes 245768 | tf_op jit(solution)/shard_map/ppermute | solution.py:647
  19.7 4.0 %copy-start.3 = (s32[8,512]{1,0:T(8,128)S(1)}, s32[8,512]{1,0:T(8,128)}, u32[]{:S(2)}) copy-start(s32[8,512]{1,0:T(8,128)} %param.9) | copy-start | bytes 49156
  19.7 4.7 %copy-start = (f32[4,256,256]{2,1,0:T(8,128)S(1)}, f32[4,256,256]{2,1,0:T(8,128)}, u32[]{:S(2)}) copy-start(f32[4,256,256]{2,1,0:T(8,128)} %t_own.1) | copy-start | bytes 3145732
  21.9 4.5 %collective-permute-start.6 = (f32[4,448,128]{2,1,0:T(8,128)}, f32[4,448,128]{2,1,0:T(8,128)}, u32[]{:S(2)}, u32[]{:S(2)}) collective-permute-start(f32[4,448,128]{2,1,0:T(8,128)} %get-tuple-element.30.other), channel_id=1, source_target_pairs={{0,1},{1,0},{2,3},{3,2},{4,5},{5,4},{6,7},{7,6},{8,9},{9,8},{10,11... | collective-permute-start | bytes 2752520 | tf_op jit(solution)/shard_map/ppermute | solution.py:692
  24.4 2.0 %copy-start.1 = (s32[8]{0:T(128)S(1)}, s32[8]{0:T(128)}, u32[]{:S(2)}) copy-start(s32[8]{0:T(128)} %material.1) | copy-start | bytes 100
  24.4 2.0 %copy-start.2 = (f32[4]{0:T(128)S(1)}, f32[4]{0:T(128)}, u32[]{:S(2)}) copy-start(f32[4]{0:T(128)} %conductivity.1) | copy-start | bytes 52
  42.5 3.1 %collective-permute-start.7 = (f32[4,128,256]{2,1,0:T(8,128)S(1)}, f32[4,128,256]{2,1,0:T(8,128)S(1)}, u32[]{:S(2)}, u32[]{:S(2)}) collective-permute-start(f32[4,128,256]{2,1,0:T(8,128)S(1)} %get-tuple-element.32), channel_id=1, source_target_pairs={{0,1},{1,0},{2,3},{3,2},{4,5},{5,4},{6,7},{7,6},{8,9},{9,8},{10,11... | collective-permute-start | bytes 1572872 | tf_op jit(solution)/shard_map/ppermute | solution.py:722

commit v6 on v5

--- a/solution.py
+++ b/solution.py
@@ -425,10 +425,10 @@
     t_edge = permuted(t_edge, permutation())
     halo_lanes = (lane < WIDE) | ((lane >= 64 - WIDE) & (lane < 64 + WIDE)) | (lane >= LANES - WIDE)
 
-    @pl.loop(0, STEP_ROWS // 5)
+    @pl.loop(0, STEP_ROWS // 14)
     def _(block):
-        for part in range(5):
-            step = block * 5 + part
+        for part in range(14):
+            step = block * 14 + part
             first, second = across(2 * HALF_ROWS + 2 + step), across(2 * HALF_ROWS + 2 + step + STEP_ROWS)
             first_turned, second_turned = turn(first, 64), turn(second, 64)
             upper_lanes = jnp.where(lane < 64 + WIDE, first, first_turned)
@@ -499,10 +499,10 @@
         return [inner] * 4 + [jnp.where(low, ones[1], ones[0]) * halo_mask]
 
     def conductances(src):
-        @pl.loop(0, STEP_ROWS // 14)
+        @pl.loop(0, STEP_ROWS // 35)
         def _(block):
-            for part in range(14):
-                step = block * 14 + part
+            for part in range(35):
+                step = block * 35 + part
                 mask = masks(step)
                 for col in range(5):
                     where = at(step + 1, col)
@@ -675,6 +675,7 @@
         name="stack",
     )(t_initial, t_other)
 
+    from_first, now = lax.optimization_barrier((from_first, now))
     half = array((depth, SWAP, LANES), F32)
     own, other = pl.pallas_call(
         functools.partial(sum_kernel, in_sides),
@@ -700,6 +701,7 @@
         name="heat",
     )(own, other)
 
+    received, heat_source = lax.optimization_barrier((received, heat_source))
     work = pltpu.VMEM(grouped.shape, F32)
     t_part, sent = pl.pallas_call(
         functools.partial(solve_kernel, (n_gx * rows, n_gy * cols)),

time: 46.7 us -> 43.8 us (0.938)
  Pallas kernels: 27.3 us -> 24.7 us
    ppermute x5, waiting for transfers between devices: 7.02 us -> 4.94 us  [move(): return lax.ppermute(value, ('gx', 'gy'), pairs)]
    ppermute x1, waiting for transfers between devices: 0.01 us -> 1.81 us  [on_device(): received = lax.ppermute(sent, 'ta', swap)]
    pallas_call x1, Pallas kernels: 2.95 us -> 1.78 us  [on_device(): pl.pallas_call(heat_kernel, out_shape=whole, in_specs=[VMEM] * 2, out_spe...]
    pallas_call x1, Pallas kernels: 16.1 us -> 15.3 us  [on_device(): pl.pallas_call(functools.partial(solve_kernel, (n_gx * rows, n_gy * cols)...]
    pallas_call x1, Pallas kernels: 2.19 us -> 1.46 us  [on_device(): pl.pallas_call(functools.partial(sum_kernel, in_sides), out_shape=(half,...]
  transfers between devices with their start and end apart: 8 -> 8, of which waited for: 2 -> 3; matrix products, arithmetic and copies ran while one was open for 1% -> 2% of each run, Pallas kernels for 11% -> 9%
where the time goes in v6:
time: 43.8 us; the launch traced here: 43.6 us
  Pallas kernels  24.7 us (56%)
  starting transfers between devices  10.7 us (24%)
  waiting for transfers between devices  6.75 us (15%)
  between operations  0.75 us (2%)
  local copies, waits for them, and re-layouts  0.45 us (1%)
    pallas_call x1, Pallas kernels, on_device(): pl.pallas_call(functools.partial(solve_kernel, (n_gx * rows, n_gy * cols)...  15.3 us
    ppermute x5, starting transfers between devices, move(): return lax.ppermute(value, ('gx', 'gy'), pairs)  7.92 us
    ppermute x5, waiting for transfers between devices, move(): return lax.ppermute(value, ('gx', 'gy'), pairs)  4.94 us
    pallas_call x1, Pallas kernels, on_device(): pl.pallas_call(functools.partial(send_kernel, out_sides), out_shape=(plai...  3.34 us
    pallas_call x1, Pallas kernels, on_device(): pl.pallas_call(stack_kernel, out_shape=grouped, in_specs=[ANY] * 2, out_s...  1.99 us
    ppermute x1, starting transfers between devices, on_device(): received = lax.ppermute(other, 'ta', swap)  1.86 us
    ppermute x1, waiting for transfers between devices, on_device(): received = lax.ppermute(sent, 'ta', swap)  1.81 us
    pallas_call x1, Pallas kernels, on_device(): pl.pallas_call(heat_kernel, out_shape=whole, in_specs=[VMEM] * 2, out_spe...  1.78 us
  transfers between devices with their start and end apart: 8, of which 3 were waited for; matrix products, arithmetic and copies ran while one was open for 2% of the time, Pallas kernels for 9%

profile of v6, /device:TPU:21, one launch (start us, length us, event | category | flops | bytes accessed | tf_op | source)
XLA Modules:
  0.0 43.6 jit_solution(2268840161614370651)
XLA Ops:
  0.6 0.0 copy-start
  0.6 0.7 %collective-permute-start = (f32[4,256,256]{2,1,0:T(8,128)}, f32[4,256,256]{2,1,0:T(8,128)S(1)}, u32[]{:S(2)}, u32[]{:S(2)}) collective-permute-start(f32[4,256,256]{2,1,0:T(8,128)} %t_own.1), channel_id=1, source_target_pairs={{0,1},{1,0},{2,3},{3,2},{4,5},{5,4},{6,7},{7,6},{8,9},{9,8},{10,11... | collective-permute-start | bytes 3145736 | tf_op jit(solution)/shard_map/ppermute | solution.py:611
  1.4 3.3 %send.1 = (f32[4,3,384,128]{3,2,1,0:T(8,128)S(1)}, f32[4,168,128]{2,1,0:T(8,128)S(1)}, f32[4,168,128]{2,1,0:T(8,128)S(1)}, f32[4,168,128]{2,1,0:T(8,128)S(1)}, f...) custom-call(bf16[4,384,384]{2,1,0:T(8,128)(2,1)} %mantissa_in.1, s32[6,4,6]{2,1,0:T(4,128)} %bitcast.9, ...), custom_call_target="tpu_custom_call" | custom-call | tf_op jit(solution)/shard_map/send/pallas_call | solution.py:617
  4.7 0.0 collective-permute-done.t_other
  4.7 1.4 %collective-permute-start.2 = (f32[4,168,128]{2,1,0:T(8,128)S(1)}, f32[4,168,128]{2,1,0:T(8,128)S(1)}, u32[]{:S(2)}, u32[]{:S(2)}) collective-permute-start(f32[4,168,128]{2,1,0:T(8,128)S(1)} %get-tuple-element.29), channel_id=1, source_target_pairs={{0,4},{2,6},{4,0},{6,2},{8,12},{10,14},{12,8},{14,10},{1,5},{3,7},... | collective-permute-start | bytes 1032200 | tf_op jit(solution)/shard_map/ppermute | solution.py:647
  6.1 1.2 %collective-permute-start.1 = (f32[4,168,128]{2,1,0:T(8,128)S(1)}, f32[4,168,128]{2,1,0:T(8,128)S(1)}, u32[]{:S(2)}, u32[]{:S(2)}) collective-permute-start(f32[4,168,128]{2,1,0:T(8,128)S(1)} %get-tuple-element.28), channel_id=1, source_target_pairs={{0,2},{2,0},{4,6},{6,4},{8,10},{10,8},{12,14},{14,12},{1,3},{3,1},... | collective-permute-start | bytes 1032200 | tf_op jit(solution)/shard_map/ppermute | solution.py:647
  7.3 1.9 %collective-permute-start.3 = (f32[4,168,128]{2,1,0:T(8,128)S(1)}, f32[4,168,128]{2,1,0:T(8,128)S(1)}, u32[]{:S(2)}, u32[]{:S(2)}) collective-permute-start(f32[4,168,128]{2,1,0:T(8,128)S(1)} %get-tuple-element.32), channel_id=1, source_target_pairs={{4,8},{6,10},{8,4},{10,6},{5,9},{7,11},{9,5},{11,7},{20,24},{22,26... | collective-permute-start | bytes 1032200 | tf_op jit(solution)/shard_map/ppermute | solution.py:647
  9.2 0.1 collective-permute-start.4
  9.3 3.4 %collective-permute-start.5 = (f32[4,40,128]{2,1,0:T(8,128)S(1)}, f32[4,40,128]{2,1,0:T(8,128)S(1)}, u32[]{:S(2)}, u32[]{:S(2)}) collective-permute-start(f32[4,40,128]{2,1,0:T(8,128)S(1)} %get-tuple-element.34), channel_id=1, source_target_pairs={{4,10},{6,8},{8,6},{10,4},{5,11},{7,9},{9,7},{11,5},{20,26},{22,24... | collective-permute-start | bytes 245768 | tf_op jit(solution)/shard_map/ppermute | solution.py:647
  12.7 0.0 copy-done
  12.7 2.0 %stack.1.now_in = f32[2880,128]{1,0:T(8,128)S(1)} custom-call(f32[4,256,256]{2,1,0:T(8,128)S(1)} %copy-done, f32[4,256,256]{2,1,0:T(8,128)S(1)} %collective-permute-done.t_other), custom_call_target="tpu_custom_call" | custom-call | tf_op jit(solution)/shard_map/stack/pallas_call | solution.py:665
  14.7 0.0 collective-permute-done.2.refs_2_
  14.7 2.4 %collective-permute-done.4.refs_4_ = f32[4,40,128]{2,1,0:T(8,128)S(1)} collective-permute-done((f32[4,40,128]{2,1,0:T(8,128)S(1)}, f32[4,40,128]{2,1,0:T(8,128)S(1)}, u32[]{:S(2)}, u32[]{:S(2)}) %collective-permute-start.4) | collective-permute-done | bytes 81952 | tf_op jit(solution)/shard_map/ppermute | solution.py:647
  17.1 2.5 %collective-permute-done.5.refs_5_ = f32[4,40,128]{2,1,0:T(8,128)S(1)} collective-permute-done((f32[4,40,128]{2,1,0:T(8,128)S(1)}, f32[4,40,128]{2,1,0:T(8,128)S(1)}, u32[]{:S(2)}, u32[]{:S(2)}) %collective-permute-start.5) | collective-permute-done | bytes 81952 | tf_op jit(solution)/shard_map/ppermute | solution.py:647
  19.6 0.0 collective-permute-done.1.refs_1_
  19.6 0.0 collective-permute-done.3.refs_3_
  19.6 0.0 copy-start.3
  19.6 1.5 %sum.1 = (f32[4,448,128]{2,1,0:T(8,128)S(1)}, f32[4,448,128]{2,1,0:T(8,128)S(1)}) custom-call(f32[4,3,384,128]{3,2,1,0:T(8,128)S(1)} %get-tuple-element.22.refs_0_, f32[4,168,128]{2,1,0:T(8,128)S(1)} %collective-permute-done.1.refs_1_, f32[4,168,128]{2,1,0:T(8,128)S(1)} %collective-permute-done.2.refs_2_, f32[4,168,128]{2,1,0:T(8,128)S(1)} %collective-permute-done.3.refs_3_, ...), custom_call_target="tpu_custom_call" | custom-call | tf_op jit(solution)/shard_map/sum/pallas_call | solution.py:680
  21.1 1.9 %collective-permute-start.6 = (f32[4,448,128]{2,1,0:T(8,128)S(1)}, f32[4,448,128]{2,1,0:T(8,128)}, u32[]{:S(2)}, u32[]{:S(2)}) collective-permute-start(f32[4,448,128]{2,1,0:T(8,128)S(1)} %get-tuple-element.36.other), channel_id=1, source_target_pairs={{0,1},{1,0},{2,3},{3,2},{4,5},{5,4},{6,7},{7,6},{8,9},{9,8},{10,11... | collective-permute-start | bytes 2752520 | tf_op jit(solution)/shard_map/ppermute | solution.py:693
  23.0 0.0 copy-done.3
  23.0 0.1 fusion.1
  23.1 0.1 slice.14
  23.1 0.1 copy.12
  23.3 0.1 copy.13
  23.3 0.1 pad.10.clone
  23.4 0.1 fusion.2
  23.5 0.1 maximum_bitcast_fusion.1
  23.6 0.0 copy-start.1
  23.6 0.0 copy-start.2
  23.6 0.1 pad_maximum_fusion.flow
  23.7 1.8 %heat.1 = f32[4,256,256]{2,1,0:T(8,128)} custom-call(f32[4,448,128]{2,1,0:T(8,128)S(1)} %get-tuple-element.35.own, f32[4,448,128]{2,1,0:T(8,128)S(1)} %get-tuple-element.36.other), custom_call_target="tpu_custom_call" | custom-call | tf_op jit(solution)/shard_map/heat/pallas_call | solution.py:695
  25.5 0.0 collective-permute-done.6.other
  25.5 0.0 copy-done.1
  25.5 0.0 copy-done.2
  25.5 15.3 %solve.1 = (f32[4,256,256]{2,1,0:T(8,128)}, f32[4,128,256]{2,1,0:T(8,128)S(1)}) custom-call(f32[4,448,128]{2,1,0:T(8,128)S(1)} %get-tuple-element.35.own, f32[4,448,128]{2,1,0:T(8,128)} %collective-permute-done.6.other, f32[2880,128]{1,0:T(8,128)S(1)} %stack.1.now_in, f32[40,128]{1,0:T(8,128)S(1)} %pad_maximum_fusion.flow, s32[8]{0:T(128)S(1)} %copy-done.1, ...), custom_call_target="tpu_custom_call" | custom-call | tf_op jit(solution)/shard_map/solve/pallas_call | solution.py:706
  40.8 0.2 collective-permute-start.7
  41.0 1.8 %collective-permute-done.7.received = f32[4,128,256]{2,1,0:T(8,128)S(1)} collective-permute-done((f32[4,128,256]{2,1,0:T(8,128)S(1)}, f32[4,128,256]{2,1,0:T(8,128)S(1)}, u32[]{:S(2)}, u32[]{:S(2)}) %collective-permute-start.7) | collective-permute-done | bytes 524320 | tf_op jit(solution)/shard_map/ppermute | solution.py:724
  42.8 0.8 %place.1 = f32[4,256,256]{2,1,0:T(8,128)} custom-call(f32[4,128,256]{2,1,0:T(8,128)S(1)} %collective-permute-done.7.received, f32[4,256,256]{2,1,0:T(8,128)} %get-tuple-element.40.t_in), custom_call_target="tpu_custom_call", output_to_operand_aliasing={{}: (1, {})} | custom-call | tf_op jit(solution)/shard_map/place/pallas_call | solution.py:725
  (2 shorter events, 0.0 us)
Async XLA Ops:
  0.6 12.1 %copy-start = (f32[4,256,256]{2,1,0:T(8,128)S(1)}, f32[4,256,256]{2,1,0:T(8,128)}, u32[]{:S(2)}) copy-start(f32[4,256,256]{2,1,0:T(8,128)} %t_own.1) | copy-start | bytes 3145732
  0.6 4.1 %collective-permute-start = (f32[4,256,256]{2,1,0:T(8,128)}, f32[4,256,256]{2,1,0:T(8,128)S(1)}, u32[]{:S(2)}, u32[]{:S(2)}) collective-permute-start(f32[4,256,256]{2,1,0:T(8,128)} %t_own.1), channel_id=1, source_target_pairs={{0,1},{1,0},{2,3},{3,2},{4,5},{5,4},{6,7},{7,6},{8,9},{9,8},{10,11... | collective-permute-start | bytes 3145736 | tf_op jit(solution)/shard_map/ppermute | solution.py:611
  4.7 10.0 %collective-permute-start.2 = (f32[4,168,128]{2,1,0:T(8,128)S(1)}, f32[4,168,128]{2,1,0:T(8,128)S(1)}, u32[]{:S(2)}, u32[]{:S(2)}) collective-permute-start(f32[4,168,128]{2,1,0:T(8,128)S(1)} %get-tuple-element.29), channel_id=1, source_target_pairs={{0,4},{2,6},{4,0},{6,2},{8,12},{10,14},{12,8},{14,10},{1,5},{3,7},... | collective-permute-start | bytes 1032200 | tf_op jit(solution)/shard_map/ppermute | solution.py:647
  6.1 13.5 %collective-permute-start.1 = (f32[4,168,128]{2,1,0:T(8,128)S(1)}, f32[4,168,128]{2,1,0:T(8,128)S(1)}, u32[]{:S(2)}, u32[]{:S(2)}) collective-permute-start(f32[4,168,128]{2,1,0:T(8,128)S(1)} %get-tuple-element.28), channel_id=1, source_target_pairs={{0,2},{2,0},{4,6},{6,4},{8,10},{10,8},{12,14},{14,12},{1,3},{3,1},... | collective-permute-start | bytes 1032200 | tf_op jit(solution)/shard_map/ppermute | solution.py:647
  7.3 12.3 %collective-permute-start.3 = (f32[4,168,128]{2,1,0:T(8,128)S(1)}, f32[4,168,128]{2,1,0:T(8,128)S(1)}, u32[]{:S(2)}, u32[]{:S(2)}) collective-permute-start(f32[4,168,128]{2,1,0:T(8,128)S(1)} %get-tuple-element.32), channel_id=1, source_target_pairs={{4,8},{6,10},{8,4},{10,6},{5,9},{7,11},{9,5},{11,7},{20,24},{22,26... | collective-permute-start | bytes 1032200 | tf_op jit(solution)/shard_map/ppermute | solution.py:647
  9.2 7.8 %collective-permute-start.4 = (f32[4,40,128]{2,1,0:T(8,128)S(1)}, f32[4,40,128]{2,1,0:T(8,128)S(1)}, u32[]{:S(2)}, u32[]{:S(2)}) collective-permute-start(f32[4,40,128]{2,1,0:T(8,128)S(1)} %get-tuple-element.33), channel_id=1, source_target_pairs={{0,6},{2,4},{4,2},{6,0},{8,14},{10,12},{12,10},{14,8},{1,7},{3,5},... | collective-permute-start | bytes 245768 | tf_op jit(solution)/shard_map/ppermute | solution.py:647
  9.3 10.3 %collective-permute-start.5 = (f32[4,40,128]{2,1,0:T(8,128)S(1)}, f32[4,40,128]{2,1,0:T(8,128)S(1)}, u32[]{:S(2)}, u32[]{:S(2)}) collective-permute-start(f32[4,40,128]{2,1,0:T(8,128)S(1)} %get-tuple-element.34), channel_id=1, source_target_pairs={{4,10},{6,8},{8,6},{10,4},{5,11},{7,9},{9,7},{11,5},{20,26},{22,24... | collective-permute-start | bytes 245768 | tf_op jit(solution)/shard_map/ppermute | solution.py:647
  19.6 3.3 %copy-start.3 = (s32[8,512]{1,0:T(8,128)S(1)}, s32[8,512]{1,0:T(8,128)}, u32[]{:S(2)}) copy-start(s32[8,512]{1,0:T(8,128)} %param.9) | copy-start | bytes 49156
  21.1 4.4 %collective-permute-start.6 = (f32[4,448,128]{2,1,0:T(8,128)S(1)}, f32[4,448,128]{2,1,0:T(8,128)}, u32[]{:S(2)}, u32[]{:S(2)}) collective-permute-start(f32[4,448,128]{2,1,0:T(8,128)S(1)} %get-tuple-element.36.other), channel_id=1, source_target_pairs={{0,1},{1,0},{2,3},{3,2},{4,5},{5,4},{6,7},{7,6},{8,9},{9,8},{10,11... | collective-permute-start | bytes 2752520 | tf_op jit(solution)/shard_map/ppermute | solution.py:693
  23.6 1.9 %copy-start.1 = (s32[8]{0:T(128)S(1)}, s32[8]{0:T(128)}, u32[]{:S(2)}) copy-start(s32[8]{0:T(128)} %material.1) | copy-start | bytes 100
  23.6 1.9 %copy-start.2 = (f32[4]{0:T(128)S(1)}, f32[4]{0:T(128)}, u32[]{:S(2)}) copy-start(f32[4]{0:T(128)} %conductivity.1) | copy-start | bytes 52
  40.8 2.0 %collective-permute-start.7 = (f32[4,128,256]{2,1,0:T(8,128)S(1)}, f32[4,128,256]{2,1,0:T(8,128)S(1)}, u32[]{:S(2)}, u32[]{:S(2)}) collective-permute-start(f32[4,128,256]{2,1,0:T(8,128)S(1)} %get-tuple-element.39), channel_id=1, source_target_pairs={{0,1},{1,0},{2,3},{3,2},{4,5},{5,4},{6,7},{7,6},{8,9},{9,8},{10,11... | collective-permute-start | bytes 1572872 | tf_op jit(solution)/shard_map/ppermute | solution.py:724

commit v7 on v6

--- a/solution.py
+++ b/solution.py
@@ -370,7 +370,7 @@
     group_cells(load, now, permutation())
 
 
-def solve_kernel(bounds, own, other, now_in, flow, material, conductivity, t_out, sent, *refs):
+def solve_kernel(bounds, own, other, now_in, flow, material, conductivity, kept, sent, *refs):
     cells, rows_t, heat, now, later, cond, f_down, f_right, f_above, inverse, base, t_stage, in_sems, sems = refs
     core = lax.axis_index("ta")
     gx, gy = lax.axis_index("gx"), lax.axis_index("gy")
@@ -389,6 +389,14 @@
     ]
     for copy in incoming:
         copy.start()
+
+    @pl.loop(0, STEP_ROWS // 14)
+    def _(block):
+        for part in range(14):
+            for col in range(4):
+                where = at(block * 14 + part + 1, col)
+                now[where, :] = now_in[where, :]
+
     for copy in incoming:
         copy.wait()
     flat = cells.reshape(layers * SWAP, LANES)
@@ -407,11 +415,9 @@
     def outputs():
         mine = t_stage.at[pl.ds(core * depth, depth)]
         theirs = t_stage.at[pl.ds((1 - core) * depth, depth)]
-        half = t_stage.shape[1]
-        place = pl.ds(pl.multiple_of(core * half, half), half)
         return (
             pltpu.make_async_copy(theirs, sent, sems.at[0]),
-            pltpu.make_async_copy(mine, t_out.at[:, place, :], sems.at[1]),
+            pltpu.make_async_copy(mine, kept, sems.at[1]),
         )
 
     group_cells(lambda row, half: across(half * HALF_ROWS + 2 + row), heat, permutation(shift=64))
@@ -437,9 +443,6 @@
             upper_lanes = jnp.where(lane < 64 + WIDE, first_turned, first)
             lower_lanes = jnp.where(lane < WIDE, second, second_turned)
             now[at(step + 1, 4), :] = jnp.where(halo_lanes, jnp.where(low, lower_lanes, upper_lanes), 0.0)
-            for col in range(4):
-                now[at(step + 1, col), :] = now_in[at(step + 1, col), :]
-
     @pl.when(core == 0)
     def _():
         for row in range(6):
@@ -537,7 +540,7 @@
         for col in range(5):
             f_down[at(0, col), :] = 0.5 * (cond[at(0, col), :] + cond[at(1, col), :])
 
-    def sweep(src, dst):
+    def sweep(src, dst, cols=5):
         @pl.loop(0, STEP_ROWS // SPAN)
         def _(block):
             start = block * SPAN
@@ -548,7 +551,7 @@
                 face_right = [f_right[at(start + part + 1, col), :] for col in range(5)]
                 rights = to_right(here)
                 lefts = to_left([face * value for face, value in zip(face_right, here)])
-                for col in range(5):
+                for col in range(cols):
                     where = at(start + part + 1, col)
                     face_above = f_above[where, :]
                     total = base[where, :] + (faces[part][col] + flows[col]) * up[col]
@@ -557,14 +560,15 @@
                     total = total + (face_above * upper(here[col]) + lower(face_above * here[col]))
                     dst[where, :] = total * inverse[where, :]
 
-        ghosts(dst)
+        if cols == 5:
+            ghosts(dst)
 
     ghosts(now)
-    for _ in range(STEPS):
+    for step in range(STEPS):
         conductances(now)
         coefficients(now)
-        for _ in range(SWEEPS):
-            sweep(now, later)
+        for turn_of in range(SWEEPS):
+            sweep(now, later, 4 if (step, turn_of) == (STEPS - 1, SWEEPS - 1) else 5)
             now, later = later, now
 
     back = permutation(inverse=True)
@@ -589,11 +593,11 @@
         copy.wait()
 
 
-def place_kernel(received, t_in, t_out, sem):
-    core = lax.axis_index("ta")
-    half = received.shape[1]
-    place = pl.ds(pl.multiple_of((1 - core) * half, half), half)
-    copy = pltpu.make_async_copy(received, t_out.at[:, place, :], sem)
+def place_kernel(mine, part, *refs):
+    t_out, sem = refs[-2:]
+    core = lax.axis_index("ta") if mine else 1 - lax.axis_index("ta")
+    half = part.shape[1]
+    copy = pltpu.make_async_copy(part, t_out.at[:, pl.ds(pl.multiple_of(core * half, half), half), :], sem)
     copy.start()
     copy.wait()
 
@@ -703,9 +707,9 @@
 
     received, heat_source = lax.optimization_barrier((received, heat_source))
     work = pltpu.VMEM(grouped.shape, F32)
-    t_part, sent = pl.pallas_call(
+    kept, sent = pl.pallas_call(
         functools.partial(solve_kernel, (n_gx * rows, n_gy * cols)),
-        out_shape=(whole, array((depth, rows // 2, cols), F32)),
+        out_shape=(array((depth, rows // 2, cols), F32),) * 2,
         in_specs=[ANY, ANY] + [VMEM] * 2 + [SMEM, SMEM],
         out_specs=(ANY, ANY),
         scratch_shapes=[
@@ -722,16 +726,20 @@
         name="solve",
     )(own, received, now, flow, material, conductivity)
     received = lax.ppermute(sent, "ta", swap)
-    temperature = pl.pallas_call(
-        place_kernel,
-        out_shape=whole,
-        in_specs=[ANY, ANY],
-        out_specs=ANY,
-        scratch_shapes=[pltpu.SemaphoreType.DMA],
-        input_output_aliases={1: 0},
-        compiler_params=params(4),
-        name="place",
-    )(received, t_part)
+
+    def place(mine, part, *whole_in):
+        return pl.pallas_call(
+            functools.partial(place_kernel, mine),
+            out_shape=whole,
+            in_specs=[ANY] * (1 + len(whole_in)),
+            out_specs=ANY,
+            scratch_shapes=[pltpu.SemaphoreType.DMA],
+            input_output_aliases={1: 0} if whole_in else {},
+            compiler_params=params(4),
+            name="keep" if mine else "place",
+        )(part, *whole_in)
+
+    temperature = place(False, received, place(True, kept))
     return temperature, heat_source
 
 

time: 43.8 us -> 42.8 us (0.977)
  waiting for transfers between devices: 6.75 us -> 5.94 us
    pallas_call x1, Pallas kernels: 15.3 us -> 14.4 us  [on_device(): pl.pallas_call(functools.partial(solve_kernel, (n_gx * rows, n_gy * cols)...]
    ppermute x1, waiting for transfers between devices: 1.81 us -> 1 us  [on_device(): received = lax.ppermute(sent, 'ta', swap)]
    pallas_call x1 -> x2, Pallas kernels: 0.8 us -> 1.6 us  [place(): pl.pallas_call(functools.partial(place_kernel, mine), out_shape=whole, in...]
  transfers between devices with their start and end apart: 8 -> 8, of which waited for: 3 -> 3; matrix products, arithmetic and copies ran while one was open for 2% -> 2% of each run, Pallas kernels for 9% -> 11%
where the time goes in v7:
time: 42.8 us; the launch traced here: 42.6 us
  Pallas kernels  24.5 us (57%)
  starting transfers between devices  10.7 us (25%)
  waiting for transfers between devices  5.94 us (14%)
  between operations  0.76 us (2%)
  local copies, waits for them, and re-layouts  0.45 us (1%)
    pallas_call x1, Pallas kernels, on_device(): pl.pallas_call(functools.partial(solve_kernel, (n_gx * rows, n_gy * cols)...  14.4 us
    ppermute x5, starting transfers between devices, move(): return lax.ppermute(value, ('gx', 'gy'), pairs)  7.92 us
    ppermute x5, waiting for transfers between devices, move(): return lax.ppermute(value, ('gx', 'gy'), pairs)  4.94 us
    pallas_call x1, Pallas kernels, on_device(): pl.pallas_call(functools.partial(send_kernel, out_sides), out_shape=(plai...  3.34 us
    pallas_call x1, Pallas kernels, on_device(): pl.pallas_call(stack_kernel, out_shape=grouped, in_specs=[ANY] * 2, out_s...  1.99 us
    ppermute x1, starting transfers between devices, on_device(): received = lax.ppermute(other, 'ta', swap)  1.86 us
    pallas_call x1, Pallas kernels, on_device(): pl.pallas_call(heat_kernel, out_shape=whole, in_specs=[VMEM] * 2, out_spe...  1.78 us
    pallas_call x2, Pallas kernels, place(): pl.pallas_call(functools.partial(place_kernel, mine), out_shape=whole, in...  1.6 us
  transfers between devices with their start and end apart: 8, of which 3 were waited for; matrix products, arithmetic and copies ran while one was open for 2% of the time, Pallas kernels for 11%

profile of v7, /device:TPU:21, one launch (start us, length us, event | category | flops | bytes accessed | tf_op | source)
XLA Modules:
  0.0 42.6 jit_solution(16294472054195042795)
XLA Ops:
  0.6 0.0 copy-start
  0.6 0.7 %collective-permute-start = (f32[4,256,256]{2,1,0:T(8,128)}, f32[4,256,256]{2,1,0:T(8,128)S(1)}, u32[]{:S(2)}, u32[]{:S(2)}) collective-permute-start(f32[4,256,256]{2,1,0:T(8,128)} %t_own.1), channel_id=1, source_target_pairs={{0,1},{1,0},{2,3},{3,2},{4,5},{5,4},{6,7},{7,6},{8,9},{9,8},{10,11... | collective-permute-start | bytes 3145736 | tf_op jit(solution)/shard_map/ppermute | solution.py:615
  1.4 3.3 %send.1 = (f32[4,3,384,128]{3,2,1,0:T(8,128)S(1)}, f32[4,168,128]{2,1,0:T(8,128)S(1)}, f32[4,168,128]{2,1,0:T(8,128)S(1)}, f32[4,168,128]{2,1,0:T(8,128)S(1)}, f...) custom-call(bf16[4,384,384]{2,1,0:T(8,128)(2,1)} %mantissa_in.1, s32[6,4,6]{2,1,0:T(4,128)} %bitcast.9, ...), custom_call_target="tpu_custom_call" | custom-call | tf_op jit(solution)/shard_map/send/pallas_call | solution.py:621
  4.7 0.0 collective-permute-done.t_other
  4.7 1.4 %collective-permute-start.2 = (f32[4,168,128]{2,1,0:T(8,128)S(1)}, f32[4,168,128]{2,1,0:T(8,128)S(1)}, u32[]{:S(2)}, u32[]{:S(2)}) collective-permute-start(f32[4,168,128]{2,1,0:T(8,128)S(1)} %get-tuple-element.29), channel_id=1, source_target_pairs={{0,4},{2,6},{4,0},{6,2},{8,12},{10,14},{12,8},{14,10},{1,5},{3,7},... | collective-permute-start | bytes 1032200 | tf_op jit(solution)/shard_map/ppermute | solution.py:651
  6.1 1.2 %collective-permute-start.1 = (f32[4,168,128]{2,1,0:T(8,128)S(1)}, f32[4,168,128]{2,1,0:T(8,128)S(1)}, u32[]{:S(2)}, u32[]{:S(2)}) collective-permute-start(f32[4,168,128]{2,1,0:T(8,128)S(1)} %get-tuple-element.28), channel_id=1, source_target_pairs={{0,2},{2,0},{4,6},{6,4},{8,10},{10,8},{12,14},{14,12},{1,3},{3,1},... | collective-permute-start | bytes 1032200 | tf_op jit(solution)/shard_map/ppermute | solution.py:651
  7.3 1.9 %collective-permute-start.3 = (f32[4,168,128]{2,1,0:T(8,128)S(1)}, f32[4,168,128]{2,1,0:T(8,128)S(1)}, u32[]{:S(2)}, u32[]{:S(2)}) collective-permute-start(f32[4,168,128]{2,1,0:T(8,128)S(1)} %get-tuple-element.32), channel_id=1, source_target_pairs={{4,8},{6,10},{8,4},{10,6},{5,9},{7,11},{9,5},{11,7},{20,24},{22,26... | collective-permute-start | bytes 1032200 | tf_op jit(solution)/shard_map/ppermute | solution.py:651
  9.2 0.1 collective-permute-start.4
  9.3 3.4 %collective-permute-start.5 = (f32[4,40,128]{2,1,0:T(8,128)S(1)}, f32[4,40,128]{2,1,0:T(8,128)S(1)}, u32[]{:S(2)}, u32[]{:S(2)}) collective-permute-start(f32[4,40,128]{2,1,0:T(8,128)S(1)} %get-tuple-element.34), channel_id=1, source_target_pairs={{4,10},{6,8},{8,6},{10,4},{5,11},{7,9},{9,7},{11,5},{20,26},{22,24... | collective-permute-start | bytes 245768 | tf_op jit(solution)/shard_map/ppermute | solution.py:651
  12.7 0.0 copy-done
  12.7 2.0 %stack.1.now_in = f32[2880,128]{1,0:T(8,128)S(1)} custom-call(f32[4,256,256]{2,1,0:T(8,128)S(1)} %copy-done, f32[4,256,256]{2,1,0:T(8,128)S(1)} %collective-permute-done.t_other), custom_call_target="tpu_custom_call" | custom-call | tf_op jit(solution)/shard_map/stack/pallas_call | solution.py:669
  14.7 0.0 collective-permute-done.2.refs_2_
  14.7 2.4 %collective-permute-done.4.refs_4_ = f32[4,40,128]{2,1,0:T(8,128)S(1)} collective-permute-done((f32[4,40,128]{2,1,0:T(8,128)S(1)}, f32[4,40,128]{2,1,0:T(8,128)S(1)}, u32[]{:S(2)}, u32[]{:S(2)}) %collective-permute-start.4) | collective-permute-done | bytes 81952 | tf_op jit(solution)/shard_map/ppermute | solution.py:651
  17.1 2.5 %collective-permute-done.5.refs_5_ = f32[4,40,128]{2,1,0:T(8,128)S(1)} collective-permute-done((f32[4,40,128]{2,1,0:T(8,128)S(1)}, f32[4,40,128]{2,1,0:T(8,128)S(1)}, u32[]{:S(2)}, u32[]{:S(2)}) %collective-permute-start.5) | collective-permute-done | bytes 81952 | tf_op jit(solution)/shard_map/ppermute | solution.py:651
  19.6 0.0 collective-permute-done.1.refs_1_
  19.6 0.0 collective-permute-done.3.refs_3_
  19.6 0.0 copy-start.3
  19.6 1.5 %sum.1 = (f32[4,448,128]{2,1,0:T(8,128)S(1)}, f32[4,448,128]{2,1,0:T(8,128)S(1)}) custom-call(f32[4,3,384,128]{3,2,1,0:T(8,128)S(1)} %get-tuple-element.22.refs_0_, f32[4,168,128]{2,1,0:T(8,128)S(1)} %collective-permute-done.1.refs_1_, f32[4,168,128]{2,1,0:T(8,128)S(1)} %collective-permute-done.2.refs_2_, f32[4,168,128]{2,1,0:T(8,128)S(1)} %collective-permute-done.3.refs_3_, ...), custom_call_target="tpu_custom_call" | custom-call | tf_op jit(solution)/shard_map/sum/pallas_call | solution.py:684
  21.1 1.9 %collective-permute-start.6 = (f32[4,448,128]{2,1,0:T(8,128)S(1)}, f32[4,448,128]{2,1,0:T(8,128)}, u32[]{:S(2)}, u32[]{:S(2)}) collective-permute-start(f32[4,448,128]{2,1,0:T(8,128)S(1)} %get-tuple-element.36.other), channel_id=1, source_target_pairs={{0,1},{1,0},{2,3},{3,2},{4,5},{5,4},{6,7},{7,6},{8,9},{9,8},{10,11... | collective-permute-start | bytes 2752520 | tf_op jit(solution)/shard_map/ppermute | solution.py:697
  23.0 0.0 copy-done.3
  23.0 0.1 fusion.1
  23.1 0.1 slice.14
  23.1 0.1 copy.12
  23.3 0.1 copy.13
  23.3 0.1 pad.10.clone
  23.4 0.1 fusion.2
  23.5 0.1 maximum_bitcast_fusion.1
  23.6 0.0 copy-start.1
  23.6 0.0 copy-start.2
  23.6 0.1 pad_maximum_fusion.flow
  23.7 1.8 %heat.1 = f32[4,256,256]{2,1,0:T(8,128)} custom-call(f32[4,448,128]{2,1,0:T(8,128)S(1)} %get-tuple-element.35.own, f32[4,448,128]{2,1,0:T(8,128)S(1)} %get-tuple-element.36.other), custom_call_target="tpu_custom_call" | custom-call | tf_op jit(solution)/shard_map/heat/pallas_call | solution.py:699
  25.5 0.0 collective-permute-done.6.other
  25.5 0.0 copy-done.1
  25.5 0.0 copy-done.2
  25.5 14.4 %solve.1 = (f32[4,128,256]{2,1,0:T(8,128)S(1)}, f32[4,128,256]{2,1,0:T(8,128)S(1)}) custom-call(f32[4,448,128]{2,1,0:T(8,128)S(1)} %get-tuple-element.35.own, f32[4,448,128]{2,1,0:T(8,128)} %collective-permute-done.6.other, f32[2880,128]{1,0:T(8,128)S(1)} %stack.1.now_in, f32[40,128]{1,0:T(8,128)S(1)} %pad_maximum_fusion.flow, s32[8]{0:T(128)S(1)} %copy-done.1, ...), custom_call_target="tpu_custom_call" | custom-call | tf_op jit(solution)/shard_map/solve/pallas_call | solution.py:710
  39.9 0.2 collective-permute-start.7
  40.0 0.8 %keep.1.refs_0_ = f32[4,256,256]{2,1,0:T(8,128)} custom-call(f32[4,128,256]{2,1,0:T(8,128)S(1)} %get-tuple-element.40.part), custom_call_target="tpu_custom_call" | custom-call | tf_op jit(solution)/shard_map/keep/pallas_call | solution.py:731
  40.8 1.0 %collective-permute-done.7.part = f32[4,128,256]{2,1,0:T(8,128)S(1)} collective-permute-done((f32[4,128,256]{2,1,0:T(8,128)S(1)}, f32[4,128,256]{2,1,0:T(8,128)S(1)}, u32[]{:S(2)}, u32[]{:S(2)}) %collective-permute-start.7) | collective-permute-done | bytes 524320 | tf_op jit(solution)/shard_map/ppermute | solution.py:728
  41.8 0.8 %place.1 = f32[4,256,256]{2,1,0:T(8,128)} custom-call(f32[4,128,256]{2,1,0:T(8,128)S(1)} %collective-permute-done.7.part, f32[4,256,256]{2,1,0:T(8,128)} %keep.1.refs_0_), custom_call_target="tpu_custom_call", output_to_operand_aliasing={{}: (1, {})} | custom-call | tf_op jit(solution)/shard_map/place/pallas_call | solution.py:731
  (2 shorter events, 0.0 us)
Async XLA Ops:
  0.6 12.1 %copy-start = (f32[4,256,256]{2,1,0:T(8,128)S(1)}, f32[4,256,256]{2,1,0:T(8,128)}, u32[]{:S(2)}) copy-start(f32[4,256,256]{2,1,0:T(8,128)} %t_own.1) | copy-start | bytes 3145732
  0.6 4.1 %collective-permute-start = (f32[4,256,256]{2,1,0:T(8,128)}, f32[4,256,256]{2,1,0:T(8,128)S(1)}, u32[]{:S(2)}, u32[]{:S(2)}) collective-permute-start(f32[4,256,256]{2,1,0:T(8,128)} %t_own.1), channel_id=1, source_target_pairs={{0,1},{1,0},{2,3},{3,2},{4,5},{5,4},{6,7},{7,6},{8,9},{9,8},{10,11... | collective-permute-start | bytes 3145736 | tf_op jit(solution)/shard_map/ppermute | solution.py:615
  4.7 10.0 %collective-permute-start.2 = (f32[4,168,128]{2,1,0:T(8,128)S(1)}, f32[4,168,128]{2,1,0:T(8,128)S(1)}, u32[]{:S(2)}, u32[]{:S(2)}) collective-permute-start(f32[4,168,128]{2,1,0:T(8,128)S(1)} %get-tuple-element.29), channel_id=1, source_target_pairs={{0,4},{2,6},{4,0},{6,2},{8,12},{10,14},{12,8},{14,10},{1,5},{3,7},... | collective-permute-start | bytes 1032200 | tf_op jit(solution)/shard_map/ppermute | solution.py:651
  6.1 13.5 %collective-permute-start.1 = (f32[4,168,128]{2,1,0:T(8,128)S(1)}, f32[4,168,128]{2,1,0:T(8,128)S(1)}, u32[]{:S(2)}, u32[]{:S(2)}) collective-permute-start(f32[4,168,128]{2,1,0:T(8,128)S(1)} %get-tuple-element.28), channel_id=1, source_target_pairs={{0,2},{2,0},{4,6},{6,4},{8,10},{10,8},{12,14},{14,12},{1,3},{3,1},... | collective-permute-start | bytes 1032200 | tf_op jit(solution)/shard_map/ppermute | solution.py:651
  7.3 12.3 %collective-permute-start.3 = (f32[4,168,128]{2,1,0:T(8,128)S(1)}, f32[4,168,128]{2,1,0:T(8,128)S(1)}, u32[]{:S(2)}, u32[]{:S(2)}) collective-permute-start(f32[4,168,128]{2,1,0:T(8,128)S(1)} %get-tuple-element.32), channel_id=1, source_target_pairs={{4,8},{6,10},{8,4},{10,6},{5,9},{7,11},{9,5},{11,7},{20,24},{22,26... | collective-permute-start | bytes 1032200 | tf_op jit(solution)/shard_map/ppermute | solution.py:651
  9.2 7.8 %collective-permute-start.4 = (f32[4,40,128]{2,1,0:T(8,128)S(1)}, f32[4,40,128]{2,1,0:T(8,128)S(1)}, u32[]{:S(2)}, u32[]{:S(2)}) collective-permute-start(f32[4,40,128]{2,1,0:T(8,128)S(1)} %get-tuple-element.33), channel_id=1, source_target_pairs={{0,6},{2,4},{4,2},{6,0},{8,14},{10,12},{12,10},{14,8},{1,7},{3,5},... | collective-permute-start | bytes 245768 | tf_op jit(solution)/shard_map/ppermute | solution.py:651
  9.3 10.3 %collective-permute-start.5 = (f32[4,40,128]{2,1,0:T(8,128)S(1)}, f32[4,40,128]{2,1,0:T(8,128)S(1)}, u32[]{:S(2)}, u32[]{:S(2)}) collective-permute-start(f32[4,40,128]{2,1,0:T(8,128)S(1)} %get-tuple-element.34), channel_id=1, source_target_pairs={{4,10},{6,8},{8,6},{10,4},{5,11},{7,9},{9,7},{11,5},{20,26},{22,24... | collective-permute-start | bytes 245768 | tf_op jit(solution)/shard_map/ppermute | solution.py:651
  19.6 3.3 %copy-start.3 = (s32[8,512]{1,0:T(8,128)S(1)}, s32[8,512]{1,0:T(8,128)}, u32[]{:S(2)}) copy-start(s32[8,512]{1,0:T(8,128)} %param.9) | copy-start | bytes 49156
  21.1 4.4 %collective-permute-start.6 = (f32[4,448,128]{2,1,0:T(8,128)S(1)}, f32[4,448,128]{2,1,0:T(8,128)}, u32[]{:S(2)}, u32[]{:S(2)}) collective-permute-start(f32[4,448,128]{2,1,0:T(8,128)S(1)} %get-tuple-element.36.other), channel_id=1, source_target_pairs={{0,1},{1,0},{2,3},{3,2},{4,5},{5,4},{6,7},{7,6},{8,9},{9,8},{10,11... | collective-permute-start | bytes 2752520 | tf_op jit(solution)/shard_map/ppermute | solution.py:697
  23.6 1.9 %copy-start.1 = (s32[8]{0:T(128)S(1)}, s32[8]{0:T(128)}, u32[]{:S(2)}) copy-start(s32[8]{0:T(128)} %material.1) | copy-start | bytes 100
  23.6 1.9 %copy-start.2 = (f32[4]{0:T(128)S(1)}, f32[4]{0:T(128)}, u32[]{:S(2)}) copy-start(f32[4]{0:T(128)} %conductivity.1) | copy-start | bytes 52
  39.9 2.0 %collective-permute-start.7 = (f32[4,128,256]{2,1,0:T(8,128)S(1)}, f32[4,128,256]{2,1,0:T(8,128)S(1)}, u32[]{:S(2)}, u32[]{:S(2)}) collective-permute-start(f32[4,128,256]{2,1,0:T(8,128)S(1)} %get-tuple-element.39), channel_id=1, source_target_pairs={{0,1},{1,0},{2,3},{3,2},{4,5},{5,4},{6,7},{7,6},{8,9},{9,8},{10,11... | collective-permute-start | bytes 1572872 | tf_op jit(solution)/shard_map/ppermute | solution.py:728

commit v8 on v7

--- a/solution.py
+++ b/solution.py
@@ -371,7 +371,7 @@
 
 
 def solve_kernel(bounds, own, other, now_in, flow, material, conductivity, kept, sent, *refs):
-    cells, rows_t, heat, now, later, cond, f_down, f_right, f_above, inverse, base, t_stage, in_sems, sems = refs
+    cells, rows_t, heat, now, later, cond, f_up, f_down, f_right, f_above, inverse, base, t_stage, in_sems, sems = refs
     core = lax.axis_index("ta")
     gx, gy = lax.axis_index("gx"), lax.axis_index("gy")
     lane = lane_ids()
@@ -529,23 +529,21 @@
                     under = centre + lower(centre) * not_bottom
                     face_down = 0.5 * (centre + down[col])
                     face_right = 0.5 * (centre + rights[col])
-                    total = (1.0 + flows[col]) + 0.5 * (centre + up[col]) + face_down
+                    face_up = 0.5 * (centre + up[col]) + flows[col]
+                    total = 1.0 + face_up + face_down
                     total = total + face_right + 0.5 * (centre + lefts[col]) + over + under
+                    f_up[where, :] = face_up
                     f_down[where, :] = face_down
                     f_right[where, :] = face_right
                     f_above[where, :] = over * not_top
                     inverse[where, :] = mask[col] / total
                     base[where, :] = src[where, :] + heat[where, :]
 
-        for col in range(5):
-            f_down[at(0, col), :] = 0.5 * (cond[at(0, col), :] + cond[at(1, col), :])
-
     def sweep(src, dst, cols=5):
         @pl.loop(0, STEP_ROWS // SPAN)
         def _(block):
             start = block * SPAN
             lines = [[src[at(start + part, col), :] for col in range(5)] for part in range(SPAN + 2)]
-            faces = [[f_down[at(start + part, col), :] for col in range(5)] for part in range(SPAN + 1)]
             for part in range(SPAN):
                 up, here, down = lines[part], lines[part + 1], lines[part + 2]
                 face_right = [f_right[at(start + part + 1, col), :] for col in range(5)]
@@ -554,8 +552,8 @@
                 for col in range(cols):
                     where = at(start + part + 1, col)
                     face_above = f_above[where, :]
-                    total = base[where, :] + (faces[part][col] + flows[col]) * up[col]
-                    total = total + faces[part + 1][col] * down[col]
+                    total = base[where, :] + f_up[where, :] * up[col]
+                    total = total + f_down[where, :] * down[col]
                     total = total + (face_right[col] * rights[col] + lefts[col])
                     total = total + (face_above * upper(here[col]) + lower(face_above * here[col]))
                     dst[where, :] = total * inverse[where, :]
@@ -716,7 +714,7 @@
             pltpu.VMEM((layers, SWAP, LANES), F32),
             pltpu.VMEM((2, REGION * 8, LANES), F32),
         ]
-        + [work] * 9
+        + [work] * 10
         + [
             pltpu.VMEM((layers, rows // 2, cols), F32),
             pltpu.SemaphoreType.DMA((2,)),

time: 42.8 us -> 42.6 us (level)
  no operation moved by 1% of the time
where the time goes in v8:
time: 42.6 us; the launch traced here: 42.4 us
  Pallas kernels  24.3 us (57%)
  starting transfers between devices  10.7 us (25%)
  waiting for transfers between devices  5.94 us (14%)
  between operations  0.76 us (2%)
  local copies, waits for them, and re-layouts  0.45 us (1%)
    pallas_call x1, Pallas kernels, on_device(): pl.pallas_call(functools.partial(solve_kernel, (n_gx * rows, n_gy * cols)...  14.1 us
    ppermute x5, starting transfers between devices, move(): return lax.ppermute(value, ('gx', 'gy'), pairs)  7.92 us
    ppermute x5, waiting for transfers between devices, move(): return lax.ppermute(value, ('gx', 'gy'), pairs)  4.94 us
    pallas_call x1, Pallas kernels, on_device(): pl.pallas_call(functools.partial(send_kernel, out_sides), out_shape=(plai...  3.34 us
    pallas_call x1, Pallas kernels, on_device(): pl.pallas_call(stack_kernel, out_shape=grouped, in_specs=[ANY] * 2, out_s...  1.99 us
    ppermute x1, starting transfers between devices, on_device(): received = lax.ppermute(other, 'ta', swap)  1.86 us
    pallas_call x1, Pallas kernels, on_device(): pl.pallas_call(heat_kernel, out_shape=whole, in_specs=[VMEM] * 2, out_spe...  1.78 us
    pallas_call x2, Pallas kernels, place(): pl.pallas_call(functools.partial(place_kernel, mine), out_shape=whole, in...  1.6 us
  transfers between devices with their start and end apart: 8, of which 3 were waited for; matrix products, arithmetic and copies ran while one was open for 2% of the time, Pallas kernels for 11%

profile of v8, /device:TPU:21, one launch (start us, length us, event | category | flops | bytes accessed | tf_op | source)
XLA Modules:
  0.0 42.4 jit_solution(9933514657974899016)
XLA Ops:
  0.6 0.0 copy-start
  0.6 0.7 %collective-permute-start = (f32[4,256,256]{2,1,0:T(8,128)}, f32[4,256,256]{2,1,0:T(8,128)S(1)}, u32[]{:S(2)}, u32[]{:S(2)}) collective-permute-start(f32[4,256,256]{2,1,0:T(8,128)} %t_own.1), channel_id=1, source_target_pairs={{0,1},{1,0},{2,3},{3,2},{4,5},{5,4},{6,7},{7,6},{8,9},{9,8},{10,11... | collective-permute-start | bytes 3145736 | tf_op jit(solution)/shard_map/ppermute | solution.py:613
  1.4 3.3 %send.1 = (f32[4,3,384,128]{3,2,1,0:T(8,128)S(1)}, f32[4,168,128]{2,1,0:T(8,128)S(1)}, f32[4,168,128]{2,1,0:T(8,128)S(1)}, f32[4,168,128]{2,1,0:T(8,128)S(1)}, f...) custom-call(bf16[4,384,384]{2,1,0:T(8,128)(2,1)} %mantissa_in.1, s32[6,4,6]{2,1,0:T(4,128)} %bitcast.9, ...), custom_call_target="tpu_custom_call" | custom-call | tf_op jit(solution)/shard_map/send/pallas_call | solution.py:619
  4.7 0.0 collective-permute-done.t_other
  4.7 1.4 %collective-permute-start.2 = (f32[4,168,128]{2,1,0:T(8,128)S(1)}, f32[4,168,128]{2,1,0:T(8,128)S(1)}, u32[]{:S(2)}, u32[]{:S(2)}) collective-permute-start(f32[4,168,128]{2,1,0:T(8,128)S(1)} %get-tuple-element.29), channel_id=1, source_target_pairs={{0,4},{2,6},{4,0},{6,2},{8,12},{10,14},{12,8},{14,10},{1,5},{3,7},... | collective-permute-start | bytes 1032200 | tf_op jit(solution)/shard_map/ppermute | solution.py:649
  6.1 1.2 %collective-permute-start.1 = (f32[4,168,128]{2,1,0:T(8,128)S(1)}, f32[4,168,128]{2,1,0:T(8,128)S(1)}, u32[]{:S(2)}, u32[]{:S(2)}) collective-permute-start(f32[4,168,128]{2,1,0:T(8,128)S(1)} %get-tuple-element.28), channel_id=1, source_target_pairs={{0,2},{2,0},{4,6},{6,4},{8,10},{10,8},{12,14},{14,12},{1,3},{3,1},... | collective-permute-start | bytes 1032200 | tf_op jit(solution)/shard_map/ppermute | solution.py:649
  7.3 1.9 %collective-permute-start.3 = (f32[4,168,128]{2,1,0:T(8,128)S(1)}, f32[4,168,128]{2,1,0:T(8,128)S(1)}, u32[]{:S(2)}, u32[]{:S(2)}) collective-permute-start(f32[4,168,128]{2,1,0:T(8,128)S(1)} %get-tuple-element.32), channel_id=1, source_target_pairs={{4,8},{6,10},{8,4},{10,6},{5,9},{7,11},{9,5},{11,7},{20,24},{22,26... | collective-permute-start | bytes 1032200 | tf_op jit(solution)/shard_map/ppermute | solution.py:649
  9.2 0.1 collective-permute-start.4
  9.3 3.4 %collective-permute-start.5 = (f32[4,40,128]{2,1,0:T(8,128)S(1)}, f32[4,40,128]{2,1,0:T(8,128)S(1)}, u32[]{:S(2)}, u32[]{:S(2)}) collective-permute-start(f32[4,40,128]{2,1,0:T(8,128)S(1)} %get-tuple-element.34), channel_id=1, source_target_pairs={{4,10},{6,8},{8,6},{10,4},{5,11},{7,9},{9,7},{11,5},{20,26},{22,24... | collective-permute-start | bytes 245768 | tf_op jit(solution)/shard_map/ppermute | solution.py:649
  12.7 0.0 copy-done
  12.7 2.0 %stack.1.now_in = f32[2880,128]{1,0:T(8,128)S(1)} custom-call(f32[4,256,256]{2,1,0:T(8,128)S(1)} %copy-done, f32[4,256,256]{2,1,0:T(8,128)S(1)} %collective-permute-done.t_other), custom_call_target="tpu_custom_call" | custom-call | tf_op jit(solution)/shard_map/stack/pallas_call | solution.py:667
  14.7 0.0 collective-permute-done.2.refs_2_
  14.7 2.4 %collective-permute-done.4.refs_4_ = f32[4,40,128]{2,1,0:T(8,128)S(1)} collective-permute-done((f32[4,40,128]{2,1,0:T(8,128)S(1)}, f32[4,40,128]{2,1,0:T(8,128)S(1)}, u32[]{:S(2)}, u32[]{:S(2)}) %collective-permute-start.4) | collective-permute-done | bytes 81952 | tf_op jit(solution)/shard_map/ppermute | solution.py:649
  17.1 2.5 %collective-permute-done.5.refs_5_ = f32[4,40,128]{2,1,0:T(8,128)S(1)} collective-permute-done((f32[4,40,128]{2,1,0:T(8,128)S(1)}, f32[4,40,128]{2,1,0:T(8,128)S(1)}, u32[]{:S(2)}, u32[]{:S(2)}) %collective-permute-start.5) | collective-permute-done | bytes 81952 | tf_op jit(solution)/shard_map/ppermute | solution.py:649
  19.6 0.0 collective-permute-done.1.refs_1_
  19.6 0.0 collective-permute-done.3.refs_3_
  19.6 0.0 copy-start.3
  19.6 1.5 %sum.1 = (f32[4,448,128]{2,1,0:T(8,128)S(1)}, f32[4,448,128]{2,1,0:T(8,128)S(1)}) custom-call(f32[4,3,384,128]{3,2,1,0:T(8,128)S(1)} %get-tuple-element.22.refs_0_, f32[4,168,128]{2,1,0:T(8,128)S(1)} %collective-permute-done.1.refs_1_, f32[4,168,128]{2,1,0:T(8,128)S(1)} %collective-permute-done.2.refs_2_, f32[4,168,128]{2,1,0:T(8,128)S(1)} %collective-permute-done.3.refs_3_, ...), custom_call_target="tpu_custom_call" | custom-call | tf_op jit(solution)/shard_map/sum/pallas_call | solution.py:682
  21.1 1.9 %collective-permute-start.6 = (f32[4,448,128]{2,1,0:T(8,128)S(1)}, f32[4,448,128]{2,1,0:T(8,128)}, u32[]{:S(2)}, u32[]{:S(2)}) collective-permute-start(f32[4,448,128]{2,1,0:T(8,128)S(1)} %get-tuple-element.36.other), channel_id=1, source_target_pairs={{0,1},{1,0},{2,3},{3,2},{4,5},{5,4},{6,7},{7,6},{8,9},{9,8},{10,11... | collective-permute-start | bytes 2752520 | tf_op jit(solution)/shard_map/ppermute | solution.py:695
  23.0 0.0 copy-done.3
  23.0 0.1 fusion.1
  23.1 0.1 slice.14
  23.1 0.1 copy.12
  23.3 0.1 copy.13
  23.3 0.1 pad.10.clone
  23.4 0.1 fusion.2
  23.5 0.1 maximum_bitcast_fusion.1
  23.6 0.0 copy-start.1
  23.6 0.0 copy-start.2
  23.6 0.1 pad_maximum_fusion.flow
  23.7 1.8 %heat.1 = f32[4,256,256]{2,1,0:T(8,128)} custom-call(f32[4,448,128]{2,1,0:T(8,128)S(1)} %get-tuple-element.35.own, f32[4,448,128]{2,1,0:T(8,128)S(1)} %get-tuple-element.36.other), custom_call_target="tpu_custom_call" | custom-call | tf_op jit(solution)/shard_map/heat/pallas_call | solution.py:697
  25.5 0.0 collective-permute-done.6.other
  25.5 0.0 copy-done.1
  25.5 0.0 copy-done.2
  25.5 14.1 %solve.1 = (f32[4,128,256]{2,1,0:T(8,128)S(1)}, f32[4,128,256]{2,1,0:T(8,128)S(1)}) custom-call(f32[4,448,128]{2,1,0:T(8,128)S(1)} %get-tuple-element.35.own, f32[4,448,128]{2,1,0:T(8,128)} %collective-permute-done.6.other, f32[2880,128]{1,0:T(8,128)S(1)} %stack.1.now_in, f32[40,128]{1,0:T(8,128)S(1)} %pad_maximum_fusion.flow, s32[8]{0:T(128)S(1)} %copy-done.1, ...), custom_call_target="tpu_custom_call" | custom-call | tf_op jit(solution)/shard_map/solve/pallas_call | solution.py:708
  39.6 0.2 collective-permute-start.7
  39.8 0.8 %keep.1.refs_0_ = f32[4,256,256]{2,1,0:T(8,128)} custom-call(f32[4,128,256]{2,1,0:T(8,128)S(1)} %get-tuple-element.40.part), custom_call_target="tpu_custom_call" | custom-call | tf_op jit(solution)/shard_map/keep/pallas_call | solution.py:729
  40.6 1.0 %collective-permute-done.7.part = f32[4,128,256]{2,1,0:T(8,128)S(1)} collective-permute-done((f32[4,128,256]{2,1,0:T(8,128)S(1)}, f32[4,128,256]{2,1,0:T(8,128)S(1)}, u32[]{:S(2)}, u32[]{:S(2)}) %collective-permute-start.7) | collective-permute-done | bytes 524320 | tf_op jit(solution)/shard_map/ppermute | solution.py:726
  41.6 0.8 %place.1 = f32[4,256,256]{2,1,0:T(8,128)} custom-call(f32[4,128,256]{2,1,0:T(8,128)S(1)} %collective-permute-done.7.part, f32[4,256,256]{2,1,0:T(8,128)} %keep.1.refs_0_), custom_call_target="tpu_custom_call", output_to_operand_aliasing={{}: (1, {})} | custom-call | tf_op jit(solution)/shard_map/place/pallas_call | solution.py:729
  (2 shorter events, 0.0 us)
Async XLA Ops:
  0.6 12.1 %copy-start = (f32[4,256,256]{2,1,0:T(8,128)S(1)}, f32[4,256,256]{2,1,0:T(8,128)}, u32[]{:S(2)}) copy-start(f32[4,256,256]{2,1,0:T(8,128)} %t_own.1) | copy-start | bytes 3145732
  0.6 4.1 %collective-permute-start = (f32[4,256,256]{2,1,0:T(8,128)}, f32[4,256,256]{2,1,0:T(8,128)S(1)}, u32[]{:S(2)}, u32[]{:S(2)}) collective-permute-start(f32[4,256,256]{2,1,0:T(8,128)} %t_own.1), channel_id=1, source_target_pairs={{0,1},{1,0},{2,3},{3,2},{4,5},{5,4},{6,7},{7,6},{8,9},{9,8},{10,11... | collective-permute-start | bytes 3145736 | tf_op jit(solution)/shard_map/ppermute | solution.py:613
  4.7 10.0 %collective-permute-start.2 = (f32[4,168,128]{2,1,0:T(8,128)S(1)}, f32[4,168,128]{2,1,0:T(8,128)S(1)}, u32[]{:S(2)}, u32[]{:S(2)}) collective-permute-start(f32[4,168,128]{2,1,0:T(8,128)S(1)} %get-tuple-element.29), channel_id=1, source_target_pairs={{0,4},{2,6},{4,0},{6,2},{8,12},{10,14},{12,8},{14,10},{1,5},{3,7},... | collective-permute-start | bytes 1032200 | tf_op jit(solution)/shard_map/ppermute | solution.py:649
  6.1 13.5 %collective-permute-start.1 = (f32[4,168,128]{2,1,0:T(8,128)S(1)}, f32[4,168,128]{2,1,0:T(8,128)S(1)}, u32[]{:S(2)}, u32[]{:S(2)}) collective-permute-start(f32[4,168,128]{2,1,0:T(8,128)S(1)} %get-tuple-element.28), channel_id=1, source_target_pairs={{0,2},{2,0},{4,6},{6,4},{8,10},{10,8},{12,14},{14,12},{1,3},{3,1},... | collective-permute-start | bytes 1032200 | tf_op jit(solution)/shard_map/ppermute | solution.py:649
  7.3 12.3 %collective-permute-start.3 = (f32[4,168,128]{2,1,0:T(8,128)S(1)}, f32[4,168,128]{2,1,0:T(8,128)S(1)}, u32[]{:S(2)}, u32[]{:S(2)}) collective-permute-start(f32[4,168,128]{2,1,0:T(8,128)S(1)} %get-tuple-element.32), channel_id=1, source_target_pairs={{4,8},{6,10},{8,4},{10,6},{5,9},{7,11},{9,5},{11,7},{20,24},{22,26... | collective-permute-start | bytes 1032200 | tf_op jit(solution)/shard_map/ppermute | solution.py:649
  9.2 7.8 %collective-permute-start.4 = (f32[4,40,128]{2,1,0:T(8,128)S(1)}, f32[4,40,128]{2,1,0:T(8,128)S(1)}, u32[]{:S(2)}, u32[]{:S(2)}) collective-permute-start(f32[4,40,128]{2,1,0:T(8,128)S(1)} %get-tuple-element.33), channel_id=1, source_target_pairs={{0,6},{2,4},{4,2},{6,0},{8,14},{10,12},{12,10},{14,8},{1,7},{3,5},... | collective-permute-start | bytes 245768 | tf_op jit(solution)/shard_map/ppermute | solution.py:649
  9.3 10.3 %collective-permute-start.5 = (f32[4,40,128]{2,1,0:T(8,128)S(1)}, f32[4,40,128]{2,1,0:T(8,128)S(1)}, u32[]{:S(2)}, u32[]{:S(2)}) collective-permute-start(f32[4,40,128]{2,1,0:T(8,128)S(1)} %get-tuple-element.34), channel_id=1, source_target_pairs={{4,10},{6,8},{8,6},{10,4},{5,11},{7,9},{9,7},{11,5},{20,26},{22,24... | collective-permute-start | bytes 245768 | tf_op jit(solution)/shard_map/ppermute | solution.py:649
  19.6 3.3 %copy-start.3 = (s32[8,512]{1,0:T(8,128)S(1)}, s32[8,512]{1,0:T(8,128)}, u32[]{:S(2)}) copy-start(s32[8,512]{1,0:T(8,128)} %param.9) | copy-start | bytes 49156
  21.1 4.4 %collective-permute-start.6 = (f32[4,448,128]{2,1,0:T(8,128)S(1)}, f32[4,448,128]{2,1,0:T(8,128)}, u32[]{:S(2)}, u32[]{:S(2)}) collective-permute-start(f32[4,448,128]{2,1,0:T(8,128)S(1)} %get-tuple-element.36.other), channel_id=1, source_target_pairs={{0,1},{1,0},{2,3},{3,2},{4,5},{5,4},{6,7},{7,6},{8,9},{9,8},{10,11... | collective-permute-start | bytes 2752520 | tf_op jit(solution)/shard_map/ppermute | solution.py:695
  23.6 1.9 %copy-start.1 = (s32[8]{0:T(128)S(1)}, s32[8]{0:T(128)}, u32[]{:S(2)}) copy-start(s32[8]{0:T(128)} %material.1) | copy-start | bytes 100
  23.6 1.9 %copy-start.2 = (f32[4]{0:T(128)S(1)}, f32[4]{0:T(128)}, u32[]{:S(2)}) copy-start(f32[4]{0:T(128)} %conductivity.1) | copy-start | bytes 52
  39.6 2.0 %collective-permute-start.7 = (f32[4,128,256]{2,1,0:T(8,128)S(1)}, f32[4,128,256]{2,1,0:T(8,128)S(1)}, u32[]{:S(2)}, u32[]{:S(2)}) collective-permute-start(f32[4,128,256]{2,1,0:T(8,128)S(1)} %get-tuple-element.39), channel_id=1, source_target_pairs={{0,1},{1,0},{2,3},{3,2},{4,5},{5,4},{6,7},{7,6},{8,9},{9,8},{10,11... | collective-permute-start | bytes 1572872 | tf_op jit(solution)/shard_map/ppermute | solution.py:726
